TPU v7x, 32 devices: a whole 2x2x4 slice. The times are simulated.
32 devices in a mesh: group: 2 (over y), section: 4 (over z), seq: 2 (over x), tp: 2 (over core).
Axes of the slice: x: 2, y: 2, z: 4, core: 2. Of those that a mesh axis runs over, the one named last changes fastest.
Arguments:
- handoff: bfloat16 [8, 768, 8192], P(('group', 'section'), 'seq', 'tp'), parts along dimension 0, may hold values from -6 to 6
- norm_gain: float32 [4, 8192], P('section'), may hold values from 0.5 to 1.5
- kv_weight: bfloat16 [4, 8192, 4, 256], P('section', 'seq', 'tp'), may hold values from -0.0625 to 0.0625
- span_start: int32 [8], P(('group', 'section')), parts along dimension 0, may hold values from 0 to 4095
- token_owner: int32 [8, 768, 1], P(('group', 'section'), 'seq'), parts along dimension 0, may hold values from 0 to 3; in each aligned block of 384 rows (0 to 383, 384 to 767, ..., all dimensions but the last counted through in order) at most 192 rows name the same one
- token_slot: int32 [8, 768], P(('group', 'section'), 'seq'), parts along dimension 0, may hold values from 0 to 1
- kv_cache: bfloat16 [8, 2, 4, 2, 32, 4, 256], P(('group', 'section'), 'seq', None, None, None, 'tp'), parts along dimension 0, may hold values from -4 to 4
- cache_lens: int32 [8, 2, 2], P(('group', 'section'), 'seq'), parts along dimension 0, may hold values from 2 to 32
- step_kv: bfloat16 [8, 2, 4, 2, 2, 4, 256], P(('group', 'section'), 'seq', None, None, None, 'tp'), parts along dimension 0, may hold values from -6 to 6
- queries: bfloat16 [8, 2, 4, 2, 2, 4, 1024], P(('group', 'section'), 'seq', None, None, None, 'tp'), parts along dimension 0, may hold values from -80 to 80
Outputs:
- decode_out: bfloat16 [8, 2, 4, 2, 2, 4, 1024], P(('group', 'section'), 'seq', None, None, None, 'tp'), parts along dimension 0
There are 2 independent parts, one for each index of `group`. A program takes and returns all parts, laid end to end along the dimension named above; an argument that names none is the same for every part. Nothing has to cross between parts.
Inputs may be any that keep to these rules, and one draw needn't show every extreme that they name: `token_owner`: among the 384 tokens of one device's rows (aligned blocks), no owner section is named by more than 192 tokens.
All inputs are finite; a program needn't handle non-finite values.
Results may differ from a plain program's by a relative error of at most 0.0066.
Values may be sent and summed in bfloat16 or wider, within the bound.
No kernel may reach another device: no remote copies, remote signals or barrier semaphores. Data moves between devices by JAX's collectives and lax.ppermute only.
A program may use at most 128 MiB of HBM per device.

v0:
```python
import math

import jax
import jax.numpy as jnp
from jax import lax
from jax.sharding import PartitionSpec as P

EPS = 1e-05
THETA = 500000.0


def passed_along(value, axis, by):
    length = lax.axis_size(axis)
    return lax.ppermute(value, axis, [(i, (i + by) % length) for i in range(length)])


def rotate(pairs, positions):
    width = pairs.shape[-1] // 2
    half = width // 2
    freq = jnp.exp(-(jnp.arange(half, dtype=jnp.float32) * 2.0 / width) * math.log(THETA))
    angle = positions.astype(jnp.float32)[:, None, None] * freq[None, None, :]
    cosine = jnp.cos(angle)
    sine = jnp.sin(angle)
    first = pairs[..., :half]
    second = pairs[..., half:width]
    turned = jnp.concatenate(
        [first * cosine - second * sine, second * cosine + first * sine], axis=-1
    )
    return jnp.concatenate([turned, pairs[..., width:]], axis=-1)


def attend(query, past, lens, route_pairs, route_mask, step_pairs):
    reqs, steps, heads, flat = query.shape
    width = past.shape[-1] // 2
    groups = flat // width
    scale = 1.0 / math.sqrt(width)
    shaped = query.reshape(reqs, steps, heads, groups, width)
    score_past = (
        jnp.einsum(
            "rnhgd,rphd->rnhgp", shaped, past[..., :width], preferred_element_type=jnp.float32
        )
        * scale
    )
    score_route = (
        jnp.einsum(
            "rnhgd,khd->rnhgk", shaped, route_pairs[..., :width], preferred_element_type=jnp.float32
        )
        * scale
    )
    score_step = (
        jnp.einsum(
            "rnhgd,rmhd->rnhgm", shaped, step_pairs[..., :width], preferred_element_type=jnp.float32
        )
        * scale
    )
    past_mask = jnp.arange(past.shape[1], dtype=jnp.int32)[None, :] < lens[:, None]
    step_mask = (
        jnp.arange(steps, dtype=jnp.int32)[:, None] >= jnp.arange(steps, dtype=jnp.int32)[None, :]
    )
    score_past = jnp.where(past_mask[:, None, None, None, :], score_past, -jnp.inf)
    score_route = jnp.where(route_mask[:, None, None, None, :], score_route, -jnp.inf)
    score_step = jnp.where(step_mask[None, :, None, None, :], score_step, -jnp.inf)
    top = jnp.maximum(
        jnp.maximum(
            jnp.max(score_past, axis=-1, keepdims=True),
            jnp.max(score_route, axis=-1, keepdims=True),
        ),
        jnp.max(score_step, axis=-1, keepdims=True),
    )
    exp_past = jnp.exp(score_past - top)
    exp_route = jnp.exp(score_route - top)
    exp_step = jnp.exp(score_step - top)
    total = (
        jnp.sum(exp_past, axis=-1, keepdims=True)
        + jnp.sum(exp_route, axis=-1, keepdims=True)
        + jnp.sum(exp_step, axis=-1, keepdims=True)
    )
    w_past = (exp_past / total).astype(jnp.bfloat16)
    w_route = (exp_route / total).astype(jnp.bfloat16)
    w_step = (exp_step / total).astype(jnp.bfloat16)
    result = jnp.einsum(
        "rnhgp,rphd->rnhgd", w_past, past[..., width:], preferred_element_type=jnp.float32
    )
    result = result + jnp.einsum(
        "rnhgk,khd->rnhgd", w_route, route_pairs[..., width:], preferred_element_type=jnp.float32
    )
    result = result + jnp.einsum(
        "rnhgm,rmhd->rnhgd", w_step, step_pairs[..., width:], preferred_element_type=jnp.float32
    )
    return result.astype(jnp.bfloat16).reshape(reqs, steps, heads, flat)


def local(
    handoff,
    norm_gain,
    kv_weight,
    span_start,
    token_owner,
    token_slot,
    kv_cache,
    cache_lens,
    step_kv,
    queries,
):
    received = passed_along(handoff, "section", 1)
    whole = lax.all_gather(received[0], "tp", axis=1, tiled=True)
    tokens = whole.shape[0]
    values = whole.astype(jnp.float32)
    meansq = jnp.mean(values * values, axis=-1, keepdims=True)
    normed = (values * lax.rsqrt(meansq + EPS) * norm_gain[0][None, :]).astype(jnp.bfloat16)
    weight = kv_weight[0]
    local_heads = weight.shape[1]
    pair_width = weight.shape[2]
    columns_out = local_heads * pair_width
    piece = lax.all_gather(weight, "seq", axis=0, tiled=True)
    projected = jnp.dot(
        normed, piece.reshape(piece.shape[0], columns_out), preferred_element_type=jnp.float32
    )
    positions = span_start[0] + lax.axis_index("seq") * tokens + jnp.arange(tokens, dtype=jnp.int32)
    prompt_kv = rotate(projected.reshape(tokens, local_heads, pair_width), positions).astype(
        jnp.bfloat16
    )
    sections = lax.axis_size("section")
    capacity = 2 * tokens // sections
    owner = token_owner[0, :, 0]
    slot = token_slot[0]
    onehot = (owner[:, None] == jnp.arange(sections, dtype=jnp.int32)[None, :]).astype(jnp.bfloat16)
    lower = (
        jnp.arange(tokens, dtype=jnp.int32)[:, None] >= jnp.arange(tokens, dtype=jnp.int32)[None, :]
    ).astype(jnp.bfloat16)
    running = jnp.dot(lower, onehot, preferred_element_type=jnp.float32)
    rank = (jnp.sum(running * onehot.astype(jnp.float32), axis=1) - 1.0).astype(jnp.int32)
    place = owner * capacity + rank
    select = (place[:, None] == jnp.arange(sections * capacity, dtype=jnp.int32)[None, :]).astype(
        jnp.bfloat16
    )
    packed = jnp.einsum(
        "ts,tc->sc",
        select,
        prompt_kv.reshape(tokens, columns_out),
        preferred_element_type=jnp.float32,
    )
    packed = packed.astype(jnp.bfloat16).reshape(sections, capacity, local_heads, pair_width)
    labels = jnp.einsum(
        "ts,t->s", select, (slot + 1).astype(jnp.bfloat16), preferred_element_type=jnp.float32
    )
    labels = labels.astype(jnp.bfloat16).reshape(sections, capacity)
    routed, routed_labels = (
        lax.all_to_all(packed, "section", split_axis=0, concat_axis=0, tiled=True),
        lax.all_to_all(labels, "section", split_axis=0, concat_axis=0, tiled=True),
    )
    request_ids = (jnp.arange(kv_cache.shape[3], dtype=jnp.int32) + 1).astype(jnp.float32)
    route_mask = routed_labels.astype(jnp.float32)[:, None, :] == request_ids[None, :, None]
    layered = jax.vmap(attend, in_axes=(0, 0, None, 0, 0, 0))
    result = layered(
        queries[0, 0], kv_cache[0, 0], cache_lens[0, 0], routed, route_mask, step_kv[0, 0]
    )
    return result[None, None]


def solution(mesh):
    return jax.shard_map(
        local,
        mesh=mesh,
        in_specs=(
            P(("group", "section"), "seq", "tp"),
            P("section", None),
            P("section", "seq", "tp", None),
            P(("group", "section")),
            P(("group", "section"), "seq", None),
            P(("group", "section"), "seq"),
            P(("group", "section"), "seq", None, None, None, "tp", None),
            P(("group", "section"), "seq", None),
            P(("group", "section"), "seq", None, None, None, "tp", None),
            P(("group", "section"), "seq", None, None, None, "tp", None),
        ),
        out_specs=P(("group", "section"), "seq", None, None, None, "tp", None),
        check_vma=False,
    )
```

profile of v0, /device:TPU:0, one launch (start us, length us, event | category | flops | bytes accessed | tf_op | source)
XLA Modules:
  0.0 185.1 jit_solution(8290267190579907799)
XLA Ops:
  6.5 0.7 all-gather.7.cloned.1.call-update
  7.3 3.1 %collective-permute-start = (bf16[1,384,4096]{2,1,0:T(8,128)(2,1)}, bf16[1,384,4096]{2,1,0:T(8,128)(2,1)S(1)}, u32[]{:S(2)}, u32[]{:S(2)}) collective-permute-start(bf16[1,384,4096]{2,1,0:T(8,128)(2,1)} %param.10), channel_id=1, source_target_pairs={{0,4},{4,8},{8,12},{12,0},{1,5},{5,9},{9,13},{13,1},{2,6},{6,10},{... | collective-permute-start | bytes 9437192 | tf_op jit(solution)/shard_map/ppermute | solution.py:14
  10.4 70.3 %collective-permute-done = bf16[1,384,4096]{2,1,0:T(8,128)(2,1)S(1)} collective-permute-done((bf16[1,384,4096]{2,1,0:T(8,128)(2,1)}, bf16[1,384,4096]{2,1,0:T(8,128)(2,1)S(1)}, u32[]{:S(2)}, u32[]{:S(2)}) %collective-permute-start) | collective-permute-done | bytes 3145760 | tf_op jit(solution)/shard_map/ppermute | solution.py:14
  80.7 1.7 copy-done.1
  82.7 0.4 fusion.22
  83.1 0.7 all_to_all.12
  83.8 3.2 %all-to-all-start = ((bf16[4,1,192]{2,1,0:T(2,128)(2,1)}), bf16[4,1,192]{2,1,0:T(2,128)(2,1)S(1)}, u32[]{:S(2)}, u32[]{:S(2)}) async-start(bf16[4,1,192]{2,1,0:T(2,128)(2,1)} %all_to_all.12), calls=%async_computation | async-start | bytes 8192 | tf_op jit(solution)/shard_map/all_to_all | solution.py:150
  87.7 0.4 multiply_cosine_fusion
  88.1 27.5 %all-gather.7.cloned.1.call-done = bf16[1,8192,2,256]{3,2,0,1:T(2,128)(2,1)} async-done(((bf16[1,4096,2,256]{3,2,0,1:T(2,128)(2,1)}), bf16[1,8192,2,256]{3,2,0,1:T(2,128)(2,1)}) %all-gather.7.cloned.1.call-update) | async-done | bytes 8388624 | tf_op jit(solution)/shard_map/all_gather | solution.py:115
  115.6 21.6 %copy.72 = bf16[1,8192,2,256]{1,3,2,0:T(8,128)(2,1)} copy(bf16[1,8192,2,256]{3,2,0,1:T(2,128)(2,1)} %all-gather.7.cloned.1.call-done) | data formatting | bytes 16777216 | tf_op jit(solution)/shard_map/reshape | solution.py:117
  137.2 4.3 %fusion = f32[384]{0:T(512)S(1)} fusion(bf16[1,384,8192]{2,1,0:T(8,128)(2,1)} %all-gather.5.cloned.1.call-done), kind=kLoop, calls=%fused_computation.2 | loop fusion | flops 9436800 | bytes 6292992 | tf_op jit(solution)/shard_map/reduce_sum | solution.py:109
  141.5 0.3 copy-done
  141.8 7.2 %fusion.3 = f32[384,2,256]{0,2,1:T(8,128)S(1)} fusion(bf16[1,8192,2,256]{1,3,2,0:T(8,128)(2,1)} %copy.72, bf16[1,384,8192]{2,1,0:T(8,128)(2,1)S(1)} %copy-done, f32[8192]{0:T(1024)S(1)} %bitcast.105, f32[384]{0:T(512)S(1)} %add_rsqrt_fusion), kind=kOutput, calls=%fused_computation.5 | convolution fusion | flops 3233808384 | bytes 15500800 | tf_op jit(solution)/shard_map/dot_general | solution.py:116
  149.2 0.7 convolution_convert_fusion
  150.1 1.0 copy.56
  151.1 4.6 %all-to-all-start.1 = ((bf16[4,192,2,256]{3,1,2,0:T(8,128)(2,1)}), bf16[4,192,2,256]{3,1,2,0:T(8,128)(2,1)S(1)}, u32[]{:S(2)}, u32[]{:S(2)}) async-start(bf16[4,192,2,256]{3,1,2,0:T(8,128)(2,1)} %copy.56), calls=%async_computation.1 | async-start | bytes 1572864 | tf_op jit(solution)/shard_map/all_to_all | solution.py:149
  155.9 0.4 fusion.46
  156.3 0.3 fusion.47
  156.7 19.1 %all-to-all-done.1 = bf16[4,192,2,256]{3,1,2,0:T(8,128)(2,1)S(1)} async-done(((bf16[4,192,2,256]{3,1,2,0:T(8,128)(2,1)}), bf16[4,192,2,256]{3,1,2,0:T(8,128)(2,1)S(1)}, u32[]{:S(2)}, u32[]{:S(2)}) %all-to-all-start.1) | async-done | bytes 786464 | tf_op jit(solution)/shard_map/all_to_all | solution.py:149
  175.8 0.4 fusion.48
  176.6 0.2 fusion.26
  177.0 0.3 convolution_bitcast_fusion.1
  177.3 0.3 fusion.18
  177.6 0.7 copy.65
  (45 shorter events, 1.5 us)
Async XLA Ops:
  6.5 75.9 %copy-start.5 = (s32[1,384,1]{1,2,0:T(1,128)S(1)}, s32[1,384,1]{1,2,0:T(1,128)}, u32[]{:S(2)}) copy-start(s32[1,384,1]{1,2,0:T(1,128)} %param.14) | copy-start | bytes 4612
  6.5 76.2 %copy-start.7 = (s32[1,384]{1,0:T(1,128)S(1)}, s32[1,384]{1,0:T(1,128)}, u32[]{:S(2)}) copy-start(s32[1,384]{1,0:T(1,128)} %param.15) | copy-start | bytes 4612
  6.5 109.1 %all-gather.7.cloned.1.call-start = ((), (), s32[]{:S(2)}) async-start(), calls=%async_computation.3 | async-start | bytes 12582912 | tf_op jit(solution)/shard_map/all_gather | solution.py:115
  7.3 129.9 %all-gather.5.cloned.1.call-start = ((), (), s32[]{:S(2)}) async-start(), calls=%async_computation.2 | async-start | bytes 9437184 | tf_op jit(solution)/shard_map/all_gather | solution.py:106
  7.3 73.4 %collective-permute-start = (bf16[1,384,4096]{2,1,0:T(8,128)(2,1)}, bf16[1,384,4096]{2,1,0:T(8,128)(2,1)S(1)}, u32[]{:S(2)}, u32[]{:S(2)}) collective-permute-start(bf16[1,384,4096]{2,1,0:T(8,128)(2,1)} %param.10), channel_id=1, source_target_pairs={{0,4},{4,8},{8,12},{12,0},{1,5},{5,9},{9,13},{13,1},{2,6},{6,10},{... | collective-permute-start | bytes 9437192 | tf_op jit(solution)/shard_map/ppermute | solution.py:14
  80.7 1.7 copy-start.1
  83.8 67.3 %all-to-all-start = ((bf16[4,1,192]{2,1,0:T(2,128)(2,1)}), bf16[4,1,192]{2,1,0:T(2,128)(2,1)S(1)}, u32[]{:S(2)}, u32[]{:S(2)}) async-start(bf16[4,1,192]{2,1,0:T(2,128)(2,1)} %all_to_all.12), calls=%async_computation | async-start | bytes 8192 | tf_op jit(solution)/shard_map/all_to_all | solution.py:150
  115.6 25.8 %copy-start.6 = (f32[1,8192]{1,0:T(1,128)S(1)}, f32[1,8192]{1,0:T(1,128)}, u32[]{:S(2)}) copy-start(f32[1,8192]{1,0:T(1,128)} %param.11) | copy-start | bytes 98308
  137.2 4.6 %copy-start = (bf16[1,384,8192]{2,1,0:T(8,128)(2,1)S(1)}, bf16[1,384,8192]{2,1,0:T(8,128)(2,1)}, u32[]{:S(2)}) copy-start(bf16[1,384,8192]{2,1,0:T(8,128)(2,1)} %all-gather.5.cloned.1.call-done) | copy-start | bytes 18874372
  149.0 6.7 %copy-start.3 = (bf16[1,1,4,2,2,2,1024]{6,5,4,3,2,1,0:T(2,128)(2,1)S(1)}, bf16[1,1,4,2,2,2,1024]{6,5,4,3,2,1,0:T(2,128)(2,1)}, u32[]{:S(2)}) copy-start(bf16[1,1,4,2,2,2,1024]{6,5,4,3,2,1,0:T(2,128)(2,1)} %param.19) | copy-start | bytes 196612
  149.0 6.7 %copy-start.4 = (bf16[1,1,4,2,2,2,256]{6,5,4,3,2,1,0:T(2,128)(2,1)S(1)}, bf16[1,1,4,2,2,2,256]{6,5,4,3,2,1,0:T(2,128)(2,1)}, u32[]{:S(2)}) copy-start(bf16[1,1,4,2,2,2,256]{6,5,4,3,2,1,0:T(2,128)(2,1)} %param.18) | copy-start | bytes 49156
  149.0 6.8 %copy-start.2 = (bf16[1,1,4,2,32,2,256]{6,5,4,3,2,1,0:T(2,128)(2,1)S(1)}, bf16[1,1,4,2,32,2,256]{6,5,4,3,2,1,0:T(2,128)(2,1)}, u32[]{:S(2)}) copy-start(bf16[1,1,4,2,32,2,256]{6,5,4,3,2,1,0:T(2,128)(2,1)} %param.16) | copy-start | bytes 786436
  149.0 6.8 %copy-start.8 = (s32[1,1,2]{2,1,0:T(1,128)S(1)}, s32[1,1,2]{2,1,0:T(1,128)}, u32[]{:S(2)}) copy-start(s32[1,1,2]{2,1,0:T(1,128)} %param.17) | copy-start | bytes 28
  151.1 24.7 %all-to-all-start.1 = ((bf16[4,192,2,256]{3,1,2,0:T(8,128)(2,1)}), bf16[4,192,2,256]{3,1,2,0:T(8,128)(2,1)S(1)}, u32[]{:S(2)}, u32[]{:S(2)}) async-start(bf16[4,192,2,256]{3,1,2,0:T(8,128)(2,1)} %copy.56), calls=%async_computation.1 | async-start | bytes 1572864 | tf_op jit(solution)/shard_map/all_to_all | solution.py:149
Sparse Core Ops, SparseCore 0:
  8.9 106.6 all-gather.6
  117.2 16.7 all-gather.4
where the time goes:
time: 186 us; the launch traced here: 185 us
  waiting for transfers between devices  118 us (63%)
  local copies, waits for them, and re-layouts  26.3 us (14%)
  between operations  14.3 us (8%)
  starting transfers between devices  10.9 us (6%)
  matrix products  10.4 us (6%)
  other arithmetic  5.54 us (3%)
    ppermute x1, waiting for transfers between devices, passed_along(): lax.ppermute(value, axis, [(i, (i + by) % length) for i in range(length)])  70.3 us
    all_gather x1, waiting for transfers between devices, local(): piece = lax.all_gather(weight, 'seq', axis=0, tiled=True)  27.5 us
    reshape x1, local copies, waits for them, and re-layouts, local(): piece.reshape(piece.shape[0], columns_out)  21.6 us
    all_to_all x1, waiting for transfers between devices, local(): lax.all_to_all(packed, 'section', split_axis=0, concat_axis=0, tiled=True)  19.1 us
    dot_general x1, matrix products, local(): jnp.dot(normed, piece.reshape(piece.shape[0], columns_out), preferred_ele...  7.17 us
    all_to_all x1, starting transfers between devices, local(): lax.all_to_all(packed, 'section', split_axis=0, concat_axis=0, tiled=True)  4.57 us
    reduce_sum x1, other arithmetic, local(): meansq = jnp.mean(values * values, axis=-1, keepdims=True)  4.25 us
  transfers between devices with their start and end apart: 5, of which 3 were waited for; matrix products, arithmetic and copies ran while one was open for 20% of the time, Pallas kernels for 0%

commit v1 on v0

--- a/solution.py
+++ b/solution.py
@@ -3,10 +3,13 @@
 import jax
 import jax.numpy as jnp
 from jax import lax
+from jax.experimental import pallas as pl
+from jax.experimental.pallas import tpu as pltpu
 from jax.sharding import PartitionSpec as P
 
 EPS = 1e-05
 THETA = 500000.0
+NEG = -1e30
 
 
 def passed_along(value, axis, by):
@@ -158,9 +161,323 @@
     return result[None, None]
 
 
+def steered(value, pairs_of, sizes):
+    groups, seqs, cores = sizes
+    pairs = []
+    for g in range(groups):
+        for q in range(seqs):
+            for t in range(cores):
+                a, b, c = pairs_of(g, q, t)
+                pairs.append(((g * seqs + q) * cores + t, (a * seqs + b) * cores + c))
+    return lax.ppermute(value, ("group", "seq", "tp"), pairs)
+
+
+def swapped(value):
+    return lax.ppermute(value, "tp", [(0, 1), (1, 0)])
+
+
+def split_heads(mixed, gain, joined, blocks):
+    rows = mixed.shape[0] // 2
+    width = mixed.shape[1]
+    tall = rows // blocks
+
+    def body(mixed_ref, gain_ref, *rest):
+        outs, wide = rest[:-1], rest[-1]
+        wide[...] = mixed_ref[...].astype(jnp.float32)
+        gains = jnp.concatenate(
+            [
+                jnp.broadcast_to(gain_ref[:, b * width : (b + 1) * width], (width, width)).T
+                for b in range(tall // width)
+            ],
+            axis=0,
+        )
+        for head in range(2):
+            scaled = (wide[pl.ds(head, tall, stride=2), :] * gains).astype(jnp.bfloat16)
+            if joined:
+                outs[0][:, head * width : (head + 1) * width] = scaled
+            else:
+                outs[head][...] = scaled
+
+    if joined:
+        shapes = [jax.ShapeDtypeStruct((rows, 2 * width), jnp.bfloat16)]
+        out_specs = [pl.BlockSpec((tall, 2 * width), lambda i: (i, 0))]
+    else:
+        shapes = [jax.ShapeDtypeStruct((rows, width), jnp.bfloat16)] * 2
+        out_specs = [pl.BlockSpec((tall, width), lambda i: (i, 0))] * 2
+    return pl.pallas_call(
+        body,
+        out_shape=shapes,
+        grid=(blocks,),
+        in_specs=[
+            pl.BlockSpec((2 * tall, width), lambda i: (i, 0)),
+            pl.BlockSpec((1, tall), lambda i: (0, i)),
+        ],
+        out_specs=out_specs,
+        scratch_shapes=[pltpu.VMEM((2 * tall, width), jnp.float32)],
+        name="split_heads",
+    )(mixed, gain)
+
+
+def partial_products(same, acts, weights):
+    tokens = acts[0].shape[0]
+    columns = weights[0].shape[1]
+    depths = [w.shape[0] for w in weights]
+
+    def body(same_ref, near_ref, near_mate_ref, far_ref, far_mate_ref, *rest):
+        w_refs, outs = rest[: len(depths)], rest[len(depths) :]
+
+        def product(ref):
+            total = None
+            start = 0
+            for w_ref, depth in zip(w_refs, depths):
+                part = jnp.dot(
+                    ref[:, start : start + depth], w_ref[...], preferred_element_type=jnp.float32
+                )
+                total = part if total is None else total + part
+                start += depth
+            return total
+
+        def fill(own, across, far_own, far_across):
+            outs[1][...] = product(across).astype(jnp.bfloat16)
+            outs[2][...] = product(far_own).astype(jnp.bfloat16)
+            outs[3][...] = product(far_across).astype(jnp.bfloat16)
+            outs[0][...] = product(own)
+
+        @pl.when(same_ref[0] == 1)
+        def _():
+            fill(near_ref, near_mate_ref, far_ref, far_mate_ref)
+
+        @pl.when(same_ref[0] == 0)
+        def _():
+            fill(near_mate_ref, near_ref, far_mate_ref, far_ref)
+
+    vmem = pl.BlockSpec(memory_space=pltpu.VMEM)
+    return pl.pallas_call(
+        body,
+        out_shape=[jax.ShapeDtypeStruct((tokens, columns), jnp.float32)]
+        + [jax.ShapeDtypeStruct((tokens, columns), jnp.bfloat16)] * 3,
+        in_specs=[pl.BlockSpec(memory_space=pltpu.SMEM)] + [vmem] * (4 + len(weights)),
+        out_specs=[vmem] * 4,
+        compiler_params=pltpu.CompilerParams(vmem_limit_bytes=40 << 20),
+        name="partial_products",
+    )(same, *acts, *weights)
+
+
+def summed_over_chips(parts, sizes):
+    own, across, far, far_across = parts
+    groups, seqs, _ = sizes
+    return (
+        own,
+        steered(across, lambda g, q, t: (g, seqs - 1 - q, t), sizes),
+        steered(far, lambda g, q, t: (groups - 1 - g, q, t), sizes),
+        steered(far_across, lambda g, q, t: (groups - 1 - g, seqs - 1 - q, t), sizes),
+    )
+
+
+def attend_routed(asked, keys, values, scale, cosine, sine, code):
+    owners, heads, rows, width = asked.shape
+    tokens = code.shape[1]
+    half = width // 2
+    requests = 2
+    factor = 1.0 / math.sqrt(width)
+
+    def body(asked_ref, *rest):
+        key_refs = rest[:4]
+        value_refs = [rest[4 + 4 * h : 8 + 4 * h] for h in range(heads)]
+        scale_ref, cos_ref, sin_ref, code_ref, out_ref = rest[4 + 4 * heads :]
+        span = owners * rows
+        request = lax.broadcasted_iota(jnp.int32, (span, tokens), 0) // (rows // requests)
+        mine = request == code_ref[...]
+        lane = lax.broadcasted_iota(jnp.int32, (span, width), 1)
+        for h in range(heads):
+            columns = slice(h * width, (h + 1) * width)
+            key = key_refs[0][:, columns]
+            for ref in key_refs[1:]:
+                key = key + ref[:, columns].astype(jnp.float32)
+            key = key * scale_ref[...]
+            first = key[:, :half]
+            second = key[:, half:]
+            cosine_ = cos_ref[...]
+            sine_ = sin_ref[...]
+            key = jnp.concatenate(
+                [first * cosine_ - second * sine_, second * cosine_ + first * sine_], axis=1
+            ).astype(jnp.bfloat16)
+            value = value_refs[h][0][...]
+            for ref in value_refs[h][1:]:
+                value = value + ref[...].astype(jnp.float32)
+            value = (value * scale_ref[...]).astype(jnp.bfloat16)
+            query = jnp.concatenate([asked_ref[o, h] for o in range(owners)], axis=0)
+            score = (
+                lax.dot_general(
+                    query, key, (((1,), (1,)), ((), ())), preferred_element_type=jnp.float32
+                )
+                * factor
+            )
+            score = jnp.where(mine, score, NEG)
+            top = jnp.max(score, axis=1, keepdims=True)
+            weight = jnp.where(mine, jnp.exp(score - top), 0.0)
+            total = jnp.sum(weight, axis=1, keepdims=True)
+            mixed = jnp.dot(
+                weight.astype(jnp.bfloat16), value, preferred_element_type=jnp.float32
+            )
+            some = total > 0.0
+            safe = jnp.where(some, total, 1.0)
+            mixed = (mixed / safe).astype(jnp.bfloat16)
+            level = jnp.where(some, top + jnp.log(safe), NEG)
+            high = level.astype(jnp.bfloat16).astype(jnp.float32)
+            middle = (level - high).astype(jnp.bfloat16).astype(jnp.float32)
+            low = level - high - middle
+            marks = jnp.where(
+                lane == 0, high, jnp.where(lane == 1, middle, jnp.where(lane == 2, low, 0.0))
+            ).astype(jnp.bfloat16)
+            for o in range(owners):
+                out_ref[o, h, :, :width] = mixed[o * rows : (o + 1) * rows]
+                out_ref[o, h, :, width:] = marks[o * rows : (o + 1) * rows]
+
+    vmem = pl.BlockSpec(memory_space=pltpu.VMEM)
+    operands = (asked, *keys, *[v for chunk in values for v in chunk], scale, cosine, sine, code)
+    return pl.pallas_call(
+        body,
+        out_shape=jax.ShapeDtypeStruct((owners, heads, rows, 2 * width), jnp.bfloat16),
+        in_specs=[vmem] * len(operands),
+        out_specs=vmem,
+        name="attend_routed",
+    )(*operands)
+
+
+def attend_kept(query, past, lens, step_pairs):
+    layers, reqs, steps, heads, flat = query.shape
+    width = past.shape[-1] // 2
+    scale = 1.0 / math.sqrt(width)
+    shaped = query.reshape(layers, reqs, steps, heads, flat // width, width)
+    score_past = scale * jnp.einsum(
+        "lrnhgd,lrphd->lrhngp", shaped, past[..., :width], preferred_element_type=jnp.float32
+    )
+    score_step = scale * jnp.einsum(
+        "lrnhgd,lrmhd->lrhngm", shaped, step_pairs[..., :width], preferred_element_type=jnp.float32
+    )
+    filled = jnp.arange(past.shape[2], dtype=jnp.int32)[None, :] < lens[:, None]
+    turn = jnp.arange(steps, dtype=jnp.int32)
+    score_past = jnp.where(filled[None, :, None, None, None, :], score_past, NEG)
+    score_step = jnp.where(
+        (turn[:, None] >= turn[None, :])[None, None, None, :, None, :], score_step, NEG
+    )
+    top = jnp.maximum(
+        jnp.max(score_past, axis=-1, keepdims=True), jnp.max(score_step, axis=-1, keepdims=True)
+    )
+    exp_past = jnp.exp(score_past - top)
+    exp_step = jnp.exp(score_step - top)
+    total = jnp.sum(exp_past, axis=-1, keepdims=True) + jnp.sum(exp_step, axis=-1, keepdims=True)
+    mixed = jnp.einsum(
+        "lrhngp,lrphd->lrhngd",
+        exp_past.astype(jnp.bfloat16),
+        past[..., width:],
+        preferred_element_type=jnp.float32,
+    ) + jnp.einsum(
+        "lrhngm,lrmhd->lrhngd",
+        exp_step.astype(jnp.bfloat16),
+        step_pairs[..., width:],
+        preferred_element_type=jnp.float32,
+    )
+    return mixed, top, total
+
+
+def meet_local(
+    handoff,
+    norm_gain,
+    kv_weight,
+    span_start,
+    token_owner,
+    token_slot,
+    kv_cache,
+    cache_lens,
+    step_kv,
+    queries,
+):
+    sizes = (lax.axis_size("group"), lax.axis_size("seq"), lax.axis_size("tp"))
+    sections = lax.axis_size("section")
+    g = lax.axis_index("group")
+    q = lax.axis_index("seq")
+    t = lax.axis_index("tp")
+    weight = kv_weight[0]
+    depth = weight.shape[0] // sizes[0]
+    width = weight.shape[2] // 2
+    first = depth // 4
+
+    gain = lax.dynamic_slice_in_dim(norm_gain[0], (q * sizes[0] + g) * depth, depth, 0)[None]
+
+    def piece(start, rows, column):
+        cut = lax.dynamic_slice(weight, (g * depth + start, 0, column * width), (rows, 2, width))
+        return cut.reshape(2 * rows, width)
+
+    (keys_a,) = split_heads(piece(0, first, 0), gain[:, :first], True, 1)
+    (keys_b,) = split_heads(piece(first, depth - first, 0), gain[:, first:], True, 3)
+    values_0, values_1 = split_heads(piece(0, depth, 1), gain, False, 4)
+    keys_a = passed_along(keys_a, "section", -1)
+    keys_b = passed_along(keys_b, "section", -1)
+    values_0 = passed_along(values_0, "section", -1)
+    values_1 = passed_along(values_1, "section", -1)
+
+    block = handoff[0]
+    tokens = block.shape[0]
+    near = lax.dynamic_slice_in_dim(block, g * depth, depth, 1)
+    far = lax.dynamic_slice_in_dim(block, (sizes[0] - 1 - g) * depth, depth, 1)
+    near = steered(near, lambda a, b, c: (a, c, b), sizes)
+    far = steered(far, lambda a, b, c: (sizes[0] - 1 - a, c, b), sizes)
+    acts = (near, swapped(near), far, swapped(far))
+    same = (q == t).astype(jnp.int32)[None]
+
+    wide = block.astype(jnp.float32)
+    square = jnp.sum(wide * wide, axis=-1, keepdims=True)
+    square = square + swapped(square)
+    scale = lax.rsqrt(square / (block.shape[1] * sizes[2]) + EPS)
+
+    code = token_owner[0, :, 0] * 2 + token_slot[0]
+    notes = jnp.concatenate([code, jnp.broadcast_to(span_start, (width,))])[None]
+    notes = passed_along(notes, "section", -1)
+    code = notes[:, :tokens]
+    positions = notes[0, tokens] + q * tokens + jnp.arange(tokens, dtype=jnp.int32)
+    half = width // 2
+    freq = jnp.exp(-(jnp.arange(half, dtype=jnp.float32) * 2.0 / width) * math.log(THETA))
+    angle = positions.astype(jnp.float32)[:, None] * freq[None, :]
+    cosine = jnp.cos(angle)
+    sine = jnp.sin(angle)
+
+    query = queries[0, 0]
+    layers, reqs, steps, heads, flat = query.shape
+    rows = reqs * steps * flat // width
+    asked = query.reshape(layers, reqs, steps, heads, flat // width, width)
+    asked = asked.transpose(0, 3, 1, 2, 4, 5).reshape(layers, heads, rows, width)
+    asked = lax.all_to_all(
+        jnp.roll(asked, -1, axis=0), "section", split_axis=0, concat_axis=0, tiled=True
+    )
+
+    keys = summed_over_chips(partial_products(same, acts, (keys_a, keys_b)), sizes)
+    values = [
+        summed_over_chips(partial_products(same, acts, (v,)), sizes) for v in (values_0, values_1)
+    ]
+    routed = attend_routed(asked, keys, values, scale, cosine, sine, code)
+    routed = lax.all_to_all(routed, "section", split_axis=0, concat_axis=0, tiled=True)
+    routed = jnp.roll(routed, 1, axis=0)
+    routed = routed.reshape(layers, heads, reqs, steps, flat // width, 2 * width)
+    routed = routed.transpose(0, 2, 1, 3, 4, 5).astype(jnp.float32)
+    level = jnp.sum(routed[..., width : width + 3], axis=-1, keepdims=True)
+    mixed, top, total = attend_kept(query, kv_cache[0, 0], cache_lens[0, 0], step_kv[0, 0])
+    peak = jnp.maximum(level, top)
+    kept_part = jnp.exp(top - peak)
+    routed_part = jnp.exp(level - peak)
+    result = (mixed * kept_part + routed[..., :width] * routed_part) / (
+        total * kept_part + routed_part
+    )
+    result = result.astype(jnp.bfloat16).transpose(0, 1, 3, 2, 4, 5)
+    return result.reshape(layers, reqs, steps, heads, flat)[None, None]
+
+
 def solution(mesh):
+    shape = mesh.shape
+    body = meet_local if shape["group"] == shape["seq"] == shape["tp"] == 2 else local
     return jax.shard_map(
-        local,
+        body,
         mesh=mesh,
         in_specs=(
             P(("group", "section"), "seq", "tp"),

time: 186 us -> 115 us (0.62)
  waiting for transfers between devices: 118 us -> 20.6 us
  starting transfers between devices: 10.9 us -> 36.7 us
  Pallas kernels: 0 us -> 25.2 us
  between operations: 14.3 us -> 1.71 us
  matrix products: 10.4 us -> 1.14 us
  local copies, waits for them, and re-layouts: 26.3 us -> 20.8 us
  other arithmetic: 5.54 us -> 7.81 us
    ppermute x1 -> x5, waiting for transfers between devices: 70.3 us -> 0.65 us  [passed_along(): lax.ppermute(value, axis, [(i, (i + by) % length) for i in range(length)])]
    all_gather x2 -> x0, waiting for transfers between devices: 27.5 us -> none  [the longest x1 27.5 us: local(): piece = lax.all_gather(weight, 'seq', axis=0, tiled=True)]
    pallas_call x0 -> x7, Pallas kernels: none -> 25.2 us  [the longest x3 13.1 us: partial_products(): pl.pallas_call(body, out_shape=[jax.ShapeDtypeStruct((tokens, columns), j...]
    reshape x5 -> x0, local copies, waits for them, and re-layouts: 23.4 us -> none  [the longest x1 21.6 us: local(): piece.reshape(piece.shape[0], columns_out)]
    ppermute x0 -> x14, starting transfers between devices: none -> 17.2 us  [the longest x11 15.7 us: steered(): return lax.ppermute(value, ('group', 'seq', 'tp'), pairs)]
    ppermute x0 -> x14, waiting for transfers between devices: none -> 14.3 us  [the longest x11 14.3 us: steered(): return lax.ppermute(value, ('group', 'seq', 'tp'), pairs)]
    all_to_all x2, waiting for transfers between devices: 19.1 us -> 5.65 us  [the longest x1 5.65 us: meet_local(): lax.all_to_all(routed, 'section', split_axis=0, concat_axis=0, tiled=True)]
    dynamic_slice x0 -> x5, local copies, waits for them, and re-layouts: none -> 11.4 us  [the longest x3 6.82 us: piece(): lax.dynamic_slice(weight, (g * depth + start, 0, column * width), (rows,...]
  transfers between devices with their start and end apart: 5 -> 21, of which waited for: 3 -> 5; matrix products, arithmetic and copies ran while one was open for 20% -> 19% of each run, Pallas kernels for 0% -> 19%
where the time goes in v1:
time: 115 us; the launch traced here: 114 us
  starting transfers between devices  36.7 us (32%)
  Pallas kernels  25.2 us (22%)
  local copies, waits for them, and re-layouts  20.8 us (18%)
  waiting for transfers between devices  20.6 us (18%)
  other arithmetic  7.81 us (7%)
  between operations  1.71 us (1%)
    ppermute x11, starting transfers between devices, steered(): return lax.ppermute(value, ('group', 'seq', 'tp'), pairs)  15.7 us
    ppermute x11, waiting for transfers between devices, steered(): return lax.ppermute(value, ('group', 'seq', 'tp'), pairs)  14.3 us
    pallas_call x3, Pallas kernels, partial_products(): pl.pallas_call(body, out_shape=[jax.ShapeDtypeStruct((tokens, columns), j...  13.1 us
    ppermute x5, starting transfers between devices, passed_along(): lax.ppermute(value, axis, [(i, (i + by) % length) for i in range(length)])  12.2 us
    pallas_call x3, Pallas kernels, split_heads(): pl.pallas_call(body, out_shape=shapes, grid=(blocks,), in_specs=[pl.Block...  8.44 us
    dynamic_slice x3, local copies, waits for them, and re-layouts, piece(): lax.dynamic_slice(weight, (g * depth + start, 0, column * width), (rows,...  6.82 us
    all_to_all x1, waiting for transfers between devices, meet_local(): lax.all_to_all(routed, 'section', split_axis=0, concat_axis=0, tiled=True)  5.65 us
    dynamic_slice x1, local copies, waits for them, and re-layouts, meet_local(): far = lax.dynamic_slice_in_dim(block, (sizes[0] - 1 - g) * depth, depth, 1)  3.97 us
  transfers between devices with their start and end apart: 21, of which 5 were waited for; matrix products, arithmetic and copies ran while one was open for 19% of the time, Pallas kernels for 19%

profile of v1, /device:TPU:0, one launch (start us, length us, event | category | flops | bytes accessed | tf_op | source)
XLA Modules:
  0.0 114.0 jit_solution(1083796884216697337)
XLA Ops:
  0.0 4.0 %dynamic-slice_bitcast_fusion = (bf16[384,2048]{1,0:T(8,128)(2,1)}, bf16[384,2048]{1,0:T(8,128)(2,1)}) fusion(bf16[1,384,4096]{2,1,0:T(8,128)(2,1)} %param.10, s32[]{:T(128)S(6)} %select_n.25, s32[]{:T(128)S(6)} %select_n.24), kind=kLoop, calls=%fused_computation.1 | loop fusion | bytes 6291464 | tf_op jit(solution)/shard_map/dynamic_slice | solution.py:424
  4.0 2.1 %collective-permute-start = (bf16[384,2048]{1,0:T(8,128)(2,1)}, bf16[384,2048]{1,0:T(8,128)(2,1)S(1)}, u32[]{:S(2)}, u32[]{:S(2)}) collective-permute-start(bf16[384,2048]{1,0:T(8,128)(2,1)} %get-tuple-element.37), channel_id=1, source_target_pairs={{0,0},{1,2},{2,1},{3,3},{16,16},{17,18},{18,17},{19,19},{4,4},{5,6... | collective-permute-start | bytes 4718600 | tf_op jit(solution)/shard_map/ppermute | solution.py:172
  6.0 3.0 %collective-permute-start.2 = (bf16[384,2048]{1,0:T(8,128)(2,1)}, bf16[384,2048]{1,0:T(8,128)(2,1)S(1)}, u32[]{:S(2)}, u32[]{:S(2)}) collective-permute-start(bf16[384,2048]{1,0:T(8,128)(2,1)} %get-tuple-element.36), channel_id=1, source_target_pairs={{0,16},{1,18},{2,17},{3,19},{16,0},{17,2},{18,1},{19,3},{4,20},{5,... | collective-permute-start | bytes 4718600 | tf_op jit(solution)/shard_map/ppermute | solution.py:172
  9.0 2.6 %constant_dynamic-slice_fusion.2 = bf16[1,2048,2,128]{3,2,1,0:T(2,128)(2,1)} fusion(bf16[1,4096,2,256]{3,2,1,0:T(2,128)(2,1)} %param.12, s32[]{:T(128)S(6)} %select_n.24), kind=kLoop, calls=%fused_computation.46 | loop fusion | bytes 2097156 | tf_op jit(solution)/shard_map/dynamic_slice | solution.py:410
  12.2 3.6 %split_heads.5 = (bf16[2048,128]{1,0:T(8,128)(2,1)}, bf16[2048,128]{1,0:T(8,128)(2,1)}) custom-call(bf16[4096,128]{1,0:T(8,128)(2,1)} %bitcast.58, f32[1,2048]{1,0:T(1,128)} %constant_dynamic-slice_fusion.4.gain_ref), custom_call_target="tpu_custom_call" | custom-call | tf_op jit(solution)/shard_map/split_heads/pallas_call | solution.py:207
  15.8 3.6 %collective-permute-start.13 = (bf16[2048,128]{1,0:T(8,128)(2,1)}, bf16[2048,128]{1,0:T(8,128)(2,1)}, u32[]{:S(2)}, u32[]{:S(2)}) collective-permute-start(bf16[2048,128]{1,0:T(8,128)(2,1)} %get-tuple-element.28), channel_id=1, source_target_pairs={{0,12},{4,0},{8,4},{12,8},{1,13},{5,1},{9,5},{13,9},{2,14},{6,2},{... | collective-permute-start | bytes 1572872 | tf_op jit(solution)/shard_map/ppermute | solution.py:17
  19.4 2.4 %constant_dynamic-slice_fusion.3 = bf16[1,1536,2,128]{3,2,1,0:T(2,128)(2,1)} fusion(bf16[1,4096,2,256]{3,2,1,0:T(2,128)(2,1)} %param.12, s32[]{:T(128)S(6)} %select_n.27), kind=kLoop, calls=%fused_computation.47 | loop fusion | bytes 1572868 | tf_op jit(solution)/shard_map/dynamic_slice | solution.py:410
  22.4 3.0 %split_heads.4 = bf16[1536,256]{1,0:T(8,128)(2,1)} custom-call(bf16[3072,128]{1,0:T(8,128)(2,1)} %bitcast.59, f32[1,1536]{1,0:T(1,128)} %constant_dynamic-slice_fusion.gain_ref), custom_call_target="tpu_custom_call" | custom-call | tf_op jit(solution)/shard_map/split_heads/pallas_call | solution.py:207
  27.4 3.9 %all-to-all-start = ((bf16[4,2,32,128]{3,2,1,0:T(8,128)(2,1)}), bf16[4,2,32,128]{3,2,1,0:T(8,128)(2,1)}, u32[]{:S(2)}, u32[]{:S(2)}) async-start(bf16[4,2,32,128]{3,2,1,0:T(8,128)(2,1)} %pad_maximum_fusion.1), calls=%async_computation | async-start | bytes 131072 | tf_op jit(solution)/shard_map/all_to_all | solution.py:451
  31.3 2.6 %multiply_reduce_fusion = f32[384]{0:T(512)S(1)} fusion(bf16[1,384,4096]{2,1,0:T(8,128)(2,1)} %param.10), kind=kLoop, calls=%fused_computation | loop fusion | flops 4718208 | bytes 3147264 | tf_op jit(solution)/shard_map/reduce_sum | solution.py:431
  34.7 9.4 %collective-permute-done.2.far_ref = bf16[384,2048]{1,0:T(8,128)(2,1)S(1)} collective-permute-done((bf16[384,2048]{1,0:T(8,128)(2,1)}, bf16[384,2048]{1,0:T(8,128)(2,1)S(1)}, u32[]{:S(2)}, u32[]{:S(2)}) %collective-permute-start.2) | collective-permute-done | bytes 1572896 | tf_op jit(solution)/shard_map/ppermute | solution.py:172
  45.9 1.9 %constant_dynamic-slice_fusion.5 = bf16[1,512,2,128]{3,2,1,0:T(2,128)(2,1)} fusion(bf16[1,4096,2,256]{3,2,1,0:T(2,128)(2,1)} %param.12, s32[]{:T(128)S(6)} %select_n.24), kind=kLoop, calls=%fused_computation.49 | loop fusion | bytes 524292 | tf_op jit(solution)/shard_map/dynamic_slice | solution.py:410
  48.5 4.1 %collective-permute-start.18 = (s32[1,512]{1,0:T(1,128)S(1)}, s32[1,512]{1,0:T(1,128)S(1)}, u32[]{:S(2)}, u32[]{:S(2)}) collective-permute-start(s32[1,512]{1,0:T(1,128)S(1)} %bitcast.70), channel_id=1, source_target_pairs={{0,12},{4,0},{8,4},{12,8},{1,13},{5,1},{9,5},{13,9},{2,14},{6,2},{... | collective-permute-start | bytes 6152 | tf_op jit(solution)/shard_map/ppermute | solution.py:17
  53.9 4.1 %collective-permute-start.9 = (bf16[2048,128]{1,0:T(8,128)(2,1)}, bf16[2048,128]{1,0:T(8,128)(2,1)}, u32[]{:S(2)}, u32[]{:S(2)}) collective-permute-start(bf16[2048,128]{1,0:T(8,128)(2,1)} %get-tuple-element.23), channel_id=1, source_target_pairs={{0,12},{4,0},{8,4},{12,8},{1,13},{5,1},{9,5},{13,9},{2,14},{6,2},{... | collective-permute-start | bytes 1572872 | tf_op jit(solution)/shard_map/ppermute | solution.py:17
  66.1 3.8 %partial_products.5 = (f32[384,128]{1,0:T(8,128)S(1)}, bf16[384,128]{1,0:T(8,128)(2,1)S(1)}, bf16[384,128]{1,0:T(8,128)(2,1)S(1)}, bf16[384,128]{1,0:T(8,128)(2,1)S(1)}) custom-call(s32[1]{0:T(128)} %bitcast.14.same_ref, bf16[384,2048]{1,0:T(8,128)(2,1)S(1)} %collective-permute-done.near_ref, bf16[384,2048]{1,0:T(8,128)(2,1)} %collective-permute-done.1.near_mate_ref, ...), custom_call_target="tpu_custom_call" | custom-call | tf_op jit(solution)/shard_map/partial_products/pallas_call | solution.py:255
  74.1 4.4 %partial_products.4 = (f32[384,128]{1,0:T(8,128)S(1)}, bf16[384,128]{1,0:T(8,128)(2,1)S(1)}, bf16[384,128]{1,0:T(8,128)(2,1)}, bf16[384,128]{1,0:T(8,128)(2,1)S(1)}) custom-call(s32[1]{0:T(128)} %bitcast.14.same_ref, bf16[384,2048]{1,0:T(8,128)(2,1)S(1)} %collective-permute-done.near_ref, bf16[384,2048]{1,0:T(8,128)(2,1)} %collective-permute-done.1.near_mate_ref, ...), custom_call_target="tpu_custom_call" | custom-call | tf_op jit(solution)/shard_map/partial_products/pallas_call | solution.py:255
  81.0 4.9 %partial_products.3 = (f32[384,256]{1,0:T(8,128)S(1)}, bf16[384,256]{1,0:T(8,128)(2,1)}, bf16[384,256]{1,0:T(8,128)(2,1)}, bf16[384,256]{1,0:T(8,128)(2,1)}) custom-call(s32[1]{0:T(128)} %bitcast.14.same_ref, bf16[384,2048]{1,0:T(8,128)(2,1)S(1)} %collective-permute-done.near_ref, bf16[384,2048]{1,0:T(8,128)(2,1)} %collective-permute-done.1.near_mate_ref, ...), custom_call_target="tpu_custom_call" | custom-call | tf_op jit(solution)/shard_map/partial_products/pallas_call | solution.py:255
  86.6 1.8 %collective-permute-start.12 = (bf16[384,128]{1,0:T(8,128)(2,1)S(1)}, bf16[384,128]{1,0:T(8,128)(2,1)S(1)}, u32[]{:S(2)}, u32[]{:S(2)}) collective-permute-start(bf16[384,128]{1,0:T(8,128)(2,1)S(1)} %get-tuple-element.27), channel_id=1, source_target_pairs={{0,18},{1,19},{2,16},{3,17},{16,2},{17,3},{18,0},{19,1},{4,22},{5,... | collective-permute-start | bytes 294920 | tf_op jit(solution)/shard_map/ppermute | solution.py:172
  90.2 1.8 %collective-permute-start.8 = (bf16[384,256]{1,0:T(8,128)(2,1)}, bf16[384,256]{1,0:T(8,128)(2,1)S(1)}, u32[]{:S(2)}, u32[]{:S(2)}) collective-permute-start(bf16[384,256]{1,0:T(8,128)(2,1)} %get-tuple-element.22), channel_id=1, source_target_pairs={{0,18},{1,19},{2,16},{3,17},{16,2},{17,3},{18,0},{19,1},{4,22},{5,... | collective-permute-start | bytes 589832 | tf_op jit(solution)/shard_map/ppermute | solution.py:172
  94.2 2.1 %collective-permute-done.6.rest_1_ = bf16[384,256]{1,0:T(8,128)(2,1)S(1)} collective-permute-done((bf16[384,256]{1,0:T(8,128)(2,1)}, bf16[384,256]{1,0:T(8,128)(2,1)S(1)}, u32[]{:S(2)}, u32[]{:S(2)}) %collective-permute-start.6) | collective-permute-done | bytes 196640 | tf_op jit(solution)/shard_map/ppermute | solution.py:172
  96.4 2.7 %collective-permute-done.7.rest_2_ = bf16[384,256]{1,0:T(8,128)(2,1)S(1)} collective-permute-done((bf16[384,256]{1,0:T(8,128)(2,1)}, bf16[384,256]{1,0:T(8,128)(2,1)S(1)}, u32[]{:S(2)}, u32[]{:S(2)}) %collective-permute-start.7) | collective-permute-done | bytes 196640 | tf_op jit(solution)/shard_map/ppermute | solution.py:172
  99.9 3.7 %attend_routed.1 = bf16[4,2,32,256]{3,2,1,0:T(8,128)(2,1)} custom-call(bf16[4,2,32,128]{3,2,1,0:T(8,128)(2,1)} %all-to-all-done.asked_ref, f32[384,256]{1,0:T(8,128)} %copy-done.1, bf16[384,256]{1,0:T(8,128)(2,1)} %copy-done.9, bf16[384,256]{1,0:T(8,128)(2,1)} %copy-done.10, bf16[384,256]{1,0:T(8,128)(2,1)} %copy-done.11, f32[384,128]{1,0:T(8,128)} %copy-done.3, ...), custom_call_target="tpu_custom_call" | custom-call | tf_op jit(solution)/shard_map/attend_routed/pallas_call | solution.py:339
  103.6 3.3 %all-to-all-start.1 = ((bf16[4,2,32,256]{3,2,1,0:T(8,128)(2,1)}), bf16[4,2,32,256]{3,2,1,0:T(8,128)(2,1)S(1)}, u32[]{:S(2)}, u32[]{:S(2)}) async-start(bf16[4,2,32,256]{3,2,1,0:T(8,128)(2,1)} %attend_routed.1), calls=%async_computation.1 | async-start | bytes 262144 | tf_op jit(solution)/shard_map/all_to_all | solution.py:460
  107.2 5.7 %all-to-all-done.1 = bf16[4,2,32,256]{3,2,1,0:T(8,128)(2,1)S(1)} async-done(((bf16[4,2,32,256]{3,2,1,0:T(8,128)(2,1)}), bf16[4,2,32,256]{3,2,1,0:T(8,128)(2,1)S(1)}, u32[]{:S(2)}, u32[]{:S(2)}) %all-to-all-start.1) | async-done | bytes 131104 | tf_op jit(solution)/shard_map/all_to_all | solution.py:460
  (130 shorter events, 27.9 us)
Async XLA Ops:
  4.0 30.5 %collective-permute-start = (bf16[384,2048]{1,0:T(8,128)(2,1)}, bf16[384,2048]{1,0:T(8,128)(2,1)S(1)}, u32[]{:S(2)}, u32[]{:S(2)}) collective-permute-start(bf16[384,2048]{1,0:T(8,128)(2,1)} %get-tuple-element.37), channel_id=1, source_target_pairs={{0,0},{1,2},{2,1},{3,3},{16,16},{17,18},{18,17},{19,19},{4,4},{5,6... | collective-permute-start | bytes 4718600 | tf_op jit(solution)/shard_map/ppermute | solution.py:172
  6.0 38.1 %collective-permute-start.2 = (bf16[384,2048]{1,0:T(8,128)(2,1)}, bf16[384,2048]{1,0:T(8,128)(2,1)S(1)}, u32[]{:S(2)}, u32[]{:S(2)}) collective-permute-start(bf16[384,2048]{1,0:T(8,128)(2,1)} %get-tuple-element.36), channel_id=1, source_target_pairs={{0,16},{1,18},{2,17},{3,19},{16,0},{17,2},{18,1},{19,3},{4,20},{5,... | collective-permute-start | bytes 4718600 | tf_op jit(solution)/shard_map/ppermute | solution.py:172
  15.8 45.3 %collective-permute-start.13 = (bf16[2048,128]{1,0:T(8,128)(2,1)}, bf16[2048,128]{1,0:T(8,128)(2,1)}, u32[]{:S(2)}, u32[]{:S(2)}) collective-permute-start(bf16[2048,128]{1,0:T(8,128)(2,1)} %get-tuple-element.28), channel_id=1, source_target_pairs={{0,12},{4,0},{8,4},{12,8},{1,13},{5,1},{9,5},{13,9},{2,14},{6,2},{... | collective-permute-start | bytes 1572872 | tf_op jit(solution)/shard_map/ppermute | solution.py:17
  25.4 55.0 %collective-permute-start.5 = (bf16[1536,256]{1,0:T(8,128)(2,1)}, bf16[1536,256]{1,0:T(8,128)(2,1)}, u32[]{:S(2)}, u32[]{:S(2)}) collective-permute-start(bf16[1536,256]{1,0:T(8,128)(2,1)} %split_heads.4), channel_id=1, source_target_pairs={{0,12},{4,0},{8,4},{12,8},{1,13},{5,1},{9,5},{13,9},{2,14},{6,2},{... | collective-permute-start | bytes 2359304 | tf_op jit(solution)/shard_map/ppermute | solution.py:17
  27.4 66.8 %all-to-all-start = ((bf16[4,2,32,128]{3,2,1,0:T(8,128)(2,1)}), bf16[4,2,32,128]{3,2,1,0:T(8,128)(2,1)}, u32[]{:S(2)}, u32[]{:S(2)}) async-start(bf16[4,2,32,128]{3,2,1,0:T(8,128)(2,1)} %pad_maximum_fusion.1), calls=%async_computation | async-start | bytes 131072 | tf_op jit(solution)/shard_map/all_to_all | solution.py:451
  33.9 14.6 %collective-permute-start.17 = (f32[384,1]{0,1:T(1,128)S(1)}, f32[384,1]{0,1:T(1,128)}, u32[]{:S(2)}, u32[]{:S(2)}) collective-permute-start(f32[384,1]{0,1:T(1,128)S(1)} %broadcast_in_dim.59), channel_id=1, source_target_pairs={{0,1},{1,0},{2,3},{3,2},{4,5},{5,4},{6,7},{7,6},{8,9},{9,8},{10,11... | collective-permute-start | bytes 4616 | tf_op jit(solution)/shard_map/ppermute | solution.py:176
  34.5 31.6 %collective-permute-start.1 = (bf16[384,2048]{1,0:T(8,128)(2,1)S(1)}, bf16[384,2048]{1,0:T(8,128)(2,1)}, u32[]{:S(2)}, u32[]{:S(2)}) collective-permute-start(bf16[384,2048]{1,0:T(8,128)(2,1)S(1)} %collective-permute-done.near_ref), channel_id=1, source_target_pairs={{0,1},{1,0},{2,3},{3,2},{4,5},{5,4},{6,7},{7,6},{8,9},{9,8},{10,11... | collective-permute-start | bytes 4718600 | tf_op jit(solution)/shard_map/ppermute | solution.py:176
  44.1 22.0 %collective-permute-start.3 = (bf16[384,2048]{1,0:T(8,128)(2,1)S(1)}, bf16[384,2048]{1,0:T(8,128)(2,1)}, u32[]{:S(2)}, u32[]{:S(2)}) collective-permute-start(bf16[384,2048]{1,0:T(8,128)(2,1)S(1)} %collective-permute-done.2.far_ref), channel_id=1, source_target_pairs={{0,1},{1,0},{2,3},{3,2},{4,5},{5,4},{6,7},{7,6},{8,9},{9,8},{10,11... | collective-permute-start | bytes 4718600 | tf_op jit(solution)/shard_map/ppermute | solution.py:176
  48.5 5.4 %collective-permute-start.18 = (s32[1,512]{1,0:T(1,128)S(1)}, s32[1,512]{1,0:T(1,128)S(1)}, u32[]{:S(2)}, u32[]{:S(2)}) collective-permute-start(s32[1,512]{1,0:T(1,128)S(1)} %bitcast.70), channel_id=1, source_target_pairs={{0,12},{4,0},{8,4},{12,8},{1,13},{5,1},{9,5},{13,9},{2,14},{6,2},{... | collective-permute-start | bytes 6152 | tf_op jit(solution)/shard_map/ppermute | solution.py:17
  53.9 18.4 %collective-permute-start.9 = (bf16[2048,128]{1,0:T(8,128)(2,1)}, bf16[2048,128]{1,0:T(8,128)(2,1)}, u32[]{:S(2)}, u32[]{:S(2)}) collective-permute-start(bf16[2048,128]{1,0:T(8,128)(2,1)} %get-tuple-element.23), channel_id=1, source_target_pairs={{0,12},{4,0},{8,4},{12,8},{1,13},{5,1},{9,5},{13,9},{2,14},{6,2},{... | collective-permute-start | bytes 1572872 | tf_op jit(solution)/shard_map/ppermute | solution.py:17
  61.1 18.0 %collective-permute-start.4 = (bf16[512,256]{1,0:T(8,128)(2,1)}, bf16[512,256]{1,0:T(8,128)(2,1)S(1)}, u32[]{:S(2)}, u32[]{:S(2)}) collective-permute-start(bf16[512,256]{1,0:T(8,128)(2,1)} %split_heads.3), channel_id=1, source_target_pairs={{0,12},{4,0},{8,4},{12,8},{1,13},{5,1},{9,5},{13,9},{2,14},{6,2},{... | collective-permute-start | bytes 786440 | tf_op jit(solution)/shard_map/ppermute | solution.py:17
  70.6 16.1 %collective-permute-start.14 = (bf16[384,128]{1,0:T(8,128)(2,1)S(1)}, bf16[384,128]{1,0:T(8,128)(2,1)S(1)}, u32[]{:S(2)}, u32[]{:S(2)}) collective-permute-start(bf16[384,128]{1,0:T(8,128)(2,1)S(1)} %get-tuple-element.30), channel_id=1, source_target_pairs={{0,2},{1,3},{2,0},{3,1},{16,18},{17,19},{18,16},{19,17},{4,6},{5,7... | collective-permute-start | bytes 294920 | tf_op jit(solution)/shard_map/ppermute | solution.py:172
  71.8 16.7 %collective-permute-start.15 = (bf16[384,128]{1,0:T(8,128)(2,1)S(1)}, bf16[384,128]{1,0:T(8,128)(2,1)S(1)}, u32[]{:S(2)}, u32[]{:S(2)}) collective-permute-start(bf16[384,128]{1,0:T(8,128)(2,1)S(1)} %get-tuple-element.31), channel_id=1, source_target_pairs={{0,16},{1,17},{2,18},{3,19},{16,0},{17,1},{18,2},{19,3},{4,20},{5,... | collective-permute-start | bytes 294920 | tf_op jit(solution)/shard_map/ppermute | solution.py:172
  72.3 17.4 %collective-permute-start.16 = (bf16[384,128]{1,0:T(8,128)(2,1)S(1)}, bf16[384,128]{1,0:T(8,128)(2,1)S(1)}, u32[]{:S(2)}, u32[]{:S(2)}) collective-permute-start(bf16[384,128]{1,0:T(8,128)(2,1)S(1)} %get-tuple-element.32), channel_id=1, source_target_pairs={{0,18},{1,19},{2,16},{3,17},{16,2},{17,3},{18,0},{19,1},{4,22},{5,... | collective-permute-start | bytes 294920 | tf_op jit(solution)/shard_map/ppermute | solution.py:172
  79.2 11.1 %collective-permute-start.10 = (bf16[384,128]{1,0:T(8,128)(2,1)S(1)}, bf16[384,128]{1,0:T(8,128)(2,1)S(1)}, u32[]{:S(2)}, u32[]{:S(2)}) collective-permute-start(bf16[384,128]{1,0:T(8,128)(2,1)S(1)} %get-tuple-element.25), channel_id=1, source_target_pairs={{0,2},{1,3},{2,0},{3,1},{16,18},{17,19},{18,16},{19,17},{4,6},{5,7... | collective-permute-start | bytes 294920 | tf_op jit(solution)/shard_map/ppermute | solution.py:172
  80.4 13.8 %collective-permute-start.11 = (bf16[384,128]{1,0:T(8,128)(2,1)}, bf16[384,128]{1,0:T(8,128)(2,1)}, u32[]{:S(2)}, u32[]{:S(2)}) collective-permute-start(bf16[384,128]{1,0:T(8,128)(2,1)} %get-tuple-element.26), channel_id=1, source_target_pairs={{0,16},{1,17},{2,18},{3,19},{16,0},{17,1},{18,2},{19,3},{4,20},{5,... | collective-permute-start | bytes 294920 | tf_op jit(solution)/shard_map/ppermute | solution.py:172
  86.6 26.4 %copy-start.20 = (f32[4,2,2,2,8]{4,3,2,1,0:T(2,128)S(1)}, f32[4,2,2,2,8]{4,3,2,1,0:T(2,128)}, u32[]{:S(2)}) copy-start(f32[4,2,2,2,8]{4,3,2,1,0:T(2,128)} %fusion.13) | copy-start | bytes 3076
  86.6 26.5 %copy-start.5 = (bf16[1,1,4,2,32,2,256]{6,4,5,3,2,1,0:T(8,128)(2,1)S(1)}, bf16[1,1,4,2,32,2,256]{6,4,5,3,2,1,0:T(8,128)(2,1)}, u32[]{:S(2)}) copy-start(bf16[1,1,4,2,32,2,256]{6,4,5,3,2,1,0:T(8,128)(2,1)} %copy-done.4) | copy-start | bytes 786436
  86.6 26.5 %copy-start.7 = (f32[4,2,2,2,8,32]{5,4,3,2,1,0:T(8,128)S(1)}, f32[4,2,2,2,8,32]{5,4,3,2,1,0:T(8,128)}, u32[]{:S(2)}) copy-start(f32[4,2,2,2,8,32]{5,4,3,2,1,0:T(8,128)} %copy-done.6) | copy-start | bytes 98308
  86.6 7.6 %collective-permute-start.12 = (bf16[384,128]{1,0:T(8,128)(2,1)S(1)}, bf16[384,128]{1,0:T(8,128)(2,1)S(1)}, u32[]{:S(2)}, u32[]{:S(2)}) collective-permute-start(bf16[384,128]{1,0:T(8,128)(2,1)S(1)} %get-tuple-element.27), channel_id=1, source_target_pairs={{0,18},{1,19},{2,16},{3,17},{16,2},{17,3},{18,0},{19,1},{4,22},{5,... | collective-permute-start | bytes 294920 | tf_op jit(solution)/shard_map/ppermute | solution.py:172
  88.5 7.9 %collective-permute-start.6 = (bf16[384,256]{1,0:T(8,128)(2,1)}, bf16[384,256]{1,0:T(8,128)(2,1)S(1)}, u32[]{:S(2)}, u32[]{:S(2)}) collective-permute-start(bf16[384,256]{1,0:T(8,128)(2,1)} %get-tuple-element.20), channel_id=1, source_target_pairs={{0,2},{1,3},{2,0},{3,1},{16,18},{17,19},{18,16},{19,17},{4,6},{5,7... | collective-permute-start | bytes 589832 | tf_op jit(solution)/shard_map/ppermute | solution.py:172
  89.7 9.4 %collective-permute-start.7 = (bf16[384,256]{1,0:T(8,128)(2,1)}, bf16[384,256]{1,0:T(8,128)(2,1)S(1)}, u32[]{:S(2)}, u32[]{:S(2)}) collective-permute-start(bf16[384,256]{1,0:T(8,128)(2,1)} %get-tuple-element.21), channel_id=1, source_target_pairs={{0,16},{1,17},{2,18},{3,19},{16,0},{17,1},{18,2},{19,3},{4,20},{5,... | collective-permute-start | bytes 589832 | tf_op jit(solution)/shard_map/ppermute | solution.py:172
  90.2 8.9 %collective-permute-start.8 = (bf16[384,256]{1,0:T(8,128)(2,1)}, bf16[384,256]{1,0:T(8,128)(2,1)S(1)}, u32[]{:S(2)}, u32[]{:S(2)}) collective-permute-start(bf16[384,256]{1,0:T(8,128)(2,1)} %get-tuple-element.22), channel_id=1, source_target_pairs={{0,18},{1,19},{2,16},{3,17},{16,2},{17,3},{18,0},{19,1},{4,22},{5,... | collective-permute-start | bytes 589832 | tf_op jit(solution)/shard_map/ppermute | solution.py:172
  103.6 9.2 %all-to-all-start.1 = ((bf16[4,2,32,256]{3,2,1,0:T(8,128)(2,1)}), bf16[4,2,32,256]{3,2,1,0:T(8,128)(2,1)S(1)}, u32[]{:S(2)}, u32[]{:S(2)}) async-start(bf16[4,2,32,256]{3,2,1,0:T(8,128)(2,1)} %attend_routed.1), calls=%async_computation.1 | async-start | bytes 262144 | tf_op jit(solution)/shard_map/all_to_all | solution.py:460
  (27 other events, 290.5 us)

commit v2 on v1

--- a/solution.py
+++ b/solution.py
@@ -176,13 +176,18 @@
     return lax.ppermute(value, "tp", [(0, 1), (1, 0)])
 
 
-def split_heads(mixed, gain, joined, blocks):
-    rows = mixed.shape[0] // 2
-    width = mixed.shape[1]
-    tall = rows // blocks
-
-    def body(mixed_ref, gain_ref, *rest):
-        outs, wide = rest[:-1], rest[-1]
+def after(value, early):
+    return lax.optimization_barrier((value, early))[0]
+
+
+def split_heads(rows4, gain, group, quarter, depth, start, count, blocks, parts, notes=None):
+    width = rows4.shape[1]
+    tall = count // blocks
+    columns = 4 * width // parts
+    extra = 0 if notes is None else 16
+
+    def body(group_ref, quarter_ref, mixed_ref, gain_ref, *rest):
+        outs, wide = rest[len(rest) - 1 - parts : -1], rest[-1]
         wide[...] = mixed_ref[...].astype(jnp.float32)
         gains = jnp.concatenate(
             [
@@ -191,74 +196,144 @@
             ],
             axis=0,
         )
-        for head in range(2):
-            scaled = (wide[pl.ds(head, tall, stride=2), :] * gains).astype(jnp.bfloat16)
-            if joined:
-                outs[0][:, head * width : (head + 1) * width] = scaled
-            else:
-                outs[head][...] = scaled
-
-    if joined:
-        shapes = [jax.ShapeDtypeStruct((rows, 2 * width), jnp.bfloat16)]
-        out_specs = [pl.BlockSpec((tall, 2 * width), lambda i: (i, 0))]
-    else:
-        shapes = [jax.ShapeDtypeStruct((rows, width), jnp.bfloat16)] * 2
-        out_specs = [pl.BlockSpec((tall, width), lambda i: (i, 0))] * 2
+        for kind in range(2):
+            for head in range(2):
+                scaled = wide[pl.ds(2 * kind + head, tall, stride=4), :] * gains
+                column = (2 * kind + head) * width
+                out = outs[column * parts // (4 * width)]
+                column = column % (4 * width // parts)
+                out[:tall, column : column + width] = scaled.astype(jnp.bfloat16)
+        if extra:
+            outs[0][tall:, :] = jnp.broadcast_to(rest[0][...], (extra, columns)).astype(jnp.bfloat16)
+
+    operands = [group, quarter, rows4, gain]
+    in_specs = [
+        pl.BlockSpec(
+            (4 * tall, width),
+            lambda i, group, quarter: (group[0] * (depth // tall) + start // tall + i, 0),
+        ),
+        pl.BlockSpec(
+            (1, tall),
+            lambda i, group, quarter: (0, quarter[0] * (depth // tall) + start // tall + i),
+        ),
+    ]
+    if extra:
+        operands.append(notes)
+        in_specs.append(pl.BlockSpec((1, columns), lambda i, group, quarter: (0, 0)))
     return pl.pallas_call(
         body,
-        out_shape=shapes,
-        grid=(blocks,),
-        in_specs=[
-            pl.BlockSpec((2 * tall, width), lambda i: (i, 0)),
-            pl.BlockSpec((1, tall), lambda i: (0, i)),
-        ],
-        out_specs=out_specs,
-        scratch_shapes=[pltpu.VMEM((2 * tall, width), jnp.float32)],
+        out_shape=[jax.ShapeDtypeStruct((count + extra, columns), jnp.bfloat16)] * parts,
+        grid_spec=pltpu.PrefetchScalarGridSpec(
+            num_scalar_prefetch=2,
+            grid=(blocks,),
+            in_specs=in_specs,
+            out_specs=[pl.BlockSpec((tall + extra, columns), lambda i, group, quarter: (i, 0))]
+            * parts,
+            scratch_shapes=[pltpu.VMEM((4 * tall, width), jnp.float32)],
+        ),
+        compiler_params=pltpu.CompilerParams(vmem_limit_bytes=60 << 20),
         name="split_heads",
-    )(mixed, gain)
-
-
-def partial_products(same, acts, weights):
-    tokens = acts[0].shape[0]
-    columns = weights[0].shape[1]
-    depths = [w.shape[0] for w in weights]
-
-    def body(same_ref, near_ref, near_mate_ref, far_ref, far_mate_ref, *rest):
-        w_refs, outs = rest[: len(depths)], rest[len(depths) :]
-
-        def product(ref):
-            total = None
-            start = 0
-            for w_ref, depth in zip(w_refs, depths):
-                part = jnp.dot(
-                    ref[:, start : start + depth], w_ref[...], preferred_element_type=jnp.float32
-                )
-                total = part if total is None else total + part
-                start += depth
-            return total
-
-        def fill(own, across, far_own, far_across):
-            outs[1][...] = product(across).astype(jnp.bfloat16)
-            outs[2][...] = product(far_own).astype(jnp.bfloat16)
-            outs[3][...] = product(far_across).astype(jnp.bfloat16)
-            outs[0][...] = product(own)
-
-        @pl.when(same_ref[0] == 1)
-        def _():
-            fill(near_ref, near_mate_ref, far_ref, far_mate_ref)
-
-        @pl.when(same_ref[0] == 0)
-        def _():
-            fill(near_mate_ref, near_ref, far_mate_ref, far_ref)
-
-    vmem = pl.BlockSpec(memory_space=pltpu.VMEM)
+    )(*operands)
+
+
+def cut_columns(block, group, depth, cuts):
+    tokens = block.shape[0]
+
+    def body(group_ref, block_ref, *rest):
+        outs, sems = rest[:-1], rest[-1]
+        copies = []
+        for n, (other, start, count) in enumerate(cuts):
+            which = (1 - group_ref[0]) if other else group_ref[0]
+            column = pl.multiple_of(which * depth + start, 128)
+            copies.append(
+                pltpu.make_async_copy(block_ref.at[:, pl.ds(column, count)], outs[n], sems.at[n])
+            )
+        for copy in copies:
+            copy.start()
+        for copy in copies:
+            copy.wait()
+
+    anywhere = pl.BlockSpec(memory_space=pl.ANY)
     return pl.pallas_call(
         body,
-        out_shape=[jax.ShapeDtypeStruct((tokens, columns), jnp.float32)]
-        + [jax.ShapeDtypeStruct((tokens, columns), jnp.bfloat16)] * 3,
-        in_specs=[pl.BlockSpec(memory_space=pltpu.SMEM)] + [vmem] * (4 + len(weights)),
-        out_specs=[vmem] * 4,
-        compiler_params=pltpu.CompilerParams(vmem_limit_bytes=40 << 20),
+        out_shape=[jax.ShapeDtypeStruct((tokens, count), block.dtype) for _, _, count in cuts],
+        in_specs=[pl.BlockSpec(memory_space=pltpu.SMEM), anywhere],
+        out_specs=[pl.BlockSpec(memory_space=pltpu.VMEM)] * len(cuts),
+        scratch_shapes=[pltpu.SemaphoreType.DMA((len(cuts),))],
+        compiler_params=pltpu.CompilerParams(vmem_limit_bytes=60 << 20),
+        name="cut_columns",
+    )(group, block)
+
+
+def partial_products(same, pairs, weights, first_column, columns, first_kind):
+    tokens = pairs[0][0][0].shape[0]
+    depth = pairs[0][0][0].shape[1]
+    acts = [piece for pair in pairs for side in pair for piece in side]
+    count = len(acts) + len(weights)
+
+    def body(same_ref, *refs):
+        act_refs = refs[: len(acts)]
+        weight_refs = refs[len(acts) : count]
+        outs = refs[count : count + 2 * len(pairs)]
+        held, weight, sems = refs[count + 2 * len(pairs) :]
+        weight_copies = []
+        row = 0
+        for n, ref in enumerate(weight_refs):
+            taken = min(ref.shape[0], depth - row) // 128 * 128
+            column = first_column if ref.shape[1] > columns else 0
+            weight_copies.append(
+                pltpu.make_async_copy(
+                    ref.at[pl.ds(0, taken), pl.ds(column, columns)],
+                    weight.at[pl.ds(row, taken), :],
+                    sems.at[len(acts) + n],
+                )
+            )
+            row += taken
+        for copy in weight_copies:
+            copy.start()
+        act_copies = []
+        n = 0
+        for p, pair in enumerate(pairs):
+            mine = []
+            for side in range(2):
+                slot = 2 * p + ((1 - same_ref[0]) if side == 0 else same_ref[0])
+                column = 0
+                for piece in pair[side]:
+                    wide = piece.shape[1]
+                    copy = pltpu.make_async_copy(
+                        act_refs[n], held.at[slot, :, pl.ds(column, wide)], sems.at[n]
+                    )
+                    copy.start()
+                    mine.append(copy)
+                    column += wide
+                    n += 1
+            act_copies.append(mine)
+        for copy in weight_copies:
+            copy.wait()
+        for p in range(len(pairs)):
+            for copy in act_copies[p]:
+                copy.wait()
+            for side in range(2):
+                out = outs[2 * p + side]
+                out[...] = jnp.dot(
+                    held[2 * p + side], weight[...], preferred_element_type=jnp.float32
+                ).astype(out.dtype)
+
+    anywhere = pl.BlockSpec(memory_space=pl.ANY)
+    vmem = pl.BlockSpec(memory_space=pltpu.VMEM)
+    kinds = [jnp.float32, jnp.bfloat16, jnp.bfloat16, jnp.bfloat16]
+    kinds = kinds[first_kind : first_kind + 2 * len(pairs)]
+    return pl.pallas_call(
+        body,
+        out_shape=[jax.ShapeDtypeStruct((tokens, columns), kind) for kind in kinds],
+        in_specs=[pl.BlockSpec(memory_space=pltpu.SMEM)] + [anywhere] * count,
+        out_specs=[vmem] * len(kinds),
+        scratch_shapes=[
+            pltpu.VMEM((2 * len(pairs), tokens, depth), jnp.bfloat16),
+            pltpu.VMEM((depth, columns), jnp.bfloat16),
+            pltpu.SemaphoreType.DMA((count,)),
+        ],
+        compiler_params=pltpu.CompilerParams(vmem_limit_bytes=(5 + 4 * len(pairs)) << 20),
         name="partial_products",
     )(same, *acts, *weights)
 
@@ -274,18 +349,18 @@
     )
 
 
-def attend_routed(asked, keys, values, scale, cosine, sine, code):
+def weigh(asked, keys, square, cosine, sine, code, features):
     owners, heads, rows, width = asked.shape
     tokens = code.shape[1]
     half = width // 2
     requests = 2
     factor = 1.0 / math.sqrt(width)
+    span = owners * rows
 
     def body(asked_ref, *rest):
         key_refs = rest[:4]
-        value_refs = [rest[4 + 4 * h : 8 + 4 * h] for h in range(heads)]
-        scale_ref, cos_ref, sin_ref, code_ref, out_ref = rest[4 + 4 * heads :]
-        span = owners * rows
+        square_ref, cos_ref, sin_ref, code_ref, weight_ref, mark_ref = rest[4:]
+        scale = lax.rsqrt(square_ref[...] / features + EPS)
         request = lax.broadcasted_iota(jnp.int32, (span, tokens), 0) // (rows // requests)
         mine = request == code_ref[...]
         lane = lax.broadcasted_iota(jnp.int32, (span, width), 1)
@@ -294,54 +369,77 @@
             key = key_refs[0][:, columns]
             for ref in key_refs[1:]:
                 key = key + ref[:, columns].astype(jnp.float32)
-            key = key * scale_ref[...]
             first = key[:, :half]
             second = key[:, half:]
-            cosine_ = cos_ref[...]
-            sine_ = sin_ref[...]
             key = jnp.concatenate(
-                [first * cosine_ - second * sine_, second * cosine_ + first * sine_], axis=1
+                [
+                    first * cos_ref[...] - second * sin_ref[...],
+                    second * cos_ref[...] + first * sin_ref[...],
+                ],
+                axis=1,
             ).astype(jnp.bfloat16)
-            value = value_refs[h][0][...]
-            for ref in value_refs[h][1:]:
-                value = value + ref[...].astype(jnp.float32)
-            value = (value * scale_ref[...]).astype(jnp.bfloat16)
             query = jnp.concatenate([asked_ref[o, h] for o in range(owners)], axis=0)
-            score = (
-                lax.dot_general(
-                    query, key, (((1,), (1,)), ((), ())), preferred_element_type=jnp.float32
-                )
-                * factor
-            )
+            score = lax.dot_general(
+                query, key, (((1,), (1,)), ((), ())), preferred_element_type=jnp.float32
+            ) * (scale * factor)
             score = jnp.where(mine, score, NEG)
             top = jnp.max(score, axis=1, keepdims=True)
             weight = jnp.where(mine, jnp.exp(score - top), 0.0)
             total = jnp.sum(weight, axis=1, keepdims=True)
-            mixed = jnp.dot(
-                weight.astype(jnp.bfloat16), value, preferred_element_type=jnp.float32
-            )
             some = total > 0.0
             safe = jnp.where(some, total, 1.0)
-            mixed = (mixed / safe).astype(jnp.bfloat16)
+            weight_ref[h] = (weight / safe * scale).astype(jnp.bfloat16)
             level = jnp.where(some, top + jnp.log(safe), NEG)
             high = level.astype(jnp.bfloat16).astype(jnp.float32)
             middle = (level - high).astype(jnp.bfloat16).astype(jnp.float32)
             low = level - high - middle
-            marks = jnp.where(
+            mark_ref[h] = jnp.where(
                 lane == 0, high, jnp.where(lane == 1, middle, jnp.where(lane == 2, low, 0.0))
+            ).astype(jnp.bfloat16)
+
+    vmem = pl.BlockSpec(memory_space=pltpu.VMEM)
+    operands = (asked, *keys, square, cosine, sine, code)
+    return pl.pallas_call(
+        body,
+        out_shape=[
+            jax.ShapeDtypeStruct((heads, span, tokens), jnp.bfloat16),
+            jax.ShapeDtypeStruct((heads, span, width), jnp.bfloat16),
+        ],
+        in_specs=[vmem] * len(operands),
+        out_specs=[vmem] * 2,
+        compiler_params=pltpu.CompilerParams(vmem_limit_bytes=6 << 20),
+        name="weigh",
+    )(*operands)
+
+
+def mix(weights, marks, values, owners):
+    heads, span, _ = weights.shape
+    width = marks.shape[2]
+    rows = span // owners
+
+    def body(weight_ref, mark_ref, *rest):
+        value_refs, out_ref = rest[:-1], rest[-1]
+        for h in range(heads):
+            columns = slice(h * width, (h + 1) * width)
+            value = value_refs[0][:, columns]
+            for ref in value_refs[1:]:
+                value = value + ref[:, columns].astype(jnp.float32)
+            mixed = jnp.dot(
+                weight_ref[h], value.astype(jnp.bfloat16), preferred_element_type=jnp.float32
             ).astype(jnp.bfloat16)
             for o in range(owners):
                 out_ref[o, h, :, :width] = mixed[o * rows : (o + 1) * rows]
-                out_ref[o, h, :, width:] = marks[o * rows : (o + 1) * rows]
+                out_ref[o, h, :, width:] = mark_ref[h, o * rows : (o + 1) * rows, :]
 
     vmem = pl.BlockSpec(memory_space=pltpu.VMEM)
-    operands = (asked, *keys, *[v for chunk in values for v in chunk], scale, cosine, sine, code)
+    operands = (weights, marks, *values)
     return pl.pallas_call(
         body,
         out_shape=jax.ShapeDtypeStruct((owners, heads, rows, 2 * width), jnp.bfloat16),
         in_specs=[vmem] * len(operands),
         out_specs=vmem,
-        name="attend_routed",
+        compiler_params=pltpu.CompilerParams(vmem_limit_bytes=4 << 20),
+        name="mix",
     )(*operands)
 
 
@@ -402,48 +500,53 @@
     weight = kv_weight[0]
     depth = weight.shape[0] // sizes[0]
     width = weight.shape[2] // 2
-    first = depth // 4
-
-    gain = lax.dynamic_slice_in_dim(norm_gain[0], (q * sizes[0] + g) * depth, depth, 0)[None]
-
-    def piece(start, rows, column):
-        cut = lax.dynamic_slice(weight, (g * depth + start, 0, column * width), (rows, 2, width))
-        return cut.reshape(2 * rows, width)
-
-    (keys_a,) = split_heads(piece(0, first, 0), gain[:, :first], True, 1)
-    (keys_b,) = split_heads(piece(first, depth - first, 0), gain[:, first:], True, 3)
-    values_0, values_1 = split_heads(piece(0, depth, 1), gain, False, 4)
-    keys_a = passed_along(keys_a, "section", -1)
-    keys_b = passed_along(keys_b, "section", -1)
-    values_0 = passed_along(values_0, "section", -1)
-    values_1 = passed_along(values_1, "section", -1)
-
+    first = depth // 8
     block = handoff[0]
     tokens = block.shape[0]
-    near = lax.dynamic_slice_in_dim(block, g * depth, depth, 1)
-    far = lax.dynamic_slice_in_dim(block, (sizes[0] - 1 - g) * depth, depth, 1)
-    near = steered(near, lambda a, b, c: (a, c, b), sizes)
-    far = steered(far, lambda a, b, c: (sizes[0] - 1 - a, c, b), sizes)
-    acts = (near, swapped(near), far, swapped(far))
+
+    code = token_owner[0, :, 0] * 2 + token_slot[0]
+    where = jnp.stack([span_start[0] // 64, span_start[0] % 64])
+    notes = jnp.concatenate([code, where, jnp.zeros((4 * width - tokens - 2,), jnp.int32)])
+    notes = notes.astype(jnp.float32)[None]
+
+    rows4 = weight.reshape(weight.shape[0], 2, 2, width).transpose(0, 2, 1, 3).reshape(-1, width)
+    group = g.astype(jnp.int32)[None]
+    quarter = (q * sizes[0] + g).astype(jnp.int32)[None]
+    (head_start,) = split_heads(
+        rows4, norm_gain, group, quarter, depth, 0, first, 1, 1, notes
+    )
+    start_got = passed_along(head_start, "section", -1)
+
+    cuts = ((False, 0, depth), (True, 0, depth))
+    near, far = cut_columns(after(block, head_start), group, depth, cuts)
+    near_got = steered(near, lambda a, b, c: (a, c, b), sizes)
+    far_got = steered(far, lambda a, b, c: (sizes[0] - 1 - a, c, b), sizes)
+
+    keys_rest, values_rest = split_heads(
+        after(rows4, near), norm_gain, group, quarter, depth, first, depth - first, 7, 2
+    )
+    keys_got = passed_along(keys_rest, "section", -1)
+    values_got = passed_along(after(values_rest, start_got), "section", -1)
+
+    near_mate = swapped(near_got)
+    far_mate = swapped(far_got)
     same = (q == t).astype(jnp.int32)[None]
 
-    wide = block.astype(jnp.float32)
-    square = jnp.sum(wide * wide, axis=-1, keepdims=True)
+    wide = after(block, near_got).astype(jnp.float32)
+    square = jnp.sum(wide * wide, axis=-1)[None]
     square = square + swapped(square)
-    scale = lax.rsqrt(square / (block.shape[1] * sizes[2]) + EPS)
-
-    code = token_owner[0, :, 0] * 2 + token_slot[0]
-    notes = jnp.concatenate([code, jnp.broadcast_to(span_start, (width,))])[None]
-    notes = passed_along(notes, "section", -1)
-    code = notes[:, :tokens]
-    positions = notes[0, tokens] + q * tokens + jnp.arange(tokens, dtype=jnp.int32)
+
+    notes = start_got[first].astype(jnp.int32)
+    code = notes[None, :tokens]
+    begin = notes[tokens] * 64 + notes[tokens + 1]
+    positions = begin + q * tokens + jnp.arange(tokens, dtype=jnp.int32)
     half = width // 2
     freq = jnp.exp(-(jnp.arange(half, dtype=jnp.float32) * 2.0 / width) * math.log(THETA))
     angle = positions.astype(jnp.float32)[:, None] * freq[None, :]
     cosine = jnp.cos(angle)
     sine = jnp.sin(angle)
 
-    query = queries[0, 0]
+    query = after(queries[0, 0], near_got)
     layers, reqs, steps, heads, flat = query.shape
     rows = reqs * steps * flat // width
     asked = query.reshape(layers, reqs, steps, heads, flat // width, width)
@@ -451,18 +554,28 @@
     asked = lax.all_to_all(
         jnp.roll(asked, -1, axis=0), "section", split_axis=0, concat_axis=0, tiled=True
     )
-
-    keys = summed_over_chips(partial_products(same, acts, (keys_a, keys_b)), sizes)
-    values = [
-        summed_over_chips(partial_products(same, acts, (v,)), sizes) for v in (values_0, values_1)
-    ]
-    routed = attend_routed(asked, keys, values, scale, cosine, sine, code)
+    mixed, top, total = attend_kept(query, kv_cache[0, 0], cache_lens[0, 0], step_kv[0, 0])
+    near_mate = after(near_mate, (cosine, sine, code, square, mixed, top, total))
+
+    keys_w = (start_got, keys_got)
+    values_w = (start_got, values_got)
+    near_pair = ((near_got,), (near_mate,))
+    near_part = partial_products(same, (near_pair,), keys_w, 0, 2 * width, 0)
+    far_mate = after(far_mate, near_part)
+    far_pair = ((far_got,), (far_mate,))
+    far_part = partial_products(same, (far_pair,), keys_w, 0, 2 * width, 2)
+    keys = summed_over_chips(near_part + far_part, sizes)
+    values = summed_over_chips(
+        partial_products(same, (near_pair, far_pair), values_w, 2 * width, 2 * width, 0), sizes
+    )
+    features = block.shape[1] * sizes[2]
+    weights, marks = weigh(asked, keys, square, cosine, sine, code, features)
+    routed = mix(weights, marks, values, layers)
     routed = lax.all_to_all(routed, "section", split_axis=0, concat_axis=0, tiled=True)
     routed = jnp.roll(routed, 1, axis=0)
     routed = routed.reshape(layers, heads, reqs, steps, flat // width, 2 * width)
     routed = routed.transpose(0, 2, 1, 3, 4, 5).astype(jnp.float32)
     level = jnp.sum(routed[..., width : width + 3], axis=-1, keepdims=True)
-    mixed, top, total = attend_kept(query, kv_cache[0, 0], cache_lens[0, 0], step_kv[0, 0])
     peak = jnp.maximum(level, top)
     kept_part = jnp.exp(top - peak)
     routed_part = jnp.exp(level - peak)

time: 115 us -> 94.1 us (0.82)
  local copies, waits for them, and re-layouts: 20.8 us -> 4.12 us
  starting transfers between devices: 36.7 us -> 26 us
  blocking collectives: 0 us -> 9.44 us
  Pallas kernels: 25.2 us -> 21.2 us
  other arithmetic: 7.81 us -> 6.23 us
  matrix products: 1.14 us -> 2.49 us
    dynamic_slice x5 -> x0, local copies, waits for them, and re-layouts: 11.4 us -> none  [the longest x3 6.82 us: piece(): lax.dynamic_slice(weight, (g * depth + start, 0, column * width), (rows,...]
    all_to_all x0 -> x1, blocking collectives: none -> 9.44 us  [meet_local(): lax.all_to_all(jnp.roll(asked, -1, axis=0), 'section', split_axis=0, conc...]
    ppermute x5 -> x3, starting transfers between devices: 12.2 us -> 7.89 us  [passed_along(): lax.ppermute(value, axis, [(i, (i + by) % length) for i in range(length)])]
    pallas_call x7 -> x8, Pallas kernels: 25.2 us -> 21.2 us  [the longest x3 8.7 us: partial_products(): pl.pallas_call(body, out_shape=[jax.ShapeDtypeStruct((tokens, columns), k...]
    all_to_all x1 -> x0, starting transfers between devices: 3.9 us -> none  [meet_local(): lax.all_to_all(jnp.roll(asked, -1, axis=0), 'section', split_axis=0, conc...]
    ppermute x11 -> x8, starting transfers between devices: 15.7 us -> 12.3 us  [steered(): return lax.ppermute(value, ('group', 'seq', 'tp'), pairs)]
    slice x4 -> x2, local copies, waits for them, and re-layouts: 2.33 us -> 0.65 us  [the longest x1 0.65 us: meet_local(): begin = notes[tokens] * 64 + notes[tokens + 1]]
    rsqrt x1 -> x0, local copies, waits for them, and re-layouts: 1.64 us -> none  [meet_local(): scale = lax.rsqrt(square / (block.shape[1] * sizes[2]) + EPS)]
  transfers between devices with their start and end apart: 21 -> 15, of which waited for: 5 -> 3; matrix products, arithmetic and copies ran while one was open for 19% -> 11% of each run, Pallas kernels for 19% -> 16%
where the time goes in v2:
time: 94.1 us; the launch traced here: 93.4 us
  starting transfers between devices  26 us (28%)
  waiting for transfers between devices  21.6 us (23%)
  Pallas kernels  21.2 us (23%)
  blocking collectives  9.44 us (10%)
  other arithmetic  6.23 us (7%)
  local copies, waits for them, and re-layouts  4.12 us (4%)
  matrix products  2.49 us (3%)
  between operations  2.33 us (2%)
    ppermute x8, waiting for transfers between devices, steered(): return lax.ppermute(value, ('group', 'seq', 'tp'), pairs)  14.1 us
    ppermute x8, starting transfers between devices, steered(): return lax.ppermute(value, ('group', 'seq', 'tp'), pairs)  12.3 us
    all_to_all x1, blocking collectives, meet_local(): lax.all_to_all(jnp.roll(asked, -1, axis=0), 'section', split_axis=0, conc...  9.44 us
    pallas_call x3, Pallas kernels, partial_products(): pl.pallas_call(body, out_shape=[jax.ShapeDtypeStruct((tokens, columns), k...  8.7 us
    ppermute x3, starting transfers between devices, passed_along(): lax.ppermute(value, axis, [(i, (i + by) % length) for i in range(length)])  7.89 us
    pallas_call x2, Pallas kernels, split_heads(): pl.pallas_call(body, out_shape=[jax.ShapeDtypeStruct((count + extra, colu...  7.16 us
    all_to_all x1, waiting for transfers between devices, meet_local(): lax.all_to_all(routed, 'section', split_axis=0, concat_axis=0, tiled=True)  5.58 us
    pallas_call x1, Pallas kernels, cut_columns(): pl.pallas_call(body, out_shape=[jax.ShapeDtypeStruct((tokens, count), blo...  3.55 us
  transfers between devices with their start and end apart: 15, of which 3 were waited for; matrix products, arithmetic and copies ran while one was open for 11% of the time, Pallas kernels for 16%

profile of v2, /device:TPU:0, one launch (start us, length us, event | category | flops | bytes accessed | tf_op | source)
XLA Modules:
  0.0 93.4 jit_solution(856519185047537957)
XLA Ops:
  2.1 1.8 %split_heads.2 = bf16[272,512]{1,0:T(8,128)(2,1)} custom-call(s32[1]{0:T(128)} %bitcast.2.group_ref, s32[1]{0:T(128)} %bitcast.4.quarter_ref, bf16[16384,128]{1,0:T(8,128)(2,1)} %bitcast.67, f32[1,8192]{1,0:T(1,128)} %gain_ref.3, f32[1,512]{1,0:T(1,128)} %add_convert_fusion.rest_0_), custom_call_target="tpu_custom_call" | custom-call | tf_op jit(solution)/shard_map/split_heads/pallas_call | solution.py:223
  3.9 3.5 %cut_columns.1 = (bf16[384,2048]{1,0:T(8,128)(2,1)}, bf16[384,2048]{1,0:T(8,128)(2,1)}) custom-call(s32[1]{0:T(128)} %bitcast.2.group_ref, bf16[384,4096]{1,0:T(8,128)(2,1)} %bitcast.69), custom_call_target="tpu_custom_call" | custom-call | tf_op jit(solution)/shard_map/cut_columns/pallas_call | solution.py:257
  7.5 2.1 %collective-permute-start = (bf16[384,2048]{1,0:T(8,128)(2,1)}, bf16[384,2048]{1,0:T(8,128)(2,1)S(1)}, u32[]{:S(2)}, u32[]{:S(2)}) collective-permute-start(bf16[384,2048]{1,0:T(8,128)(2,1)} %get-tuple-element.27), channel_id=1, source_target_pairs={{0,0},{1,2},{2,1},{3,3},{16,16},{17,18},{18,17},{19,19},{4,4},{5,6... | collective-permute-start | bytes 4718600 | tf_op jit(solution)/shard_map/ppermute | solution.py:172
  9.5 3.0 %collective-permute-start.6 = (bf16[384,2048]{1,0:T(8,128)(2,1)}, bf16[384,2048]{1,0:T(8,128)(2,1)S(1)}, u32[]{:S(2)}, u32[]{:S(2)}) collective-permute-start(bf16[384,2048]{1,0:T(8,128)(2,1)} %get-tuple-element.35), channel_id=1, source_target_pairs={{0,16},{1,18},{2,17},{3,19},{16,0},{17,2},{18,1},{19,3},{4,20},{5,... | collective-permute-start | bytes 4718600 | tf_op jit(solution)/shard_map/ppermute | solution.py:172
  12.5 3.6 %collective-permute-start.2 = (bf16[272,512]{1,0:T(8,128)(2,1)}, bf16[272,512]{1,0:T(8,128)(2,1)S(1)}, u32[]{:S(2)}, u32[]{:S(2)}) collective-permute-start(bf16[272,512]{1,0:T(8,128)(2,1)} %split_heads.2), channel_id=1, source_target_pairs={{0,12},{4,0},{8,4},{12,8},{1,13},{5,1},{9,5},{13,9},{2,14},{6,2},{... | collective-permute-start | bytes 835592 | tf_op jit(solution)/shard_map/ppermute | solution.py:17
  16.1 5.4 %split_heads.3 = (bf16[1792,256]{1,0:T(8,128)(2,1)}, bf16[1792,256]{1,0:T(8,128)(2,1)}) custom-call(s32[1]{0:T(128)} %bitcast.2.group_ref, s32[1]{0:T(128)} %bitcast.4.quarter_ref, bf16[16384,128]{1,0:T(8,128)(2,1)} %bitcast.68, f32[1,8192]{1,0:T(1,128)} %gain_ref.3), custom_call_target="tpu_custom_call" | custom-call | tf_op jit(solution)/shard_map/split_heads/pallas_call | solution.py:223
  21.9 1.7 %copy.35 = bf16[1,1,4,2,32,2,256]{6,4,5,3,2,1,0:T(8,128)(2,1)} copy(bf16[1,1,4,2,32,2,256]{6,5,4,3,2,1,0:T(2,128)(2,1)} %param.16) | data formatting | bytes 524288 | tf_op args[6]
  23.8 3.8 %collective-permute-start.10 = (bf16[1792,256]{1,0:T(8,128)(2,1)}, bf16[1792,256]{1,0:T(8,128)(2,1)}, u32[]{:S(2)}, u32[]{:S(2)}) collective-permute-start(bf16[1792,256]{1,0:T(8,128)(2,1)} %get-tuple-element.42), channel_id=1, source_target_pairs={{0,12},{4,0},{8,4},{12,8},{1,13},{5,1},{9,5},{13,9},{2,14},{6,2},{... | collective-permute-start | bytes 2752520 | tf_op jit(solution)/shard_map/ppermute | solution.py:17
  29.6 1.5 %collective-permute-start.1 = (bf16[384,2048]{1,0:T(8,128)(2,1)S(1)}, bf16[384,2048]{1,0:T(8,128)(2,1)}, u32[]{:S(2)}, u32[]{:S(2)}) collective-permute-start(bf16[384,2048]{1,0:T(8,128)(2,1)S(1)} %collective-permute-done.refs_0_), channel_id=1, source_target_pairs={{0,1},{1,0},{2,3},{3,2},{4,5},{5,4},{6,7},{7,6},{8,9},{9,8},{10,11... | collective-permute-start | bytes 4718600 | tf_op jit(solution)/shard_map/ppermute | solution.py:176
  31.1 1.5 %multiply_sine_fusion = (f32[384,64]{1,0:T(8,128)}, f32[384,64]{1,0:T(8,128)}) fusion(f32[64]{0:T(128)S(1)} %multiply_exponential_fusion, f32[384]{0:T(512)S(1)} %add_convert_fusion.1), kind=kLoop, calls=%fused_computation.6 | loop fusion | flops 24576 | bytes 198400 | tf_op jit(solution)/shard_map/sin | solution.py:547
  33.5 14.1 %collective-permute-done.6.refs_0_.refs_2_ = bf16[384,2048]{1,0:T(8,128)(2,1)S(1)} collective-permute-done((bf16[384,2048]{1,0:T(8,128)(2,1)}, bf16[384,2048]{1,0:T(8,128)(2,1)S(1)}, u32[]{:S(2)}, u32[]{:S(2)}) %collective-permute-start.6) | collective-permute-done | bytes 1572896 | tf_op jit(solution)/shard_map/ppermute | solution.py:172
  47.6 0.9 collective-permute-start.7
  48.5 2.6 %multiply_reduce_fusion = f32[384]{0:T(512)S(1)} fusion(bf16[384,4096]{1,0:T(8,128)(2,1)} %bitcast.70), kind=kLoop, calls=%fused_computation | loop fusion | flops 4718208 | bytes 3147264 | tf_op jit(solution)/shard_map/reduce_sum | solution.py:536
  53.8 2.7 %partial_products.3 = (f32[384,256]{1,0:T(8,128)S(1)}, bf16[384,256]{1,0:T(8,128)(2,1)S(1)}) custom-call(s32[1]{0:T(128)} %bitcast.25.same_ref, bf16[384,2048]{1,0:T(8,128)(2,1)S(1)} %collective-permute-done.refs_0_, bf16[384,2048]{1,0:T(8,128)(2,1)} %collective-permute-done.1.refs_1_, bf16[272,512]{1,0:T(8,128)(2,1)S(1)} %collective-permute-done.2.refs_2_.refs_4_, ...), custom_call_target="tpu_custom_call" | custom-call | tf_op jit(solution)/shard_map/partial_products/pallas_call | solution.py:326
  56.5 2.2 %collective-permute-start.5 = (bf16[384,256]{1,0:T(8,128)(2,1)S(1)}, bf16[384,256]{1,0:T(8,128)(2,1)S(1)}, u32[]{:S(2)}, u32[]{:S(2)}) collective-permute-start(bf16[384,256]{1,0:T(8,128)(2,1)S(1)} %get-tuple-element.34), channel_id=1, source_target_pairs={{0,2},{1,3},{2,0},{3,1},{16,18},{17,19},{18,16},{19,17},{4,6},{5,7... | collective-permute-start | bytes 589832 | tf_op jit(solution)/shard_map/ppermute | solution.py:172
  58.8 2.2 %partial_products.4 = (bf16[384,256]{1,0:T(8,128)(2,1)S(1)}, bf16[384,256]{1,0:T(8,128)(2,1)S(1)}) custom-call(s32[1]{0:T(128)} %bitcast.25.same_ref, bf16[384,2048]{1,0:T(8,128)(2,1)S(1)} %collective-permute-done.6.refs_0_.refs_2_, bf16[384,2048]{1,0:T(8,128)(2,1)S(1)} %collective-permute-done.7.refs_1_.refs_3_, ...), custom_call_target="tpu_custom_call" | custom-call | tf_op jit(solution)/shard_map/partial_products/pallas_call | solution.py:326
  61.6 1.0 %collective-permute-start.9 = (bf16[384,256]{1,0:T(8,128)(2,1)S(1)}, bf16[384,256]{1,0:T(8,128)(2,1)S(1)}, u32[]{:S(2)}, u32[]{:S(2)}) collective-permute-start(bf16[384,256]{1,0:T(8,128)(2,1)S(1)} %get-tuple-element.38), channel_id=1, source_target_pairs={{0,18},{1,19},{2,16},{3,17},{16,2},{17,3},{18,0},{19,1},{4,22},{5,... | collective-permute-start | bytes 589832 | tf_op jit(solution)/shard_map/ppermute | solution.py:172
  62.5 1.9 %collective-permute-done.10.refs_5_ = bf16[1792,256]{1,0:T(8,128)(2,1)} collective-permute-done((bf16[1792,256]{1,0:T(8,128)(2,1)}, bf16[1792,256]{1,0:T(8,128)(2,1)}, u32[]{:S(2)}, u32[]{:S(2)}) %collective-permute-start.10) | collective-permute-done | bytes 917536 | tf_op jit(solution)/shard_map/ppermute | solution.py:17
  64.4 3.7 %partial_products.5 = (f32[384,256]{1,0:T(8,128)S(1)}, bf16[384,256]{1,0:T(8,128)(2,1)S(1)}, bf16[384,256]{1,0:T(8,128)(2,1)S(1)}, bf16[384,256]{1,0:T(8,128)(2,1)S(1)}) custom-call(s32[1]{0:T(128)} %bitcast.25.same_ref, bf16[384,2048]{1,0:T(8,128)(2,1)S(1)} %collective-permute-done.refs_0_, bf16[384,2048]{1,0:T(8,128)(2,1)} %collective-permute-done.1.refs_1_, ...), custom_call_target="tpu_custom_call" | custom-call | tf_op jit(solution)/shard_map/partial_products/pallas_call | solution.py:326
  68.9 2.8 %collective-permute-start.13 = (bf16[384,256]{1,0:T(8,128)(2,1)S(1)}, bf16[384,256]{1,0:T(8,128)(2,1)S(1)}, u32[]{:S(2)}, u32[]{:S(2)}) collective-permute-start(bf16[384,256]{1,0:T(8,128)(2,1)S(1)} %get-tuple-element.46), channel_id=1, source_target_pairs={{0,18},{1,19},{2,16},{3,17},{16,2},{17,3},{18,0},{19,1},{4,22},{5,... | collective-permute-start | bytes 589832 | tf_op jit(solution)/shard_map/ppermute | solution.py:172
  71.7 9.4 %all_to_all.10.asked_ref = bf16[4,2,32,128]{3,2,1,0:T(8,128)(2,1)S(1)} all-to-all(bf16[4,2,32,128]{3,2,1,0:T(8,128)(2,1)S(1)} %pad_maximum_fusion.1), channel_id=1, replica_groups=mesh['group'=2,'section'=4,'seq'=2,'tp'=2] {'section'}, dimensions={0} | all-to-all | bytes 131072 | tf_op jit(solution)/shard_map/all_to_all | solution.py:554
  82.1 0.9 mix.1
  83.0 3.3 %all-to-all-start.1 = ((bf16[4,2,32,256]{3,2,1,0:T(8,128)(2,1)}), bf16[4,2,32,256]{3,2,1,0:T(8,128)(2,1)S(1)}, u32[]{:S(2)}, u32[]{:S(2)}) async-start(bf16[4,2,32,256]{3,2,1,0:T(8,128)(2,1)} %mix.1), calls=%async_computation.1 | async-start | bytes 262144 | tf_op jit(solution)/shard_map/all_to_all | solution.py:574
  86.7 5.6 %all-to-all-done.1 = bf16[4,2,32,256]{3,2,1,0:T(8,128)(2,1)S(1)} async-done(((bf16[4,2,32,256]{3,2,1,0:T(8,128)(2,1)}), bf16[4,2,32,256]{3,2,1,0:T(8,128)(2,1)S(1)}, u32[]{:S(2)}, u32[]{:S(2)}) %all-to-all-start.1) | async-done | bytes 131104 | tf_op jit(solution)/shard_map/all_to_all | solution.py:574
  (71 shorter events, 9.8 us)
Async XLA Ops:
  7.5 22.2 %collective-permute-start = (bf16[384,2048]{1,0:T(8,128)(2,1)}, bf16[384,2048]{1,0:T(8,128)(2,1)S(1)}, u32[]{:S(2)}, u32[]{:S(2)}) collective-permute-start(bf16[384,2048]{1,0:T(8,128)(2,1)} %get-tuple-element.27), channel_id=1, source_target_pairs={{0,0},{1,2},{2,1},{3,3},{16,16},{17,18},{18,17},{19,19},{4,4},{5,6... | collective-permute-start | bytes 4718600 | tf_op jit(solution)/shard_map/ppermute | solution.py:172
  9.5 14.1 %copy-start.7 = (bf16[1,1,4,2,2,2,256]{6,5,4,3,2,1,0:T(2,128)(2,1)S(1)}, bf16[1,1,4,2,2,2,256]{6,5,4,3,2,1,0:T(2,128)(2,1)}, u32[]{:S(2)}) copy-start(bf16[1,1,4,2,2,2,256]{6,5,4,3,2,1,0:T(2,128)(2,1)} %param.18) | copy-start | bytes 49156
  9.5 14.2 %copy-start.8 = (s32[1,1,2]{2,1,0:T(1,128)S(1)}, s32[1,1,2]{2,1,0:T(1,128)}, u32[]{:S(2)}) copy-start(s32[1,1,2]{2,1,0:T(1,128)} %param.17) | copy-start | bytes 28
  9.5 38.1 %collective-permute-start.6 = (bf16[384,2048]{1,0:T(8,128)(2,1)}, bf16[384,2048]{1,0:T(8,128)(2,1)S(1)}, u32[]{:S(2)}, u32[]{:S(2)}) collective-permute-start(bf16[384,2048]{1,0:T(8,128)(2,1)} %get-tuple-element.35), channel_id=1, source_target_pairs={{0,16},{1,18},{2,17},{3,19},{16,0},{17,2},{18,1},{19,3},{4,20},{5,... | collective-permute-start | bytes 4718600 | tf_op jit(solution)/shard_map/ppermute | solution.py:172
  12.5 11.3 %collective-permute-start.2 = (bf16[272,512]{1,0:T(8,128)(2,1)}, bf16[272,512]{1,0:T(8,128)(2,1)S(1)}, u32[]{:S(2)}, u32[]{:S(2)}) collective-permute-start(bf16[272,512]{1,0:T(8,128)(2,1)} %split_heads.2), channel_id=1, source_target_pairs={{0,12},{4,0},{8,4},{12,8},{1,13},{5,1},{9,5},{13,9},{2,14},{6,2},{... | collective-permute-start | bytes 835592 | tf_op jit(solution)/shard_map/ppermute | solution.py:17
  21.5 32.3 %collective-permute-start.4 = (bf16[1792,256]{1,0:T(8,128)(2,1)}, bf16[1792,256]{1,0:T(8,128)(2,1)}, u32[]{:S(2)}, u32[]{:S(2)}) collective-permute-start(bf16[1792,256]{1,0:T(8,128)(2,1)} %get-tuple-element.32), channel_id=1, source_target_pairs={{0,12},{4,0},{8,4},{12,8},{1,13},{5,1},{9,5},{13,9},{2,14},{6,2},{... | collective-permute-start | bytes 2752520 | tf_op jit(solution)/shard_map/ppermute | solution.py:17
  23.7 27.8 %copy-start.6 = (bf16[1,1,4,2,2,2,256]{6,4,5,3,2,1,0:T(2,128)(2,1)}, bf16[1,1,4,2,2,2,256]{6,4,5,3,2,1,0:T(2,128)(2,1)S(1)}, u32[]{:S(2)}) copy-start(bf16[1,1,4,2,2,2,256]{6,4,5,3,2,1,0:T(2,128)(2,1)S(1)} %copy.37) | copy-start | bytes 49156
  23.8 40.6 %collective-permute-start.10 = (bf16[1792,256]{1,0:T(8,128)(2,1)}, bf16[1792,256]{1,0:T(8,128)(2,1)}, u32[]{:S(2)}, u32[]{:S(2)}) collective-permute-start(bf16[1792,256]{1,0:T(8,128)(2,1)} %get-tuple-element.42), channel_id=1, source_target_pairs={{0,12},{4,0},{8,4},{12,8},{1,13},{5,1},{9,5},{13,9},{2,14},{6,2},{... | collective-permute-start | bytes 2752520 | tf_op jit(solution)/shard_map/ppermute | solution.py:17
  29.6 24.1 %collective-permute-start.1 = (bf16[384,2048]{1,0:T(8,128)(2,1)S(1)}, bf16[384,2048]{1,0:T(8,128)(2,1)}, u32[]{:S(2)}, u32[]{:S(2)}) collective-permute-start(bf16[384,2048]{1,0:T(8,128)(2,1)S(1)} %collective-permute-done.refs_0_), channel_id=1, source_target_pairs={{0,1},{1,0},{2,3},{3,2},{4,5},{5,4},{6,7},{7,6},{8,9},{9,8},{10,11... | collective-permute-start | bytes 4718600 | tf_op jit(solution)/shard_map/ppermute | solution.py:176
  33.5 17.7 %copy-start.2 = (bf16[1,1,4,2,32,2,256]{6,4,5,3,2,1,0:T(8,128)(2,1)S(1)}, bf16[1,1,4,2,32,2,256]{6,4,5,3,2,1,0:T(8,128)(2,1)}, u32[]{:S(2)}) copy-start(bf16[1,1,4,2,32,2,256]{6,4,5,3,2,1,0:T(8,128)(2,1)} %copy.35) | copy-start | bytes 786436
  47.6 11.1 %collective-permute-start.7 = (bf16[384,2048]{1,0:T(8,128)(2,1)S(1)}, bf16[384,2048]{1,0:T(8,128)(2,1)S(1)}, u32[]{:S(2)}, u32[]{:S(2)}) collective-permute-start(bf16[384,2048]{1,0:T(8,128)(2,1)S(1)} %collective-permute-done.6.refs_0_.refs_2_), channel_id=1, source_target_pairs={{0,1},{1,0},{2,3},{3,2},{4,5},{5,4},{6,7},{7,6},{8,9},{9,8},{10,11... | collective-permute-start | bytes 4718600 | tf_op jit(solution)/shard_map/ppermute | solution.py:176
  51.1 2.6 %collective-permute-start.3 = (f32[1,384]{1,0:T(1,128)S(1)}, f32[1,384]{1,0:T(1,128)S(1)}, u32[]{:S(2)}, u32[]{:S(2)}) collective-permute-start(f32[1,384]{1,0:T(1,128)S(1)} %broadcast_in_dim.64), channel_id=1, source_target_pairs={{0,1},{1,0},{2,3},{3,2},{4,5},{5,4},{6,7},{7,6},{8,9},{9,8},{10,11... | collective-permute-start | bytes 4616 | tf_op jit(solution)/shard_map/ppermute | solution.py:176
  51.5 2.3 %copy-start.3 = (f32[4,2,2,2,8,32]{5,4,3,2,1,0:T(8,128)}, f32[4,2,2,2,8,32]{5,4,3,2,1,0:T(8,128)S(1)}, u32[]{:S(2)}) copy-start(f32[4,2,2,2,8,32]{5,4,3,2,1,0:T(8,128)S(1)} %get-tuple-element.55) | copy-start | bytes 98308
  56.5 12.4 %collective-permute-start.5 = (bf16[384,256]{1,0:T(8,128)(2,1)S(1)}, bf16[384,256]{1,0:T(8,128)(2,1)S(1)}, u32[]{:S(2)}, u32[]{:S(2)}) collective-permute-start(bf16[384,256]{1,0:T(8,128)(2,1)S(1)} %get-tuple-element.34), channel_id=1, source_target_pairs={{0,2},{1,3},{2,0},{3,1},{16,18},{17,19},{18,16},{19,17},{4,6},{5,7... | collective-permute-start | bytes 589832 | tf_op jit(solution)/shard_map/ppermute | solution.py:172
  61.0 20.2 %collective-permute-start.8 = (bf16[384,256]{1,0:T(8,128)(2,1)S(1)}, bf16[384,256]{1,0:T(8,128)(2,1)S(1)}, u32[]{:S(2)}, u32[]{:S(2)}) collective-permute-start(bf16[384,256]{1,0:T(8,128)(2,1)S(1)} %get-tuple-element.37), channel_id=1, source_target_pairs={{0,16},{1,17},{2,18},{3,19},{16,0},{17,1},{18,2},{19,3},{4,20},{5,... | collective-permute-start | bytes 589832 | tf_op jit(solution)/shard_map/ppermute | solution.py:172
  61.6 19.6 %copy-start = (f32[384,64]{1,0:T(8,128)S(1)}, f32[384,64]{1,0:T(8,128)}, u32[]{:S(2)}) copy-start(f32[384,64]{1,0:T(8,128)} %get-tuple-element.50.rest_6_) | copy-start | bytes 294916
  61.6 19.7 %copy-start.1 = (f32[384,64]{1,0:T(8,128)S(1)}, f32[384,64]{1,0:T(8,128)}, u32[]{:S(2)}) copy-start(f32[384,64]{1,0:T(8,128)} %get-tuple-element.51.rest_5_) | copy-start | bytes 294916
  61.6 19.6 %collective-permute-start.9 = (bf16[384,256]{1,0:T(8,128)(2,1)S(1)}, bf16[384,256]{1,0:T(8,128)(2,1)S(1)}, u32[]{:S(2)}, u32[]{:S(2)}) collective-permute-start(bf16[384,256]{1,0:T(8,128)(2,1)S(1)} %get-tuple-element.38), channel_id=1, source_target_pairs={{0,18},{1,19},{2,16},{3,17},{16,2},{17,3},{18,0},{19,1},{4,22},{5,... | collective-permute-start | bytes 589832 | tf_op jit(solution)/shard_map/ppermute | solution.py:172
  68.2 13.9 %collective-permute-start.11 = (bf16[384,256]{1,0:T(8,128)(2,1)S(1)}, bf16[384,256]{1,0:T(8,128)(2,1)S(1)}, u32[]{:S(2)}, u32[]{:S(2)}) collective-permute-start(bf16[384,256]{1,0:T(8,128)(2,1)S(1)} %get-tuple-element.44), channel_id=1, source_target_pairs={{0,2},{1,3},{2,0},{3,1},{16,18},{17,19},{18,16},{19,17},{4,6},{5,7... | collective-permute-start | bytes 589832 | tf_op jit(solution)/shard_map/ppermute | solution.py:172
  68.4 13.8 %collective-permute-start.12 = (bf16[384,256]{1,0:T(8,128)(2,1)S(1)}, bf16[384,256]{1,0:T(8,128)(2,1)S(1)}, u32[]{:S(2)}, u32[]{:S(2)}) collective-permute-start(bf16[384,256]{1,0:T(8,128)(2,1)S(1)} %get-tuple-element.45), channel_id=1, source_target_pairs={{0,16},{1,17},{2,18},{3,19},{16,0},{17,1},{18,2},{19,3},{4,20},{5,... | collective-permute-start | bytes 589832 | tf_op jit(solution)/shard_map/ppermute | solution.py:172
  68.9 13.2 %collective-permute-start.13 = (bf16[384,256]{1,0:T(8,128)(2,1)S(1)}, bf16[384,256]{1,0:T(8,128)(2,1)S(1)}, u32[]{:S(2)}, u32[]{:S(2)}) collective-permute-start(bf16[384,256]{1,0:T(8,128)(2,1)S(1)} %get-tuple-element.46), channel_id=1, source_target_pairs={{0,18},{1,19},{2,16},{3,17},{16,2},{17,3},{18,0},{19,1},{4,22},{5,... | collective-permute-start | bytes 589832 | tf_op jit(solution)/shard_map/ppermute | solution.py:172
  81.2 5.3 %copy-start.4 = (f32[4,2,2,2,8,32]{5,4,3,2,1,0:T(8,128)S(1)}, f32[4,2,2,2,8,32]{5,4,3,2,1,0:T(8,128)}, u32[]{:S(2)}) copy-start(f32[4,2,2,2,8,32]{5,4,3,2,1,0:T(8,128)} %copy-done.3) | copy-start | bytes 98308
  82.1 10.4 %copy-start.5 = (f32[4,2,2,2,8,128]{5,4,3,2,1,0:T(8,128)S(1)}, f32[4,2,2,2,8,128]{5,4,3,2,1,0:T(8,128)}, u32[]{:S(2)}) copy-start(f32[4,2,2,2,8,128]{5,4,3,2,1,0:T(8,128)} %convolution_add_fusion) | copy-start | bytes 393220
  83.0 9.2 %all-to-all-start.1 = ((bf16[4,2,32,256]{3,2,1,0:T(8,128)(2,1)}), bf16[4,2,32,256]{3,2,1,0:T(8,128)(2,1)S(1)}, u32[]{:S(2)}, u32[]{:S(2)}) async-start(bf16[4,2,32,256]{3,2,1,0:T(8,128)(2,1)} %mix.1), calls=%async_computation.1 | async-start | bytes 262144 | tf_op jit(solution)/shard_map/all_to_all | solution.py:574

commit v3 on v2

--- a/solution.py
+++ b/solution.py
@@ -176,93 +176,139 @@
     return lax.ppermute(value, "tp", [(0, 1), (1, 0)])
 
 
+def spread(pieces):
+    return [pieces[0]] + [
+        lax.ppermute(piece, "section", [(i, i ^ n) for i in range(len(pieces))])
+        for n, piece in enumerate(pieces)
+        if n
+    ]
+
+
 def after(value, early):
     return lax.optimization_barrier((value, early))[0]
 
 
-def split_heads(rows4, gain, group, quarter, depth, start, count, blocks, parts, notes=None):
+def scaled_heads(wide, gain, tall, width):
+    gains = jnp.concatenate(
+        [
+            jnp.broadcast_to(gain[:, b * width : (b + 1) * width], (width, width)).T
+            for b in range(tall // width)
+        ],
+        axis=0,
+    )
+    return [
+        (wide[pl.ds(n, tall, stride=4), :] * gains).astype(jnp.bfloat16) for n in range(4)
+    ]
+
+
+def split_heads(rows4, gain, group, quarter, depth, start, count, blocks):
     width = rows4.shape[1]
     tall = count // blocks
-    columns = 4 * width // parts
-    extra = 0 if notes is None else 16
-
-    def body(group_ref, quarter_ref, mixed_ref, gain_ref, *rest):
-        outs, wide = rest[len(rest) - 1 - parts : -1], rest[-1]
+
+    def body(group_ref, quarter_ref, mixed_ref, gain_ref, key_ref, value_ref, wide):
         wide[...] = mixed_ref[...].astype(jnp.float32)
-        gains = jnp.concatenate(
-            [
-                jnp.broadcast_to(gain_ref[:, b * width : (b + 1) * width], (width, width)).T
-                for b in range(tall // width)
-            ],
-            axis=0,
-        )
-        for kind in range(2):
-            for head in range(2):
-                scaled = wide[pl.ds(2 * kind + head, tall, stride=4), :] * gains
-                column = (2 * kind + head) * width
-                out = outs[column * parts // (4 * width)]
-                column = column % (4 * width // parts)
-                out[:tall, column : column + width] = scaled.astype(jnp.bfloat16)
-        if extra:
-            outs[0][tall:, :] = jnp.broadcast_to(rest[0][...], (extra, columns)).astype(jnp.bfloat16)
-
-    operands = [group, quarter, rows4, gain]
-    in_specs = [
-        pl.BlockSpec(
-            (4 * tall, width),
-            lambda i, group, quarter: (group[0] * (depth // tall) + start // tall + i, 0),
-        ),
-        pl.BlockSpec(
-            (1, tall),
-            lambda i, group, quarter: (0, quarter[0] * (depth // tall) + start // tall + i),
-        ),
-    ]
-    if extra:
-        operands.append(notes)
-        in_specs.append(pl.BlockSpec((1, columns), lambda i, group, quarter: (0, 0)))
+        parts = scaled_heads(wide, gain_ref[...], tall, width)
+        for head in range(2):
+            key_ref[:, head * width : (head + 1) * width] = parts[head]
+            value_ref[:, head * width : (head + 1) * width] = parts[2 + head]
+
     return pl.pallas_call(
         body,
-        out_shape=[jax.ShapeDtypeStruct((count + extra, columns), jnp.bfloat16)] * parts,
+        out_shape=[jax.ShapeDtypeStruct((count, 2 * width), jnp.bfloat16)] * 2,
         grid_spec=pltpu.PrefetchScalarGridSpec(
             num_scalar_prefetch=2,
             grid=(blocks,),
-            in_specs=in_specs,
-            out_specs=[pl.BlockSpec((tall + extra, columns), lambda i, group, quarter: (i, 0))]
-            * parts,
+            in_specs=[
+                pl.BlockSpec(
+                    (4 * tall, width),
+                    lambda i, group, quarter: (group[0] * (depth // tall) + start // tall + i, 0),
+                ),
+                pl.BlockSpec(
+                    (1, tall),
+                    lambda i, group, quarter: (0, quarter[0] * (depth // tall) + start // tall + i),
+                ),
+            ],
+            out_specs=[pl.BlockSpec((tall, 2 * width), lambda i, group, quarter: (i, 0))] * 2,
             scratch_shapes=[pltpu.VMEM((4 * tall, width), jnp.float32)],
         ),
-        compiler_params=pltpu.CompilerParams(vmem_limit_bytes=60 << 20),
+        compiler_params=pltpu.CompilerParams(vmem_limit_bytes=57 << 20),
         name="split_heads",
-    )(*operands)
-
-
-def cut_columns(block, group, depth, cuts):
+    )(group, quarter, rows4, gain)
+
+
+def prepare(block, rows4, gain, group, quarter, owner, slot, begin, depth, first):
     tokens = block.shape[0]
-
-    def body(group_ref, block_ref, *rest):
-        outs, sems = rest[:-1], rest[-1]
-        copies = []
-        for n, (other, start, count) in enumerate(cuts):
-            which = (1 - group_ref[0]) if other else group_ref[0]
-            column = pl.multiple_of(which * depth + start, 128)
-            copies.append(
-                pltpu.make_async_copy(block_ref.at[:, pl.ds(column, count)], outs[n], sems.at[n])
+    width = rows4.shape[1]
+    extra = 16
+
+    def body(
+        group_ref,
+        quarter_ref,
+        begin_ref,
+        owner_ref,
+        slot_ref,
+        block_ref,
+        rows_ref,
+        gain_ref,
+        head_ref,
+        near_ref,
+        far_ref,
+        mixed,
+        wide,
+        gains,
+        sems,
+    ):
+        row = pl.multiple_of(group_ref[0] * (4 * depth), 4 * depth)
+        lane = pl.multiple_of(quarter_ref[0] * depth, depth)
+        loads = [
+            pltpu.make_async_copy(rows_ref.at[pl.ds(row, 4 * first), :], mixed, sems.at[0]),
+            pltpu.make_async_copy(gain_ref.at[:, pl.ds(lane, first)], gains, sems.at[1]),
+        ]
+        for n, ref in enumerate((near_ref, far_ref)):
+            which = group_ref[0] if n == 0 else 1 - group_ref[0]
+            column = pl.multiple_of(which * depth, depth)
+            loads.append(
+                pltpu.make_async_copy(
+                    block_ref.at[:, pl.ds(column, depth)], ref, sems.at[2 + n]
+                )
             )
-        for copy in copies:
+        for copy in loads:
             copy.start()
-        for copy in copies:
-            copy.wait()
-
-    anywhere = pl.BlockSpec(memory_space=pl.ANY)
+        loads[0].wait()
+        loads[1].wait()
+        wide[...] = mixed[...].astype(jnp.float32)
+        for n, part in enumerate(scaled_heads(wide, gains[...], first, width)):
+            head_ref[:first, n * width : (n + 1) * width] = part
+        code = (owner_ref[...] * 2 + slot_ref[...]).astype(jnp.float32)
+        start = begin_ref[0]
+        high = start // 64
+        mark = lax.broadcasted_iota(jnp.int32, (1, 4 * width - tokens), 1)
+        mark = jnp.where(mark == 0, high, jnp.where(mark == 1, start - high * 64, 0))
+        head_ref[first:, :tokens] = jnp.broadcast_to(code, (extra, tokens)).astype(jnp.bfloat16)
+        head_ref[first:, tokens:] = jnp.broadcast_to(
+            mark.astype(jnp.float32), (extra, 4 * width - tokens)
+        ).astype(jnp.bfloat16)
+        loads[2].wait()
+        loads[3].wait()
+
+    smem = pl.BlockSpec(memory_space=pltpu.SMEM)
+    vmem = pl.BlockSpec(memory_space=pltpu.VMEM)
+    hbm = pl.BlockSpec(memory_space=pl.ANY)
     return pl.pallas_call(
         body,
-        out_shape=[jax.ShapeDtypeStruct((tokens, count), block.dtype) for _, _, count in cuts],
-        in_specs=[pl.BlockSpec(memory_space=pltpu.SMEM), anywhere],
-        out_specs=[pl.BlockSpec(memory_space=pltpu.VMEM)] * len(cuts),
-        scratch_shapes=[pltpu.SemaphoreType.DMA((len(cuts),))],
+        out_shape=[jax.ShapeDtypeStruct((first + extra, 4 * width), jnp.bfloat16)]
+        + [jax.ShapeDtypeStruct((tokens, depth), jnp.bfloat16)] * 2,
+        in_specs=[smem, smem, smem, vmem, vmem, hbm, hbm, hbm],
+        out_specs=[vmem, vmem, vmem],
+        scratch_shapes=[
+            pltpu.VMEM((4 * first, width), jnp.bfloat16),
+            pltpu.VMEM((4 * first, width), jnp.float32),
+            pltpu.VMEM((1, first), jnp.float32),
+            pltpu.SemaphoreType.DMA((4,)),
+        ],
         compiler_params=pltpu.CompilerParams(vmem_limit_bytes=60 << 20),
-        name="cut_columns",
-    )(group, block)
+        name="prepare",
+    )(group, quarter, begin, owner, slot, block, rows4, gain)
 
 
 def partial_products(same, pairs, weights, first_column, columns, first_kind):
@@ -349,19 +395,23 @@
     )
 
 
-def weigh(asked, keys, square, cosine, sine, code, features):
-    owners, heads, rows, width = asked.shape
+def weigh(section, asked, keys, squares, cosine, sine, code, features):
+    owners = len(asked)
+    heads, rows, width = asked[0].shape
     tokens = code.shape[1]
     half = width // 2
     requests = 2
     factor = 1.0 / math.sqrt(width)
     span = owners * rows
 
-    def body(asked_ref, *rest):
+    def body(section_ref, *refs):
+        asked_refs, rest = refs[:owners], refs[owners:]
         key_refs = rest[:4]
-        square_ref, cos_ref, sin_ref, code_ref, weight_ref, mark_ref = rest[4:]
-        scale = lax.rsqrt(square_ref[...] / features + EPS)
-        request = lax.broadcasted_iota(jnp.int32, (span, tokens), 0) // (rows // requests)
+        one_ref, two_ref, cos_ref, sin_ref, code_ref, weight_ref, mark_ref = rest[4:]
+        scale = lax.rsqrt((one_ref[...] + two_ref[...]) / features + EPS)
+        place = lax.broadcasted_iota(jnp.int32, (span, tokens), 0)
+        owner = (place // rows) ^ section_ref[0]
+        request = owner * requests + place % rows // (rows // requests)
         mine = request == code_ref[...]
         lane = lax.broadcasted_iota(jnp.int32, (span, width), 1)
         for h in range(heads):
@@ -378,7 +428,7 @@
                 ],
                 axis=1,
             ).astype(jnp.bfloat16)
-            query = jnp.concatenate([asked_ref[o, h] for o in range(owners)], axis=0)
+            query = jnp.concatenate([ref[h] for ref in asked_refs], axis=0)
             score = lax.dot_general(
                 query, key, (((1,), (1,)), ((), ())), preferred_element_type=jnp.float32
             ) * (scale * factor)
@@ -398,18 +448,18 @@
             ).astype(jnp.bfloat16)
 
     vmem = pl.BlockSpec(memory_space=pltpu.VMEM)
-    operands = (asked, *keys, square, cosine, sine, code)
+    operands = (*asked, *keys, *squares, cosine, sine, code)
     return pl.pallas_call(
         body,
         out_shape=[
             jax.ShapeDtypeStruct((heads, span, tokens), jnp.bfloat16),
             jax.ShapeDtypeStruct((heads, span, width), jnp.bfloat16),
         ],
-        in_specs=[vmem] * len(operands),
+        in_specs=[pl.BlockSpec(memory_space=pltpu.SMEM)] + [vmem] * len(operands),
         out_specs=[vmem] * 2,
         compiler_params=pltpu.CompilerParams(vmem_limit_bytes=6 << 20),
         name="weigh",
-    )(*operands)
+    )(section, *operands)
 
 
 def mix(weights, marks, values, owners):
@@ -418,7 +468,7 @@
     rows = span // owners
 
     def body(weight_ref, mark_ref, *rest):
-        value_refs, out_ref = rest[:-1], rest[-1]
+        value_refs, outs = rest[: len(values)], rest[len(values) :]
         for h in range(heads):
             columns = slice(h * width, (h + 1) * width)
             value = value_refs[0][:, columns]
@@ -427,57 +477,122 @@
             mixed = jnp.dot(
                 weight_ref[h], value.astype(jnp.bfloat16), preferred_element_type=jnp.float32
             ).astype(jnp.bfloat16)
-            for o in range(owners):
-                out_ref[o, h, :, :width] = mixed[o * rows : (o + 1) * rows]
-                out_ref[o, h, :, width:] = mark_ref[h, o * rows : (o + 1) * rows, :]
+            for step in range(owners):
+                outs[step][h, :, :width] = mixed[step * rows : (step + 1) * rows]
+                outs[step][h, :, width:] = mark_ref[h, step * rows : (step + 1) * rows, :]
 
     vmem = pl.BlockSpec(memory_space=pltpu.VMEM)
     operands = (weights, marks, *values)
     return pl.pallas_call(
         body,
-        out_shape=jax.ShapeDtypeStruct((owners, heads, rows, 2 * width), jnp.bfloat16),
+        out_shape=[jax.ShapeDtypeStruct((heads, rows, 2 * width), jnp.bfloat16)] * owners,
         in_specs=[vmem] * len(operands),
-        out_specs=vmem,
+        out_specs=[vmem] * owners,
         compiler_params=pltpu.CompilerParams(vmem_limit_bytes=4 << 20),
         name="mix",
     )(*operands)
 
 
-def attend_kept(query, past, lens, step_pairs):
-    layers, reqs, steps, heads, flat = query.shape
-    width = past.shape[-1] // 2
-    scale = 1.0 / math.sqrt(width)
-    shaped = query.reshape(layers, reqs, steps, heads, flat // width, width)
-    score_past = scale * jnp.einsum(
-        "lrnhgd,lrphd->lrhngp", shaped, past[..., :width], preferred_element_type=jnp.float32
-    )
-    score_step = scale * jnp.einsum(
-        "lrnhgd,lrmhd->lrhngm", shaped, step_pairs[..., :width], preferred_element_type=jnp.float32
-    )
-    filled = jnp.arange(past.shape[2], dtype=jnp.int32)[None, :] < lens[:, None]
-    turn = jnp.arange(steps, dtype=jnp.int32)
-    score_past = jnp.where(filled[None, :, None, None, None, :], score_past, NEG)
-    score_step = jnp.where(
-        (turn[:, None] >= turn[None, :])[None, None, None, :, None, :], score_step, NEG
-    )
-    top = jnp.maximum(
-        jnp.max(score_past, axis=-1, keepdims=True), jnp.max(score_step, axis=-1, keepdims=True)
-    )
-    exp_past = jnp.exp(score_past - top)
-    exp_step = jnp.exp(score_step - top)
-    total = jnp.sum(exp_past, axis=-1, keepdims=True) + jnp.sum(exp_step, axis=-1, keepdims=True)
-    mixed = jnp.einsum(
-        "lrhngp,lrphd->lrhngd",
-        exp_past.astype(jnp.bfloat16),
-        past[..., width:],
-        preferred_element_type=jnp.float32,
-    ) + jnp.einsum(
-        "lrhngm,lrmhd->lrhngd",
-        exp_step.astype(jnp.bfloat16),
-        step_pairs[..., width:],
-        preferred_element_type=jnp.float32,
-    )
-    return mixed, top, total
+def merge(section, pieces, mixed, levels):
+    layers, spans, width = mixed.shape
+    heads, rows, _ = pieces[0].shape
+
+    def body(section_ref, *rest):
+        piece_refs = rest[: len(pieces)]
+        mixed_ref, level_ref, out_ref = rest[len(pieces) :]
+        for step, ref in enumerate(piece_refs):
+            layer = ((section_ref[0] ^ step) + 1) % layers
+            routed = jnp.concatenate([ref[h] for h in range(heads)], axis=0)
+            level = jnp.sum(
+                routed[:, width : width + 3].astype(jnp.float32), axis=1, keepdims=True
+            )
+            high = level_ref[layer]
+            peak = jnp.maximum(level, high)
+            kept = jnp.exp(high - peak)
+            other = jnp.exp(level - peak)
+            share = 1.0 / (kept + other)
+            out_ref[layer] = (
+                mixed_ref[layer] * (kept * share)
+                + routed[:, :width].astype(jnp.float32) * (other * share)
+            ).astype(jnp.bfloat16)
+
+    vmem = pl.BlockSpec(memory_space=pltpu.VMEM)
+    operands = (*pieces, mixed, levels)
+    return pl.pallas_call(
+        body,
+        out_shape=jax.ShapeDtypeStruct((layers, spans, width), jnp.bfloat16),
+        in_specs=[pl.BlockSpec(memory_space=pltpu.SMEM)] + [vmem] * len(operands),
+        out_specs=vmem,
+        compiler_params=pltpu.CompilerParams(vmem_limit_bytes=6 << 20),
+        name="merge",
+    )(section, *operands)
+
+
+def keep(asked, cache, recent, lens, steps):
+    layers, heads, rows, width = asked.shape
+    reqs = lens.shape[0]
+    filled = cache.shape[2] // reqs
+    factor = 1.0 / math.sqrt(width)
+    lane = (((1,), (1,)), ((), ()))
+
+    def body(lens_ref, asked_ref, cache_ref, recent_ref, kept_ref, level_ref):
+        row = lax.broadcasted_iota(jnp.int32, (rows, reqs * filled), 0)
+        column = lax.broadcasted_iota(jnp.int32, (rows, reqs * filled), 1)
+        own = row // (rows // reqs)
+        length = lens_ref[reqs - 1]
+        for r in reversed(range(reqs - 1)):
+            length = jnp.where(own == r, lens_ref[r], length)
+        old = (column // filled == own) & (column % filled < length)
+        row = lax.broadcasted_iota(jnp.int32, (rows, reqs * steps), 0)
+        column = lax.broadcasted_iota(jnp.int32, (rows, reqs * steps), 1)
+        turn = row % (rows // reqs) // (rows // reqs // steps)
+        new = (column // steps == row // (rows // reqs)) & (column % steps <= turn)
+        for l in range(layers):
+            for h in range(heads):
+                query = asked_ref[l, h]
+                past = cache_ref[l, h]
+                step = recent_ref[l, h]
+                score_old = factor * lax.dot_general(
+                    query, past[:, :width], lane, preferred_element_type=jnp.float32
+                )
+                score_new = factor * lax.dot_general(
+                    query, step[:, :width], lane, preferred_element_type=jnp.float32
+                )
+                score_old = jnp.where(old, score_old, NEG)
+                score_new = jnp.where(new, score_new, NEG)
+                top = jnp.maximum(
+                    jnp.max(score_old, axis=1, keepdims=True),
+                    jnp.max(score_new, axis=1, keepdims=True),
+                )
+                weight_old = jnp.exp(score_old - top)
+                weight_new = jnp.exp(score_new - top)
+                total = jnp.sum(weight_old, axis=1, keepdims=True) + jnp.sum(
+                    weight_new, axis=1, keepdims=True
+                )
+                mixed = jnp.dot(
+                    weight_old.astype(jnp.bfloat16),
+                    past[:, width:],
+                    preferred_element_type=jnp.float32,
+                ) + jnp.dot(
+                    weight_new.astype(jnp.bfloat16),
+                    step[:, width:],
+                    preferred_element_type=jnp.float32,
+                )
+                kept_ref[l, h * rows : (h + 1) * rows, :] = mixed / total
+                level_ref[l, h * rows : (h + 1) * rows, :] = jnp.broadcast_to(
+                    top + jnp.log(total), (rows, width)
+                )
+
+    vmem = pl.BlockSpec(memory_space=pltpu.VMEM)
+    return pl.pallas_call(
+        body,
+        out_shape=[jax.ShapeDtypeStruct((layers, heads * rows, width), jnp.float32)] * 2,
+        in_specs=[pl.BlockSpec(memory_space=pltpu.SMEM), vmem, vmem, vmem],
+        out_specs=[vmem, vmem],
+        compiler_params=pltpu.CompilerParams(vmem_limit_bytes=6 << 20),
+        cost_estimate=pl.CostEstimate(flops=40000000000, transcendentals=0, bytes_accessed=1),
+        name="keep",
+    )(lens, asked, cache, recent)
 
 
 def meet_local(
@@ -504,26 +619,28 @@
     block = handoff[0]
     tokens = block.shape[0]
 
-    code = token_owner[0, :, 0] * 2 + token_slot[0]
-    where = jnp.stack([span_start[0] // 64, span_start[0] % 64])
-    notes = jnp.concatenate([code, where, jnp.zeros((4 * width - tokens - 2,), jnp.int32)])
-    notes = notes.astype(jnp.float32)[None]
-
     rows4 = weight.reshape(weight.shape[0], 2, 2, width).transpose(0, 2, 1, 3).reshape(-1, width)
     group = g.astype(jnp.int32)[None]
     quarter = (q * sizes[0] + g).astype(jnp.int32)[None]
-    (head_start,) = split_heads(
-        rows4, norm_gain, group, quarter, depth, 0, first, 1, 1, notes
+    head_start, near, far = prepare(
+        block,
+        rows4,
+        norm_gain,
+        group,
+        quarter,
+        token_owner.reshape(1, tokens),
+        token_slot,
+        span_start,
+        depth,
+        first,
     )
     start_got = passed_along(head_start, "section", -1)
 
-    cuts = ((False, 0, depth), (True, 0, depth))
-    near, far = cut_columns(after(block, head_start), group, depth, cuts)
     near_got = steered(near, lambda a, b, c: (a, c, b), sizes)
     far_got = steered(far, lambda a, b, c: (sizes[0] - 1 - a, c, b), sizes)
 
     keys_rest, values_rest = split_heads(
-        after(rows4, near), norm_gain, group, quarter, depth, first, depth - first, 7, 2
+        after(rows4, near), norm_gain, group, quarter, depth, first, depth - first, 7
     )
     keys_got = passed_along(keys_rest, "section", -1)
     values_got = passed_along(after(values_rest, start_got), "section", -1)
@@ -534,7 +651,7 @@
 
     wide = after(block, near_got).astype(jnp.float32)
     square = jnp.sum(wide * wide, axis=-1)[None]
-    square = square + swapped(square)
+    squares = (square, swapped(square))
 
     notes = start_got[first].astype(jnp.int32)
     code = notes[None, :tokens]
@@ -551,12 +668,17 @@
     rows = reqs * steps * flat // width
     asked = query.reshape(layers, reqs, steps, heads, flat // width, width)
     asked = asked.transpose(0, 3, 1, 2, 4, 5).reshape(layers, heads, rows, width)
-    asked = lax.all_to_all(
-        jnp.roll(asked, -1, axis=0), "section", split_axis=0, concat_axis=0, tiled=True
-    )
-    mixed, top, total = attend_kept(query, kv_cache[0, 0], cache_lens[0, 0], step_kv[0, 0])
-    near_mate = after(near_mate, (cosine, sine, code, square, mixed, top, total))
-
+    section = lax.axis_index("section")
+    everything = asked
+    chosen = [
+        lax.dynamic_index_in_dim(everything, ((section ^ n) + 1) % layers, 0, keepdims=False)
+        for n in range(layers)
+    ]
+    cache = kv_cache[0, 0].transpose(0, 3, 1, 2, 4).reshape(layers, heads, -1, 2 * width)
+    recent = step_kv[0, 0].transpose(0, 3, 1, 2, 4).reshape(layers, heads, -1, 2 * width)
+    kept, levels = keep(everything, cache, recent, cache_lens[0, 0], steps)
+
+    near_mate = after(near_mate, (cosine, sine, code, square, kept, levels, *chosen))
     keys_w = (start_got, keys_got)
     values_w = (start_got, values_got)
     near_pair = ((near_got,), (near_mate,))
@@ -565,30 +687,25 @@
     far_pair = ((far_got,), (far_mate,))
     far_part = partial_products(same, (far_pair,), keys_w, 0, 2 * width, 2)
     keys = summed_over_chips(near_part + far_part, sizes)
-    values = summed_over_chips(
-        partial_products(same, (near_pair, far_pair), values_w, 2 * width, 2 * width, 0), sizes
-    )
+    value_parts = partial_products(
+        same, (near_pair, far_pair), values_w, 2 * width, 2 * width, 0
+    )
+    values = summed_over_chips(value_parts, sizes)
+    asked = spread(list(after(tuple(chosen), keys[1])))
     features = block.shape[1] * sizes[2]
-    weights, marks = weigh(asked, keys, square, cosine, sine, code, features)
-    routed = mix(weights, marks, values, layers)
-    routed = lax.all_to_all(routed, "section", split_axis=0, concat_axis=0, tiled=True)
-    routed = jnp.roll(routed, 1, axis=0)
-    routed = routed.reshape(layers, heads, reqs, steps, flat // width, 2 * width)
-    routed = routed.transpose(0, 2, 1, 3, 4, 5).astype(jnp.float32)
-    level = jnp.sum(routed[..., width : width + 3], axis=-1, keepdims=True)
-    peak = jnp.maximum(level, top)
-    kept_part = jnp.exp(top - peak)
-    routed_part = jnp.exp(level - peak)
-    result = (mixed * kept_part + routed[..., :width] * routed_part) / (
-        total * kept_part + routed_part
-    )
-    result = result.astype(jnp.bfloat16).transpose(0, 1, 3, 2, 4, 5)
+    here = section.astype(jnp.int32)[None]
+    weights, marks = weigh(here, asked, keys, squares, cosine, sine, code, features)
+    pieces = spread(mix(weights, marks, values, layers))
+    result = merge(here, pieces, kept, levels)
+    result = result.reshape(layers, heads, reqs, steps, flat // width, width)
+    result = result.transpose(0, 2, 3, 1, 4, 5)
     return result.reshape(layers, reqs, steps, heads, flat)[None, None]
 
 
 def solution(mesh):
     shape = mesh.shape
-    body = meet_local if shape["group"] == shape["seq"] == shape["tp"] == 2 else local
+    paired = shape["group"] == shape["seq"] == shape["tp"] == 2
+    body = meet_local if paired and shape["section"] == 4 else local
     return jax.shard_map(
         body,
         mesh=mesh,

time: 94.1 us -> 90 us (0.956)
  blocking collectives: 9.44 us -> 0 us
  starting transfers between devices: 26 us -> 32.3 us
  waiting for transfers between devices: 21.6 us -> 26.8 us
  other arithmetic: 6.23 us -> 2.24 us
  matrix products: 2.49 us -> 0 us
    ppermute x0 -> x6, starting transfers between devices: none -> 11 us  [spread(): lax.ppermute(piece, 'section', [(i, i ^ n) for i in range(len(pieces))])]
    all_to_all x1 -> x0, blocking collectives: 9.44 us -> none  [meet_local(): lax.all_to_all(jnp.roll(asked, -1, axis=0), 'section', split_axis=0, conc...]
    ppermute x0 -> x6, waiting for transfers between devices: none -> 7.59 us  [spread(): lax.ppermute(piece, 'section', [(i, i ^ n) for i in range(len(pieces))])]
    all_to_all x1 -> x0, waiting for transfers between devices: 5.58 us -> none  [meet_local(): lax.all_to_all(routed, 'section', split_axis=0, concat_axis=0, tiled=True)]
    all_to_all x1 -> x0, starting transfers between devices: 3.32 us -> none  [meet_local(): lax.all_to_all(routed, 'section', split_axis=0, concat_axis=0, tiled=True)]
    dot_general x4 -> x0, matrix products: 2.49 us -> none  [the longest x1 0.91 us: attend_kept(): jnp.einsum('lrhngm,lrmhd->lrhngd', exp_step.astype(jnp.bfloat16), step_pa...]
    reduce_sum x1, other arithmetic: 2.58 us -> 0.69 us  [meet_local(): square = jnp.sum(wide * wide, axis=-1)[None]]
    ppermute x3, waiting for transfers between devices: 1.89 us -> 3.69 us  [passed_along(): lax.ppermute(value, axis, [(i, (i + by) % length) for i in range(length)])]
  transfers between devices with their start and end apart: 15 -> 20, of which waited for: 3 -> 6; matrix products, arithmetic and copies ran while one was open for 11% -> 6% of each run, Pallas kernels for 16% -> 18%
where the time goes in v3:
time: 90 us; the launch traced here: 89.5 us
  starting transfers between devices  32.3 us (36%)
  waiting for transfers between devices  26.8 us (30%)
  Pallas kernels  21.1 us (23%)
  local copies, waits for them, and re-layouts  4.88 us (5%)
  other arithmetic  2.24 us (2%)
  between operations  2.1 us (2%)
    ppermute x8, waiting for transfers between devices, steered(): return lax.ppermute(value, ('group', 'seq', 'tp'), pairs)  15.5 us
    ppermute x8, starting transfers between devices, steered(): return lax.ppermute(value, ('group', 'seq', 'tp'), pairs)  12.2 us
    ppermute x6, starting transfers between devices, spread(): lax.ppermute(piece, 'section', [(i, i ^ n) for i in range(len(pieces))])  11 us
    ppermute x3, starting transfers between devices, passed_along(): lax.ppermute(value, axis, [(i, (i + by) % length) for i in range(length)])  7.99 us
    pallas_call x3, Pallas kernels, partial_products(): pl.pallas_call(body, out_shape=[jax.ShapeDtypeStruct((tokens, columns), k...  7.62 us
    ppermute x6, waiting for transfers between devices, spread(): lax.ppermute(piece, 'section', [(i, i ^ n) for i in range(len(pieces))])  7.59 us
    pallas_call x1, Pallas kernels, split_heads(): pl.pallas_call(body, out_shape=[jax.ShapeDtypeStruct((count, 2 * width),...  5.39 us
    pallas_call x1, Pallas kernels, prepare(): pl.pallas_call(body, out_shape=[jax.ShapeDtypeStruct((first + extra, 4 *...  4.44 us
  transfers between devices with their start and end apart: 20, of which 6 were waited for; matrix products, arithmetic and copies ran while one was open for 6% of the time, Pallas kernels for 18%

profile of v3, /device:TPU:0, one launch (start us, length us, event | category | flops | bytes accessed | tf_op | source)
XLA Modules:
  0.0 89.5 jit_solution(731954207207499560)
XLA Ops:
  0.7 4.4 %prepare.1 = (bf16[272,512]{1,0:T(8,128)(2,1)}, bf16[384,2048]{1,0:T(8,128)(2,1)}, bf16[384,2048]{1,0:T(8,128)(2,1)}) custom-call(s32[1]{0:T(128)} %bitcast.2.group_ref, s32[1]{0:T(128)} %bitcast.3.quarter_ref, s32[1]{0:T(128)S(6)} %copy.18.begin_ref, s32[1,384]{1,0:T(1,128)} %bitcast.53, s32[1,384]{1,0:T(1,128)} %slot_ref.1, bf16[384,4096]{1,0:T(8,128)(2,1)} %bitcast.48, ...), custom_call_target="tpu_custom_call" | custom-call | tf_op jit(solution)/shard_map/prepare/pallas_call | solution.py:297
  5.1 2.1 %collective-permute-start = (bf16[384,2048]{1,0:T(8,128)(2,1)}, bf16[384,2048]{1,0:T(8,128)(2,1)S(1)}, u32[]{:S(2)}, u32[]{:S(2)}) collective-permute-start(bf16[384,2048]{1,0:T(8,128)(2,1)} %get-tuple-element.36), channel_id=1, source_target_pairs={{0,0},{1,2},{2,1},{3,3},{16,16},{17,18},{18,17},{19,19},{4,4},{5,6... | collective-permute-start | bytes 4718600 | tf_op jit(solution)/shard_map/ppermute | solution.py:172
  7.2 3.0 %collective-permute-start.8 = (bf16[384,2048]{1,0:T(8,128)(2,1)}, bf16[384,2048]{1,0:T(8,128)(2,1)S(1)}, u32[]{:S(2)}, u32[]{:S(2)}) collective-permute-start(bf16[384,2048]{1,0:T(8,128)(2,1)} %get-tuple-element.51), channel_id=1, source_target_pairs={{0,16},{1,18},{2,17},{3,19},{16,0},{17,2},{18,1},{19,3},{4,20},{5,... | collective-permute-start | bytes 4718600 | tf_op jit(solution)/shard_map/ppermute | solution.py:172
  10.1 3.6 %collective-permute-start.2 = (bf16[272,512]{1,0:T(8,128)(2,1)}, bf16[272,512]{1,0:T(8,128)(2,1)S(1)}, u32[]{:S(2)}, u32[]{:S(2)}) collective-permute-start(bf16[272,512]{1,0:T(8,128)(2,1)} %get-tuple-element.38), channel_id=1, source_target_pairs={{0,12},{4,0},{8,4},{12,8},{1,13},{5,1},{9,5},{13,9},{2,14},{6,2},{... | collective-permute-start | bytes 835592 | tf_op jit(solution)/shard_map/ppermute | solution.py:17
  13.7 5.4 %split_heads.1 = (bf16[1792,256]{1,0:T(8,128)(2,1)}, bf16[1792,256]{1,0:T(8,128)(2,1)}) custom-call(s32[1]{0:T(128)} %bitcast.2.group_ref, s32[1]{0:T(128)} %bitcast.3.quarter_ref, bf16[16384,128]{1,0:T(8,128)(2,1)} %bitcast.47, f32[1,8192]{1,0:T(1,128)} %gain_ref.3), custom_call_target="tpu_custom_call" | custom-call | tf_op jit(solution)/shard_map/split_heads/pallas_call | solution.py:215
  19.6 1.7 %copy.13 = bf16[4,2,2,32,256]{4,3,2,1,0:T(8,128)(2,1)} copy(bf16[4,2,2,32,256]{4,1,3,2,0:T(2,128)(2,1)} %bitcast.50) | data formatting | bytes 524288 | tf_op jit(solution)/shard_map/transpose | solution.py:677
  21.4 3.9 %collective-permute-start.13 = (bf16[1792,256]{1,0:T(8,128)(2,1)}, bf16[1792,256]{1,0:T(8,128)(2,1)}, u32[]{:S(2)}, u32[]{:S(2)}) collective-permute-start(bf16[1792,256]{1,0:T(8,128)(2,1)} %get-tuple-element.58), channel_id=1, source_target_pairs={{0,12},{4,0},{8,4},{12,8},{1,13},{5,1},{9,5},{13,9},{2,14},{6,2},{... | collective-permute-start | bytes 2752520 | tf_op jit(solution)/shard_map/ppermute | solution.py:17
  27.1 1.5 %multiply_sine_fusion = (f32[384,64]{1,0:T(8,128)}, f32[384,64]{1,0:T(8,128)}) fusion(f32[64]{0:T(128)S(1)} %multiply_exponential_fusion, f32[384]{0:T(512)S(1)} %add_convert_fusion), kind=kLoop, calls=%fused_computation.1 | loop fusion | flops 24576 | bytes 198400 | tf_op jit(solution)/shard_map/sin | solution.py:664
  29.7 15.5 %collective-permute-done.8.refs_0_.refs_2_ = bf16[384,2048]{1,0:T(8,128)(2,1)S(1)} collective-permute-done((bf16[384,2048]{1,0:T(8,128)(2,1)}, bf16[384,2048]{1,0:T(8,128)(2,1)S(1)}, u32[]{:S(2)}, u32[]{:S(2)}) %collective-permute-start.8) | collective-permute-done | bytes 1572896 | tf_op jit(solution)/shard_map/ppermute | solution.py:172
  47.1 2.4 %keep.1 = (f32[4,64,128]{2,1,0:T(8,128)S(1)}, f32[4,64,128]{2,1,0:T(8,128)S(1)}) custom-call(s32[2]{0:T(128)S(1)} %bitcast.45, bf16[4,2,32,128]{3,2,1,0:T(8,128)(2,1)S(1)} %bitcast.42, bf16[4,2,64,256]{3,2,1,0:T(8,128)(2,1)S(1)} %bitcast.41, bf16[4,2,4,256]{3,2,1,0:T(4,128)(2,1)S(1)} %copy.16.recent_ref), custom_call_target="tpu_custom_call" | custom-call | flops 40000000000 | bytes 1 | tf_op jit(solution)/shard_map/keep/pallas_call | solution.py:587
  50.3 2.2 %partial_products.3 = (f32[384,256]{1,0:T(8,128)S(1)}, bf16[384,256]{1,0:T(8,128)(2,1)S(1)}) custom-call(s32[1]{0:T(128)} %bitcast.16.same_ref, bf16[384,2048]{1,0:T(8,128)(2,1)S(1)} %collective-permute-done.refs_0_, bf16[384,2048]{1,0:T(8,128)(2,1)S(1)} %collective-permute-done.1.refs_1_, bf16[272,512]{1,0:T(8,128)(2,1)S(1)} %collective-permute-done.2.refs_2_.refs_4_, ...), custom_call_target="tpu_custom_call" | custom-call | tf_op jit(solution)/shard_map/partial_products/pallas_call | solution.py:372
  52.5 1.7 %collective-permute-start.4 = (bf16[384,256]{1,0:T(8,128)(2,1)S(1)}, bf16[384,256]{1,0:T(8,128)(2,1)S(1)}, u32[]{:S(2)}, u32[]{:S(2)}) collective-permute-start(bf16[384,256]{1,0:T(8,128)(2,1)S(1)} %get-tuple-element.45), channel_id=1, source_target_pairs={{0,2},{1,3},{2,0},{3,1},{16,18},{17,19},{18,16},{19,17},{4,6},{5,7... | collective-permute-start | bytes 589832 | tf_op jit(solution)/shard_map/ppermute | solution.py:172
  54.2 2.2 %partial_products.4 = (bf16[384,256]{1,0:T(8,128)(2,1)S(1)}, bf16[384,256]{1,0:T(8,128)(2,1)S(1)}) custom-call(s32[1]{0:T(128)} %bitcast.16.same_ref, bf16[384,2048]{1,0:T(8,128)(2,1)S(1)} %collective-permute-done.8.refs_0_.refs_2_, bf16[384,2048]{1,0:T(8,128)(2,1)S(1)} %collective-permute-done.9.refs_1_.refs_3_, ...), custom_call_target="tpu_custom_call" | custom-call | tf_op jit(solution)/shard_map/partial_products/pallas_call | solution.py:372
  57.0 1.4 %collective-permute-start.11 = (bf16[384,256]{1,0:T(8,128)(2,1)S(1)}, bf16[384,256]{1,0:T(8,128)(2,1)S(1)}, u32[]{:S(2)}, u32[]{:S(2)}) collective-permute-start(bf16[384,256]{1,0:T(8,128)(2,1)S(1)} %get-tuple-element.54), channel_id=1, source_target_pairs={{0,18},{1,19},{2,16},{3,17},{16,2},{17,3},{18,0},{19,1},{4,22},{5,... | collective-permute-start | bytes 589832 | tf_op jit(solution)/shard_map/ppermute | solution.py:172
  58.4 3.7 %collective-permute-done.13.refs_5_ = bf16[1792,256]{1,0:T(8,128)(2,1)} collective-permute-done((bf16[1792,256]{1,0:T(8,128)(2,1)}, bf16[1792,256]{1,0:T(8,128)(2,1)}, u32[]{:S(2)}, u32[]{:S(2)}) %collective-permute-start.13) | collective-permute-done | bytes 917536 | tf_op jit(solution)/shard_map/ppermute | solution.py:17
  62.1 3.2 %partial_products.5 = (f32[384,256]{1,0:T(8,128)S(1)}, bf16[384,256]{1,0:T(8,128)(2,1)S(1)}, bf16[384,256]{1,0:T(8,128)(2,1)S(1)}, bf16[384,256]{1,0:T(8,128)(2,1)S(1)}) custom-call(s32[1]{0:T(128)} %bitcast.16.same_ref, bf16[384,2048]{1,0:T(8,128)(2,1)S(1)} %collective-permute-done.refs_0_, bf16[384,2048]{1,0:T(8,128)(2,1)S(1)} %collective-permute-done.1.refs_1_, ...), custom_call_target="tpu_custom_call" | custom-call | tf_op jit(solution)/shard_map/partial_products/pallas_call | solution.py:372
  66.1 2.8 %collective-permute-start.16 = (bf16[384,256]{1,0:T(8,128)(2,1)S(1)}, bf16[384,256]{1,0:T(8,128)(2,1)S(1)}, u32[]{:S(2)}, u32[]{:S(2)}) collective-permute-start(bf16[384,256]{1,0:T(8,128)(2,1)S(1)} %get-tuple-element.62), channel_id=1, source_target_pairs={{0,18},{1,19},{2,16},{3,17},{16,2},{17,3},{18,0},{19,1},{4,22},{5,... | collective-permute-start | bytes 589832 | tf_op jit(solution)/shard_map/ppermute | solution.py:172
  68.8 1.2 %collective-permute-start.5 = (bf16[2,32,128]{2,1,0:T(8,128)(2,1)S(1)}, bf16[2,32,128]{2,1,0:T(8,128)(2,1)S(1)}, u32[]{:S(2)}, u32[]{:S(2)}) collective-permute-start(bf16[2,32,128]{2,1,0:T(8,128)(2,1)S(1)} %get-tuple-element.47), channel_id=1, source_target_pairs={{0,4},{4,0},{8,12},{12,8},{1,5},{5,1},{9,13},{13,9},{2,6},{6,2},{1... | collective-permute-start | bytes 49160 | tf_op jit(solution)/shard_map/ppermute | solution.py:181
  70.0 2.4 %collective-permute-start.6 = (bf16[2,32,128]{2,1,0:T(8,128)(2,1)S(1)}, bf16[2,32,128]{2,1,0:T(8,128)(2,1)S(1)}, u32[]{:S(2)}, u32[]{:S(2)}) collective-permute-start(bf16[2,32,128]{2,1,0:T(8,128)(2,1)S(1)} %get-tuple-element.48), channel_id=1, source_target_pairs={{0,8},{4,12},{8,0},{12,4},{1,9},{5,13},{9,1},{13,5},{2,10},{6,14},... | collective-permute-start | bytes 49160 | tf_op jit(solution)/shard_map/ppermute | solution.py:181
  72.6 3.0 %collective-permute-start.7 = (bf16[2,32,128]{2,1,0:T(8,128)(2,1)S(1)}, bf16[2,32,128]{2,1,0:T(8,128)(2,1)S(1)}, u32[]{:S(2)}, u32[]{:S(2)}) collective-permute-start(bf16[2,32,128]{2,1,0:T(8,128)(2,1)S(1)} %get-tuple-element.49), channel_id=1, source_target_pairs={{0,12},{4,8},{8,4},{12,0},{1,13},{5,9},{9,5},{13,1},{2,14},{6,10},... | collective-permute-start | bytes 49160 | tf_op jit(solution)/shard_map/ppermute | solution.py:181
  75.6 2.5 %collective-permute-done.7.refs_3_ = bf16[2,32,128]{2,1,0:T(8,128)(2,1)S(1)} collective-permute-done((bf16[2,32,128]{2,1,0:T(8,128)(2,1)S(1)}, bf16[2,32,128]{2,1,0:T(8,128)(2,1)S(1)}, u32[]{:S(2)}, u32[]{:S(2)}) %collective-permute-start.7) | collective-permute-done | bytes 16416 | tf_op jit(solution)/shard_map/ppermute | solution.py:181
  79.4 3.6 %collective-permute-start.18 = (bf16[2,32,256]{2,1,0:T(8,128)(2,1)S(1)}, bf16[2,32,256]{2,1,0:T(8,128)(2,1)S(1)}, u32[]{:S(2)}, u32[]{:S(2)}) collective-permute-start(bf16[2,32,256]{2,1,0:T(8,128)(2,1)S(1)} %get-tuple-element.65), channel_id=1, source_target_pairs={{0,8},{4,12},{8,0},{12,4},{1,9},{5,13},{9,1},{13,5},{2,10},{6,14},... | collective-permute-start | bytes 98312 | tf_op jit(solution)/shard_map/ppermute | solution.py:181
  83.7 1.2 %collective-permute-done.18.rest_2_ = bf16[2,32,256]{2,1,0:T(8,128)(2,1)S(1)} collective-permute-done((bf16[2,32,256]{2,1,0:T(8,128)(2,1)S(1)}, bf16[2,32,256]{2,1,0:T(8,128)(2,1)S(1)}, u32[]{:S(2)}, u32[]{:S(2)}) %collective-permute-start.18) | collective-permute-done | bytes 32800 | tf_op jit(solution)/shard_map/ppermute | solution.py:181
  84.9 3.7 %collective-permute-done.19.rest_3_ = bf16[2,32,256]{2,1,0:T(8,128)(2,1)S(1)} collective-permute-done((bf16[2,32,256]{2,1,0:T(8,128)(2,1)S(1)}, bf16[2,32,256]{2,1,0:T(8,128)(2,1)S(1)}, u32[]{:S(2)}, u32[]{:S(2)}) %collective-permute-start.19) | collective-permute-done | bytes 32800 | tf_op jit(solution)/shard_map/ppermute | solution.py:181
  (52 shorter events, 9.2 us)
Async XLA Ops:
  5.1 23.6 %collective-permute-start = (bf16[384,2048]{1,0:T(8,128)(2,1)}, bf16[384,2048]{1,0:T(8,128)(2,1)S(1)}, u32[]{:S(2)}, u32[]{:S(2)}) collective-permute-start(bf16[384,2048]{1,0:T(8,128)(2,1)} %get-tuple-element.36), channel_id=1, source_target_pairs={{0,0},{1,2},{2,1},{3,3},{16,16},{17,18},{18,17},{19,19},{4,4},{5,6... | collective-permute-start | bytes 4718600 | tf_op jit(solution)/shard_map/ppermute | solution.py:172
  7.2 38.1 %collective-permute-start.8 = (bf16[384,2048]{1,0:T(8,128)(2,1)}, bf16[384,2048]{1,0:T(8,128)(2,1)S(1)}, u32[]{:S(2)}, u32[]{:S(2)}) collective-permute-start(bf16[384,2048]{1,0:T(8,128)(2,1)} %get-tuple-element.51), channel_id=1, source_target_pairs={{0,16},{1,18},{2,17},{3,19},{16,0},{17,2},{18,1},{19,3},{4,20},{5,... | collective-permute-start | bytes 4718600 | tf_op jit(solution)/shard_map/ppermute | solution.py:172
  10.1 11.1 %copy-start.5 = (bf16[1,1,4,2,2,2,256]{6,5,4,3,2,1,0:T(2,128)(2,1)S(1)}, bf16[1,1,4,2,2,2,256]{6,5,4,3,2,1,0:T(2,128)(2,1)}, u32[]{:S(2)}) copy-start(bf16[1,1,4,2,2,2,256]{6,5,4,3,2,1,0:T(2,128)(2,1)} %param.18) | copy-start | bytes 49156
  10.1 36.0 %copy-start.3 = (s32[1,1,2]{2,1,0:T(1,128)S(1)}, s32[1,1,2]{2,1,0:T(1,128)}, u32[]{:S(2)}) copy-start(s32[1,1,2]{2,1,0:T(1,128)} %param.17) | copy-start | bytes 28
  10.1 11.2 %collective-permute-start.2 = (bf16[272,512]{1,0:T(8,128)(2,1)}, bf16[272,512]{1,0:T(8,128)(2,1)S(1)}, u32[]{:S(2)}, u32[]{:S(2)}) collective-permute-start(bf16[272,512]{1,0:T(8,128)(2,1)} %get-tuple-element.38), channel_id=1, source_target_pairs={{0,12},{4,0},{8,4},{12,8},{1,13},{5,1},{9,5},{13,9},{2,14},{6,2},{... | collective-permute-start | bytes 835592 | tf_op jit(solution)/shard_map/ppermute | solution.py:17
  19.1 31.2 %collective-permute-start.3 = (bf16[1792,256]{1,0:T(8,128)(2,1)}, bf16[1792,256]{1,0:T(8,128)(2,1)}, u32[]{:S(2)}, u32[]{:S(2)}) collective-permute-start(bf16[1792,256]{1,0:T(8,128)(2,1)} %get-tuple-element.44), channel_id=1, source_target_pairs={{0,12},{4,0},{8,4},{12,8},{1,13},{5,1},{9,5},{13,9},{2,14},{6,2},{... | collective-permute-start | bytes 2752520 | tf_op jit(solution)/shard_map/ppermute | solution.py:17
  21.4 40.7 %collective-permute-start.13 = (bf16[1792,256]{1,0:T(8,128)(2,1)}, bf16[1792,256]{1,0:T(8,128)(2,1)}, u32[]{:S(2)}, u32[]{:S(2)}) collective-permute-start(bf16[1792,256]{1,0:T(8,128)(2,1)} %get-tuple-element.58), channel_id=1, source_target_pairs={{0,12},{4,0},{8,4},{12,8},{1,13},{5,1},{9,5},{13,9},{2,14},{6,2},{... | collective-permute-start | bytes 2752520 | tf_op jit(solution)/shard_map/ppermute | solution.py:17
  29.6 20.7 %collective-permute-start.1 = (bf16[384,2048]{1,0:T(8,128)(2,1)S(1)}, bf16[384,2048]{1,0:T(8,128)(2,1)S(1)}, u32[]{:S(2)}, u32[]{:S(2)}) collective-permute-start(bf16[384,2048]{1,0:T(8,128)(2,1)S(1)} %collective-permute-done.refs_0_), channel_id=1, source_target_pairs={{0,1},{1,0},{2,3},{3,2},{4,5},{5,4},{6,7},{7,6},{8,9},{9,8},{10,11... | collective-permute-start | bytes 4718600 | tf_op jit(solution)/shard_map/ppermute | solution.py:176
  45.2 9.0 %collective-permute-start.9 = (bf16[384,2048]{1,0:T(8,128)(2,1)S(1)}, bf16[384,2048]{1,0:T(8,128)(2,1)S(1)}, u32[]{:S(2)}, u32[]{:S(2)}) collective-permute-start(bf16[384,2048]{1,0:T(8,128)(2,1)S(1)} %collective-permute-done.8.refs_0_.refs_2_), channel_id=1, source_target_pairs={{0,1},{1,0},{2,3},{3,2},{4,5},{5,4},{6,7},{7,6},{8,9},{9,8},{10,11... | collective-permute-start | bytes 4718600 | tf_op jit(solution)/shard_map/ppermute | solution.py:176
  52.5 13.5 %collective-permute-start.4 = (bf16[384,256]{1,0:T(8,128)(2,1)S(1)}, bf16[384,256]{1,0:T(8,128)(2,1)S(1)}, u32[]{:S(2)}, u32[]{:S(2)}) collective-permute-start(bf16[384,256]{1,0:T(8,128)(2,1)S(1)} %get-tuple-element.45), channel_id=1, source_target_pairs={{0,2},{1,3},{2,0},{3,1},{16,18},{17,19},{18,16},{19,17},{4,6},{5,7... | collective-permute-start | bytes 589832 | tf_op jit(solution)/shard_map/ppermute | solution.py:172
  56.4 12.4 %collective-permute-start.10 = (bf16[384,256]{1,0:T(8,128)(2,1)S(1)}, bf16[384,256]{1,0:T(8,128)(2,1)S(1)}, u32[]{:S(2)}, u32[]{:S(2)}) collective-permute-start(bf16[384,256]{1,0:T(8,128)(2,1)S(1)} %get-tuple-element.53), channel_id=1, source_target_pairs={{0,16},{1,17},{2,18},{3,19},{16,0},{17,1},{18,2},{19,3},{4,20},{5,... | collective-permute-start | bytes 589832 | tf_op jit(solution)/shard_map/ppermute | solution.py:172
  57.0 21.1 %copy-start = (f32[384,64]{1,0:T(8,128)S(1)}, f32[384,64]{1,0:T(8,128)}, u32[]{:S(2)}) copy-start(f32[384,64]{1,0:T(8,128)} %get-tuple-element.71.refs_11_) | copy-start | bytes 294916
  57.0 21.1 %copy-start.1 = (f32[384,64]{1,0:T(8,128)S(1)}, f32[384,64]{1,0:T(8,128)}, u32[]{:S(2)}) copy-start(f32[384,64]{1,0:T(8,128)} %get-tuple-element.72.refs_10_) | copy-start | bytes 294916
  57.0 13.0 %collective-permute-start.11 = (bf16[384,256]{1,0:T(8,128)(2,1)S(1)}, bf16[384,256]{1,0:T(8,128)(2,1)S(1)}, u32[]{:S(2)}, u32[]{:S(2)}) collective-permute-start(bf16[384,256]{1,0:T(8,128)(2,1)S(1)} %get-tuple-element.54), channel_id=1, source_target_pairs={{0,18},{1,19},{2,16},{3,17},{16,2},{17,3},{18,0},{19,1},{4,22},{5,... | collective-permute-start | bytes 589832 | tf_op jit(solution)/shard_map/ppermute | solution.py:172
  58.4 7.0 %collective-permute-start.12 = (f32[1,384]{1,0:T(1,128)S(1)}, f32[1,384]{1,0:T(1,128)S(1)}, u32[]{:S(2)}, u32[]{:S(2)}) collective-permute-start(f32[1,384]{1,0:T(1,128)S(1)} %broadcast_in_dim.25.refs_8_), channel_id=1, source_target_pairs={{0,1},{1,0},{2,3},{3,2},{4,5},{5,4},{6,7},{7,6},{8,9},{9,8},{10,11... | collective-permute-start | bytes 4616 | tf_op jit(solution)/shard_map/ppermute | solution.py:176
  65.3 13.7 %collective-permute-start.14 = (bf16[384,256]{1,0:T(8,128)(2,1)S(1)}, bf16[384,256]{1,0:T(8,128)(2,1)S(1)}, u32[]{:S(2)}, u32[]{:S(2)}) collective-permute-start(bf16[384,256]{1,0:T(8,128)(2,1)S(1)} %get-tuple-element.60), channel_id=1, source_target_pairs={{0,2},{1,3},{2,0},{3,1},{16,18},{17,19},{18,16},{19,17},{4,6},{5,7... | collective-permute-start | bytes 589832 | tf_op jit(solution)/shard_map/ppermute | solution.py:172
  65.4 13.6 %collective-permute-start.15 = (bf16[384,256]{1,0:T(8,128)(2,1)S(1)}, bf16[384,256]{1,0:T(8,128)(2,1)S(1)}, u32[]{:S(2)}, u32[]{:S(2)}) collective-permute-start(bf16[384,256]{1,0:T(8,128)(2,1)S(1)} %get-tuple-element.61), channel_id=1, source_target_pairs={{0,16},{1,17},{2,18},{3,19},{16,0},{17,1},{18,2},{19,3},{4,20},{5,... | collective-permute-start | bytes 589832 | tf_op jit(solution)/shard_map/ppermute | solution.py:172
  66.1 12.9 %collective-permute-start.16 = (bf16[384,256]{1,0:T(8,128)(2,1)S(1)}, bf16[384,256]{1,0:T(8,128)(2,1)S(1)}, u32[]{:S(2)}, u32[]{:S(2)}) collective-permute-start(bf16[384,256]{1,0:T(8,128)(2,1)S(1)} %get-tuple-element.62), channel_id=1, source_target_pairs={{0,18},{1,19},{2,16},{3,17},{16,2},{17,3},{18,0},{19,1},{4,22},{5,... | collective-permute-start | bytes 589832 | tf_op jit(solution)/shard_map/ppermute | solution.py:172
  68.8 3.7 %collective-permute-start.5 = (bf16[2,32,128]{2,1,0:T(8,128)(2,1)S(1)}, bf16[2,32,128]{2,1,0:T(8,128)(2,1)S(1)}, u32[]{:S(2)}, u32[]{:S(2)}) collective-permute-start(bf16[2,32,128]{2,1,0:T(8,128)(2,1)S(1)} %get-tuple-element.47), channel_id=1, source_target_pairs={{0,4},{4,0},{8,12},{12,8},{1,5},{5,1},{9,13},{13,9},{2,6},{6,2},{1... | collective-permute-start | bytes 49160 | tf_op jit(solution)/shard_map/ppermute | solution.py:181
  70.0 5.6 %collective-permute-start.6 = (bf16[2,32,128]{2,1,0:T(8,128)(2,1)S(1)}, bf16[2,32,128]{2,1,0:T(8,128)(2,1)S(1)}, u32[]{:S(2)}, u32[]{:S(2)}) collective-permute-start(bf16[2,32,128]{2,1,0:T(8,128)(2,1)S(1)} %get-tuple-element.48), channel_id=1, source_target_pairs={{0,8},{4,12},{8,0},{12,4},{1,9},{5,13},{9,1},{13,5},{2,10},{6,14},... | collective-permute-start | bytes 49160 | tf_op jit(solution)/shard_map/ppermute | solution.py:181
  72.6 5.5 %collective-permute-start.7 = (bf16[2,32,128]{2,1,0:T(8,128)(2,1)S(1)}, bf16[2,32,128]{2,1,0:T(8,128)(2,1)S(1)}, u32[]{:S(2)}, u32[]{:S(2)}) collective-permute-start(bf16[2,32,128]{2,1,0:T(8,128)(2,1)S(1)} %get-tuple-element.49), channel_id=1, source_target_pairs={{0,12},{4,8},{8,4},{12,0},{1,13},{5,9},{9,5},{13,1},{2,14},{6,10},... | collective-permute-start | bytes 49160 | tf_op jit(solution)/shard_map/ppermute | solution.py:181
  79.3 4.5 %collective-permute-start.17 = (bf16[2,32,256]{2,1,0:T(8,128)(2,1)S(1)}, bf16[2,32,256]{2,1,0:T(8,128)(2,1)S(1)}, u32[]{:S(2)}, u32[]{:S(2)}) collective-permute-start(bf16[2,32,256]{2,1,0:T(8,128)(2,1)S(1)} %get-tuple-element.64), channel_id=1, source_target_pairs={{0,4},{4,0},{8,12},{12,8},{1,5},{5,1},{9,13},{13,9},{2,6},{6,2},{1... | collective-permute-start | bytes 98312 | tf_op jit(solution)/shard_map/ppermute | solution.py:181
  79.4 5.6 %collective-permute-start.18 = (bf16[2,32,256]{2,1,0:T(8,128)(2,1)S(1)}, bf16[2,32,256]{2,1,0:T(8,128)(2,1)S(1)}, u32[]{:S(2)}, u32[]{:S(2)}) collective-permute-start(bf16[2,32,256]{2,1,0:T(8,128)(2,1)S(1)} %get-tuple-element.65), channel_id=1, source_target_pairs={{0,8},{4,12},{8,0},{12,4},{1,9},{5,13},{9,1},{13,5},{2,10},{6,14},... | collective-permute-start | bytes 98312 | tf_op jit(solution)/shard_map/ppermute | solution.py:181
  82.9 5.7 %collective-permute-start.19 = (bf16[2,32,256]{2,1,0:T(8,128)(2,1)S(1)}, bf16[2,32,256]{2,1,0:T(8,128)(2,1)S(1)}, u32[]{:S(2)}, u32[]{:S(2)}) collective-permute-start(bf16[2,32,256]{2,1,0:T(8,128)(2,1)S(1)} %get-tuple-element.66), channel_id=1, source_target_pairs={{0,12},{4,8},{8,4},{12,0},{1,13},{5,9},{9,5},{13,1},{2,14},{6,10},... | collective-permute-start | bytes 98312 | tf_op jit(solution)/shard_map/ppermute | solution.py:181
  (2 other events, 3.4 us)

commit v4 on v3

--- a/solution.py
+++ b/solution.py
@@ -387,11 +387,12 @@
 def summed_over_chips(parts, sizes):
     own, across, far, far_across = parts
     groups, seqs, _ = sizes
+    farthest = steered(far_across, lambda g, q, t: (groups - 1 - g, seqs - 1 - q, t), sizes)
     return (
         own,
+        farthest,
+        steered(far, lambda g, q, t: (groups - 1 - g, q, t), sizes),
         steered(across, lambda g, q, t: (g, seqs - 1 - q, t), sizes),
-        steered(far, lambda g, q, t: (groups - 1 - g, q, t), sizes),
-        steered(far_across, lambda g, q, t: (groups - 1 - g, seqs - 1 - q, t), sizes),
     )
 
 
@@ -413,7 +414,7 @@
         owner = (place // rows) ^ section_ref[0]
         request = owner * requests + place % rows // (rows // requests)
         mine = request == code_ref[...]
-        lane = lax.broadcasted_iota(jnp.int32, (span, width), 1)
+        line = lax.broadcasted_iota(jnp.int32, (8, span), 0)
         for h in range(heads):
             columns = slice(h * width, (h + 1) * width)
             key = key_refs[0][:, columns]
@@ -440,11 +441,12 @@
             safe = jnp.where(some, total, 1.0)
             weight_ref[h] = (weight / safe * scale).astype(jnp.bfloat16)
             level = jnp.where(some, top + jnp.log(safe), NEG)
+            level = jnp.broadcast_to(level, (span, span)).T[:8, :]
             high = level.astype(jnp.bfloat16).astype(jnp.float32)
             middle = (level - high).astype(jnp.bfloat16).astype(jnp.float32)
             low = level - high - middle
             mark_ref[h] = jnp.where(
-                lane == 0, high, jnp.where(lane == 1, middle, jnp.where(lane == 2, low, 0.0))
+                line == 0, high, jnp.where(line == 1, middle, jnp.where(line == 2, low, 0.0))
             ).astype(jnp.bfloat16)
 
     vmem = pl.BlockSpec(memory_space=pltpu.VMEM)
@@ -453,7 +455,7 @@
         body,
         out_shape=[
             jax.ShapeDtypeStruct((heads, span, tokens), jnp.bfloat16),
-            jax.ShapeDtypeStruct((heads, span, width), jnp.bfloat16),
+            jax.ShapeDtypeStruct((heads, 8, span), jnp.bfloat16),
         ],
         in_specs=[pl.BlockSpec(memory_space=pltpu.SMEM)] + [vmem] * len(operands),
         out_specs=[vmem] * 2,
@@ -464,7 +466,7 @@
 
 def mix(weights, marks, values, owners):
     heads, span, _ = weights.shape
-    width = marks.shape[2]
+    width = values[0].shape[1] // heads
     rows = span // owners
 
     def body(weight_ref, mark_ref, *rest):
@@ -478,14 +480,14 @@
                 weight_ref[h], value.astype(jnp.bfloat16), preferred_element_type=jnp.float32
             ).astype(jnp.bfloat16)
             for step in range(owners):
-                outs[step][h, :, :width] = mixed[step * rows : (step + 1) * rows]
-                outs[step][h, :, width:] = mark_ref[h, step * rows : (step + 1) * rows, :]
+                outs[step][h, :rows, :] = mixed[step * rows : (step + 1) * rows]
+                outs[step][h, rows:, :] = mark_ref[h]
 
     vmem = pl.BlockSpec(memory_space=pltpu.VMEM)
     operands = (weights, marks, *values)
     return pl.pallas_call(
         body,
-        out_shape=[jax.ShapeDtypeStruct((heads, rows, 2 * width), jnp.bfloat16)] * owners,
+        out_shape=[jax.ShapeDtypeStruct((heads, rows + marks.shape[1], width), jnp.bfloat16)] * owners,
         in_specs=[vmem] * len(operands),
         out_specs=[vmem] * owners,
         compiler_params=pltpu.CompilerParams(vmem_limit_bytes=4 << 20),
@@ -495,17 +497,24 @@
 
 def merge(section, pieces, mixed, levels):
     layers, spans, width = mixed.shape
-    heads, rows, _ = pieces[0].shape
+    heads = pieces[0].shape[0]
+    rows = spans // heads
 
     def body(section_ref, *rest):
         piece_refs = rest[: len(pieces)]
         mixed_ref, level_ref, out_ref = rest[len(pieces) :]
+        lane = lax.broadcasted_iota(jnp.int32, (rows, width), 1)
+        row = lax.broadcasted_iota(jnp.int32, (rows, width), 0)
         for step, ref in enumerate(piece_refs):
             layer = ((section_ref[0] ^ step) + 1) % layers
-            routed = jnp.concatenate([ref[h] for h in range(heads)], axis=0)
-            level = jnp.sum(
-                routed[:, width : width + 3].astype(jnp.float32), axis=1, keepdims=True
-            )
+            routed = jnp.concatenate([ref[h, :rows, :] for h in range(heads)], axis=0)
+            mine = lane == row + step * rows
+            level = []
+            for h in range(heads):
+                marks = ref[h, rows:, :].astype(jnp.float32)
+                marks = marks[0:1] + marks[1:2] + marks[2:3]
+                level.append(jnp.sum(jnp.where(mine, marks, 0.0), axis=1, keepdims=True))
+            level = jnp.concatenate(level, axis=0)
             high = level_ref[layer]
             peak = jnp.maximum(level, high)
             kept = jnp.exp(high - peak)
@@ -513,7 +522,7 @@
             share = 1.0 / (kept + other)
             out_ref[layer] = (
                 mixed_ref[layer] * (kept * share)
-                + routed[:, :width].astype(jnp.float32) * (other * share)
+                + routed.astype(jnp.float32) * (other * share)
             ).astype(jnp.bfloat16)
 
     vmem = pl.BlockSpec(memory_space=pltpu.VMEM)
@@ -676,9 +685,11 @@
     ]
     cache = kv_cache[0, 0].transpose(0, 3, 1, 2, 4).reshape(layers, heads, -1, 2 * width)
     recent = step_kv[0, 0].transpose(0, 3, 1, 2, 4).reshape(layers, heads, -1, 2 * width)
-    kept, levels = keep(everything, cache, recent, cache_lens[0, 0], steps)
-
-    near_mate = after(near_mate, (cosine, sine, code, square, kept, levels, *chosen))
+    kept, levels = keep(
+        everything, cache, recent, after(cache_lens[0, 0], square), steps
+    )
+
+    near_mate = after(near_mate, (cosine, sine, code, *squares, kept, levels, *chosen))
     keys_w = (start_got, keys_got)
     values_w = (start_got, values_got)
     near_pair = ((near_got,), (near_mate,))
@@ -691,7 +702,9 @@
         same, (near_pair, far_pair), values_w, 2 * width, 2 * width, 0
     )
     values = summed_over_chips(value_parts, sizes)
-    asked = spread(list(after(tuple(chosen), keys[1])))
+    late = after(tuple(chosen), keys[1])
+    soon = after(tuple(chosen), far_part[0])
+    asked = spread([soon[n] if n in (1,) else late[n] for n in range(layers)])
     features = block.shape[1] * sizes[2]
     here = section.astype(jnp.int32)[None]
     weights, marks = weigh(here, asked, keys, squares, cosine, sine, code, features)

time: 90 us -> 87.1 us (0.968)
  waiting for transfers between devices: 26.8 us -> 24.8 us
  starting transfers between devices: 32.3 us -> 30.3 us
  other arithmetic: 2.24 us -> 4.15 us
  local copies, waits for them, and re-layouts: 4.88 us -> 3.93 us
    ppermute x6, starting transfers between devices: 11 us -> 8.68 us  [spread(): lax.ppermute(piece, 'section', [(i, i ^ n) for i in range(len(pieces))])]
    ppermute x8, waiting for transfers between devices: 15.5 us -> 13.3 us  [steered(): return lax.ppermute(value, ('group', 'seq', 'tp'), pairs)]
    reduce_sum x1, other arithmetic: 0.69 us -> 2.62 us  [meet_local(): square = jnp.sum(wide * wide, axis=-1)[None]]
    unnamed x12 -> x10, local copies, waits for them, and re-layouts: 0.97 us -> 0.02 us
  transfers between devices with their start and end apart: 20 -> 20, of which waited for: 6 -> 8; matrix products, arithmetic and copies ran while one was open for 6% -> 8% of each run, Pallas kernels for 18% -> 19%
where the time goes in v4:
time: 87.1 us; the launch traced here: 86.6 us
  starting transfers between devices  30.3 us (35%)
  waiting for transfers between devices  24.8 us (28%)
  Pallas kernels  21.2 us (24%)
  other arithmetic  4.15 us (5%)
  local copies, waits for them, and re-layouts  3.93 us (5%)
  between operations  2.12 us (2%)
    ppermute x8, waiting for transfers between devices, steered(): return lax.ppermute(value, ('group', 'seq', 'tp'), pairs)  13.3 us
    ppermute x8, starting transfers between devices, steered(): return lax.ppermute(value, ('group', 'seq', 'tp'), pairs)  12.1 us
    ppermute x6, starting transfers between devices, spread(): lax.ppermute(piece, 'section', [(i, i ^ n) for i in range(len(pieces))])  8.68 us
    ppermute x3, starting transfers between devices, passed_along(): lax.ppermute(value, axis, [(i, (i + by) % length) for i in range(length)])  7.99 us
    pallas_call x3, Pallas kernels, partial_products(): pl.pallas_call(body, out_shape=[jax.ShapeDtypeStruct((tokens, columns), k...  7.62 us
    ppermute x6, waiting for transfers between devices, spread(): lax.ppermute(piece, 'section', [(i, i ^ n) for i in range(len(pieces))])  7.51 us
    pallas_call x1, Pallas kernels, split_heads(): pl.pallas_call(body, out_shape=[jax.ShapeDtypeStruct((count, 2 * width),...  5.39 us
    pallas_call x1, Pallas kernels, prepare(): pl.pallas_call(body, out_shape=[jax.ShapeDtypeStruct((first + extra, 4 *...  4.43 us
  transfers between devices with their start and end apart: 20, of which 8 were waited for; matrix products, arithmetic and copies ran while one was open for 8% of the time, Pallas kernels for 19%

profile of v4, /device:TPU:0, one launch (start us, length us, event | category | flops | bytes accessed | tf_op | source)
XLA Modules:
  0.0 86.6 jit_solution(238914352590644375)
XLA Ops:
  0.7 4.4 %prepare.1 = (bf16[272,512]{1,0:T(8,128)(2,1)}, bf16[384,2048]{1,0:T(8,128)(2,1)}, bf16[384,2048]{1,0:T(8,128)(2,1)}) custom-call(s32[1]{0:T(128)} %bitcast.2.group_ref, s32[1]{0:T(128)} %bitcast.3.quarter_ref, s32[1]{0:T(128)S(6)} %copy.18.begin_ref, s32[1,384]{1,0:T(1,128)} %bitcast.53, s32[1,384]{1,0:T(1,128)} %slot_ref.1, bf16[384,4096]{1,0:T(8,128)(2,1)} %bitcast.48, ...), custom_call_target="tpu_custom_call" | custom-call | tf_op jit(solution)/shard_map/prepare/pallas_call | solution.py:297
  5.1 2.1 %collective-permute-start = (bf16[384,2048]{1,0:T(8,128)(2,1)}, bf16[384,2048]{1,0:T(8,128)(2,1)S(1)}, u32[]{:S(2)}, u32[]{:S(2)}) collective-permute-start(bf16[384,2048]{1,0:T(8,128)(2,1)} %get-tuple-element.37), channel_id=1, source_target_pairs={{0,0},{1,2},{2,1},{3,3},{16,16},{17,18},{18,17},{19,19},{4,4},{5,6... | collective-permute-start | bytes 4718600 | tf_op jit(solution)/shard_map/ppermute | solution.py:172
  7.2 3.0 %collective-permute-start.1 = (bf16[384,2048]{1,0:T(8,128)(2,1)}, bf16[384,2048]{1,0:T(8,128)(2,1)S(1)}, u32[]{:S(2)}, u32[]{:S(2)}) collective-permute-start(bf16[384,2048]{1,0:T(8,128)(2,1)} %get-tuple-element.39), channel_id=1, source_target_pairs={{0,16},{1,18},{2,17},{3,19},{16,0},{17,2},{18,1},{19,3},{4,20},{5,... | collective-permute-start | bytes 4718600 | tf_op jit(solution)/shard_map/ppermute | solution.py:172
  10.1 3.6 %collective-permute-start.4 = (bf16[272,512]{1,0:T(8,128)(2,1)}, bf16[272,512]{1,0:T(8,128)(2,1)S(1)}, u32[]{:S(2)}, u32[]{:S(2)}) collective-permute-start(bf16[272,512]{1,0:T(8,128)(2,1)} %get-tuple-element.40), channel_id=1, source_target_pairs={{0,12},{4,0},{8,4},{12,8},{1,13},{5,1},{9,5},{13,9},{2,14},{6,2},{... | collective-permute-start | bytes 835592 | tf_op jit(solution)/shard_map/ppermute | solution.py:17
  13.7 5.4 %split_heads.1 = (bf16[1792,256]{1,0:T(8,128)(2,1)}, bf16[1792,256]{1,0:T(8,128)(2,1)}) custom-call(s32[1]{0:T(128)} %bitcast.2.group_ref, s32[1]{0:T(128)} %bitcast.3.quarter_ref, bf16[16384,128]{1,0:T(8,128)(2,1)} %bitcast.47, f32[1,8192]{1,0:T(1,128)} %gain_ref.3), custom_call_target="tpu_custom_call" | custom-call | tf_op jit(solution)/shard_map/split_heads/pallas_call | solution.py:215
  19.6 1.7 %copy.13 = bf16[4,2,2,32,256]{4,3,2,1,0:T(8,128)(2,1)} copy(bf16[4,2,2,32,256]{4,1,3,2,0:T(2,128)(2,1)} %bitcast.50) | data formatting | bytes 524288 | tf_op jit(solution)/shard_map/transpose | solution.py:686
  21.3 3.9 %collective-permute-start.13 = (bf16[1792,256]{1,0:T(8,128)(2,1)}, bf16[1792,256]{1,0:T(8,128)(2,1)}, u32[]{:S(2)}, u32[]{:S(2)}) collective-permute-start(bf16[1792,256]{1,0:T(8,128)(2,1)} %get-tuple-element.60), channel_id=1, source_target_pairs={{0,12},{4,0},{8,4},{12,8},{1,13},{5,1},{9,5},{13,9},{2,14},{6,2},{... | collective-permute-start | bytes 2752520 | tf_op jit(solution)/shard_map/ppermute | solution.py:17
  27.2 1.5 %multiply_sine_fusion = (f32[384,64]{1,0:T(8,128)}, f32[384,64]{1,0:T(8,128)}) fusion(f32[64]{0:T(128)S(1)} %multiply_exponential_fusion, f32[384]{0:T(512)S(1)} %add_convert_fusion), kind=kLoop, calls=%fused_computation.1 | loop fusion | flops 24576 | bytes 198400 | tf_op jit(solution)/shard_map/sin | solution.py:673
  29.6 2.6 %multiply_reduce_fusion = f32[384]{0:T(512)S(1)} fusion(bf16[384,4096]{1,0:T(8,128)(2,1)} %bitcast.49), kind=kLoop, calls=%fused_computation | loop fusion | flops 4718208 | bytes 3147264 | tf_op jit(solution)/shard_map/reduce_sum | solution.py:662
  32.8 12.4 %collective-permute-done.1.refs_0_.refs_2_ = bf16[384,2048]{1,0:T(8,128)(2,1)S(1)} collective-permute-done((bf16[384,2048]{1,0:T(8,128)(2,1)}, bf16[384,2048]{1,0:T(8,128)(2,1)S(1)}, u32[]{:S(2)}, u32[]{:S(2)}) %collective-permute-start.1) | collective-permute-done | bytes 1572896 | tf_op jit(solution)/shard_map/ppermute | solution.py:172
  46.2 2.4 %keep.1 = (f32[4,64,128]{2,1,0:T(8,128)S(1)}, f32[4,64,128]{2,1,0:T(8,128)S(1)}) custom-call(s32[2]{0:T(128)S(1)} %bitcast.45, bf16[4,2,32,128]{3,2,1,0:T(8,128)(2,1)S(1)} %bitcast.43, bf16[4,2,64,256]{3,2,1,0:T(8,128)(2,1)S(1)} %bitcast.42, bf16[4,2,4,256]{3,2,1,0:T(4,128)(2,1)S(1)} %copy.16.recent_ref), custom_call_target="tpu_custom_call" | custom-call | flops 40000000000 | bytes 1 | tf_op jit(solution)/shard_map/keep/pallas_call | solution.py:596
  48.6 2.2 %partial_products.3 = (f32[384,256]{1,0:T(8,128)S(1)}, bf16[384,256]{1,0:T(8,128)(2,1)S(1)}) custom-call(s32[1]{0:T(128)} %bitcast.16.same_ref, bf16[384,2048]{1,0:T(8,128)(2,1)S(1)} %collective-permute-done.refs_0_, bf16[384,2048]{1,0:T(8,128)(2,1)S(1)} %collective-permute-done.3.refs_1_, bf16[272,512]{1,0:T(8,128)(2,1)S(1)} %collective-permute-done.4.refs_2_.refs_4_, ...), custom_call_target="tpu_custom_call" | custom-call | tf_op jit(solution)/shard_map/partial_products/pallas_call | solution.py:372
  50.9 2.2 %partial_products.4 = (bf16[384,256]{1,0:T(8,128)(2,1)S(1)}, bf16[384,256]{1,0:T(8,128)(2,1)S(1)}) custom-call(s32[1]{0:T(128)} %bitcast.16.same_ref, bf16[384,2048]{1,0:T(8,128)(2,1)S(1)} %collective-permute-done.1.refs_0_.refs_2_, bf16[384,2048]{1,0:T(8,128)(2,1)S(1)} %collective-permute-done.2.refs_1_.refs_3_, ...), custom_call_target="tpu_custom_call" | custom-call | tf_op jit(solution)/shard_map/partial_products/pallas_call | solution.py:372
  53.1 1.6 %collective-permute-start.7 = (bf16[384,256]{1,0:T(8,128)(2,1)S(1)}, bf16[384,256]{1,0:T(8,128)(2,1)S(1)}, u32[]{:S(2)}, u32[]{:S(2)}) collective-permute-start(bf16[384,256]{1,0:T(8,128)(2,1)S(1)} %get-tuple-element.51), channel_id=1, source_target_pairs={{0,18},{1,19},{2,16},{3,17},{16,2},{17,3},{18,0},{19,1},{4,22},{5,... | collective-permute-start | bytes 589832 | tf_op jit(solution)/shard_map/ppermute | solution.py:172
  54.7 1.5 %collective-permute-start.11 = (bf16[384,256]{1,0:T(8,128)(2,1)S(1)}, bf16[384,256]{1,0:T(8,128)(2,1)S(1)}, u32[]{:S(2)}, u32[]{:S(2)}) collective-permute-start(bf16[384,256]{1,0:T(8,128)(2,1)S(1)} %get-tuple-element.53), channel_id=1, source_target_pairs={{0,16},{1,17},{2,18},{3,19},{16,0},{17,1},{18,2},{19,3},{4,20},{5,... | collective-permute-start | bytes 589832 | tf_op jit(solution)/shard_map/ppermute | solution.py:172
  56.6 1.6 %collective-permute-start.8 = (bf16[2,32,128]{2,1,0:T(8,128)(2,1)S(1)}, bf16[2,32,128]{2,1,0:T(8,128)(2,1)S(1)}, u32[]{:S(2)}, u32[]{:S(2)}) collective-permute-start(bf16[2,32,128]{2,1,0:T(8,128)(2,1)S(1)} %get-tuple-element.54), channel_id=1, source_target_pairs={{0,4},{4,0},{8,12},{12,8},{1,5},{5,1},{9,13},{13,9},{2,6},{6,2},{1... | collective-permute-start | bytes 49160 | tf_op jit(solution)/shard_map/ppermute | solution.py:181
  58.2 4.0 %collective-permute-done.13.refs_5_ = bf16[1792,256]{1,0:T(8,128)(2,1)} collective-permute-done((bf16[1792,256]{1,0:T(8,128)(2,1)}, bf16[1792,256]{1,0:T(8,128)(2,1)}, u32[]{:S(2)}, u32[]{:S(2)}) %collective-permute-start.13) | collective-permute-done | bytes 917536 | tf_op jit(solution)/shard_map/ppermute | solution.py:17
  62.2 3.2 %partial_products.5 = (f32[384,256]{1,0:T(8,128)S(1)}, bf16[384,256]{1,0:T(8,128)(2,1)S(1)}, bf16[384,256]{1,0:T(8,128)(2,1)S(1)}, bf16[384,256]{1,0:T(8,128)(2,1)S(1)}) custom-call(s32[1]{0:T(128)} %bitcast.16.same_ref, bf16[384,2048]{1,0:T(8,128)(2,1)S(1)} %collective-permute-done.refs_0_, bf16[384,2048]{1,0:T(8,128)(2,1)S(1)} %collective-permute-done.3.refs_1_, ...), custom_call_target="tpu_custom_call" | custom-call | tf_op jit(solution)/shard_map/partial_products/pallas_call | solution.py:372
  65.5 1.5 %collective-permute-start.15 = (bf16[384,256]{1,0:T(8,128)(2,1)S(1)}, bf16[384,256]{1,0:T(8,128)(2,1)S(1)}, u32[]{:S(2)}, u32[]{:S(2)}) collective-permute-start(bf16[384,256]{1,0:T(8,128)(2,1)S(1)} %get-tuple-element.63), channel_id=1, source_target_pairs={{0,16},{1,17},{2,18},{3,19},{16,0},{17,1},{18,2},{19,3},{4,20},{5,... | collective-permute-start | bytes 589832 | tf_op jit(solution)/shard_map/ppermute | solution.py:172
  67.1 2.0 %collective-permute-start.16 = (bf16[384,256]{1,0:T(8,128)(2,1)S(1)}, bf16[384,256]{1,0:T(8,128)(2,1)S(1)}, u32[]{:S(2)}, u32[]{:S(2)}) collective-permute-start(bf16[384,256]{1,0:T(8,128)(2,1)S(1)} %get-tuple-element.64), channel_id=1, source_target_pairs={{0,2},{1,3},{2,0},{3,1},{16,18},{17,19},{18,16},{19,17},{4,6},{5,7... | collective-permute-start | bytes 589832 | tf_op jit(solution)/shard_map/ppermute | solution.py:172
  69.0 2.6 %collective-permute-start.10 = (bf16[2,32,128]{2,1,0:T(8,128)(2,1)S(1)}, bf16[2,32,128]{2,1,0:T(8,128)(2,1)S(1)}, u32[]{:S(2)}, u32[]{:S(2)}) collective-permute-start(bf16[2,32,128]{2,1,0:T(8,128)(2,1)S(1)} %get-tuple-element.56), channel_id=1, source_target_pairs={{0,12},{4,8},{8,4},{12,0},{1,13},{5,9},{9,5},{13,1},{2,14},{6,10},... | collective-permute-start | bytes 49160 | tf_op jit(solution)/shard_map/ppermute | solution.py:181
  71.7 2.0 %collective-permute-done.9.refs_2_ = bf16[2,32,128]{2,1,0:T(8,128)(2,1)S(1)} collective-permute-done((bf16[2,32,128]{2,1,0:T(8,128)(2,1)S(1)}, bf16[2,32,128]{2,1,0:T(8,128)(2,1)S(1)}, u32[]{:S(2)}, u32[]{:S(2)}) %collective-permute-start.9) | collective-permute-done | bytes 16416 | tf_op jit(solution)/shard_map/ppermute | solution.py:181
  77.1 2.9 %collective-permute-start.18 = (bf16[2,40,128]{2,1,0:T(8,128)(2,1)S(1)}, bf16[2,40,128]{2,1,0:T(8,128)(2,1)S(1)}, u32[]{:S(2)}, u32[]{:S(2)}) collective-permute-start(bf16[2,40,128]{2,1,0:T(8,128)(2,1)S(1)} %get-tuple-element.67), channel_id=1, source_target_pairs={{0,8},{4,12},{8,0},{12,4},{1,9},{5,13},{9,1},{13,5},{2,10},{6,14},... | collective-permute-start | bytes 61448 | tf_op jit(solution)/shard_map/ppermute | solution.py:181
  81.8 3.8 %collective-permute-done.19.rest_3_ = bf16[2,40,128]{2,1,0:T(8,128)(2,1)S(1)} collective-permute-done((bf16[2,40,128]{2,1,0:T(8,128)(2,1)S(1)}, bf16[2,40,128]{2,1,0:T(8,128)(2,1)S(1)}, u32[]{:S(2)}, u32[]{:S(2)}) %collective-permute-start.19) | collective-permute-done | bytes 20512 | tf_op jit(solution)/shard_map/ppermute | solution.py:181
  (50 shorter events, 10.2 us)
Async XLA Ops:
  5.1 23.6 %collective-permute-start = (bf16[384,2048]{1,0:T(8,128)(2,1)}, bf16[384,2048]{1,0:T(8,128)(2,1)S(1)}, u32[]{:S(2)}, u32[]{:S(2)}) collective-permute-start(bf16[384,2048]{1,0:T(8,128)(2,1)} %get-tuple-element.37), channel_id=1, source_target_pairs={{0,0},{1,2},{2,1},{3,3},{16,16},{17,18},{18,17},{19,19},{4,4},{5,6... | collective-permute-start | bytes 4718600 | tf_op jit(solution)/shard_map/ppermute | solution.py:172
  7.2 38.1 %collective-permute-start.1 = (bf16[384,2048]{1,0:T(8,128)(2,1)}, bf16[384,2048]{1,0:T(8,128)(2,1)S(1)}, u32[]{:S(2)}, u32[]{:S(2)}) collective-permute-start(bf16[384,2048]{1,0:T(8,128)(2,1)} %get-tuple-element.39), channel_id=1, source_target_pairs={{0,16},{1,18},{2,17},{3,19},{16,0},{17,2},{18,1},{19,3},{4,20},{5,... | collective-permute-start | bytes 4718600 | tf_op jit(solution)/shard_map/ppermute | solution.py:172
  10.1 11.2 %collective-permute-start.4 = (bf16[272,512]{1,0:T(8,128)(2,1)}, bf16[272,512]{1,0:T(8,128)(2,1)S(1)}, u32[]{:S(2)}, u32[]{:S(2)}) collective-permute-start(bf16[272,512]{1,0:T(8,128)(2,1)} %get-tuple-element.40), channel_id=1, source_target_pairs={{0,12},{4,0},{8,4},{12,8},{1,13},{5,1},{9,5},{13,9},{2,14},{6,2},{... | collective-permute-start | bytes 835592 | tf_op jit(solution)/shard_map/ppermute | solution.py:17
  19.1 29.5 %collective-permute-start.6 = (bf16[1792,256]{1,0:T(8,128)(2,1)}, bf16[1792,256]{1,0:T(8,128)(2,1)}, u32[]{:S(2)}, u32[]{:S(2)}) collective-permute-start(bf16[1792,256]{1,0:T(8,128)(2,1)} %get-tuple-element.47), channel_id=1, source_target_pairs={{0,12},{4,0},{8,4},{12,8},{1,13},{5,1},{9,5},{13,9},{2,14},{6,2},{... | collective-permute-start | bytes 2752520 | tf_op jit(solution)/shard_map/ppermute | solution.py:17
  21.3 40.9 %collective-permute-start.13 = (bf16[1792,256]{1,0:T(8,128)(2,1)}, bf16[1792,256]{1,0:T(8,128)(2,1)}, u32[]{:S(2)}, u32[]{:S(2)}) collective-permute-start(bf16[1792,256]{1,0:T(8,128)(2,1)} %get-tuple-element.60), channel_id=1, source_target_pairs={{0,12},{4,0},{8,4},{12,8},{1,13},{5,1},{9,5},{13,9},{2,14},{6,2},{... | collective-permute-start | bytes 2752520 | tf_op jit(solution)/shard_map/ppermute | solution.py:17
  29.6 16.6 %copy-start.2 = (bf16[4,2,2,32,256]{4,3,2,1,0:T(8,128)(2,1)S(1)}, bf16[4,2,2,32,256]{4,3,2,1,0:T(8,128)(2,1)}, u32[]{:S(2)}) copy-start(bf16[4,2,2,32,256]{4,3,2,1,0:T(8,128)(2,1)} %copy.13) | copy-start | bytes 786436
  29.6 16.6 %copy-start.3 = (s32[1,1,2]{2,1,0:T(1,128)S(1)}, s32[1,1,2]{2,1,0:T(1,128)}, u32[]{:S(2)}) copy-start(s32[1,1,2]{2,1,0:T(1,128)} %param.17) | copy-start | bytes 28
  32.2 16.4 %collective-permute-start.5 = (f32[1,384]{1,0:T(1,128)S(1)}, f32[1,384]{1,0:T(1,128)S(1)}, u32[]{:S(2)}, u32[]{:S(2)}) collective-permute-start(f32[1,384]{1,0:T(1,128)S(1)} %broadcast_in_dim.25.refs_8_), channel_id=1, source_target_pairs={{0,1},{1,0},{2,3},{3,2},{4,5},{5,4},{6,7},{7,6},{8,9},{9,8},{10,11... | collective-permute-start | bytes 4616 | tf_op jit(solution)/shard_map/ppermute | solution.py:176
  32.4 16.2 %collective-permute-start.3 = (bf16[384,2048]{1,0:T(8,128)(2,1)S(1)}, bf16[384,2048]{1,0:T(8,128)(2,1)S(1)}, u32[]{:S(2)}, u32[]{:S(2)}) collective-permute-start(bf16[384,2048]{1,0:T(8,128)(2,1)S(1)} %collective-permute-done.refs_0_), channel_id=1, source_target_pairs={{0,1},{1,0},{2,3},{3,2},{4,5},{5,4},{6,7},{7,6},{8,9},{9,8},{10,11... | collective-permute-start | bytes 4718600 | tf_op jit(solution)/shard_map/ppermute | solution.py:176
  45.2 5.6 %collective-permute-start.2 = (bf16[384,2048]{1,0:T(8,128)(2,1)S(1)}, bf16[384,2048]{1,0:T(8,128)(2,1)S(1)}, u32[]{:S(2)}, u32[]{:S(2)}) collective-permute-start(bf16[384,2048]{1,0:T(8,128)(2,1)S(1)} %collective-permute-done.1.refs_0_.refs_2_), channel_id=1, source_target_pairs={{0,1},{1,0},{2,3},{3,2},{4,5},{5,4},{6,7},{7,6},{8,9},{9,8},{10,11... | collective-permute-start | bytes 4718600 | tf_op jit(solution)/shard_map/ppermute | solution.py:176
  53.1 14.0 %collective-permute-start.7 = (bf16[384,256]{1,0:T(8,128)(2,1)S(1)}, bf16[384,256]{1,0:T(8,128)(2,1)S(1)}, u32[]{:S(2)}, u32[]{:S(2)}) collective-permute-start(bf16[384,256]{1,0:T(8,128)(2,1)S(1)} %get-tuple-element.51), channel_id=1, source_target_pairs={{0,18},{1,19},{2,16},{3,17},{16,2},{17,3},{18,0},{19,1},{4,22},{5,... | collective-permute-start | bytes 589832 | tf_op jit(solution)/shard_map/ppermute | solution.py:172
  54.7 19.9 %copy-start = (f32[384,64]{1,0:T(8,128)S(1)}, f32[384,64]{1,0:T(8,128)}, u32[]{:S(2)}) copy-start(f32[384,64]{1,0:T(8,128)} %get-tuple-element.73.refs_11_) | copy-start | bytes 294916
  54.7 19.9 %copy-start.1 = (f32[384,64]{1,0:T(8,128)S(1)}, f32[384,64]{1,0:T(8,128)}, u32[]{:S(2)}) copy-start(f32[384,64]{1,0:T(8,128)} %get-tuple-element.74.refs_10_) | copy-start | bytes 294916
  54.7 14.3 %collective-permute-start.11 = (bf16[384,256]{1,0:T(8,128)(2,1)S(1)}, bf16[384,256]{1,0:T(8,128)(2,1)S(1)}, u32[]{:S(2)}, u32[]{:S(2)}) collective-permute-start(bf16[384,256]{1,0:T(8,128)(2,1)S(1)} %get-tuple-element.53), channel_id=1, source_target_pairs={{0,16},{1,17},{2,18},{3,19},{16,0},{17,1},{18,2},{19,3},{4,20},{5,... | collective-permute-start | bytes 589832 | tf_op jit(solution)/shard_map/ppermute | solution.py:172
  56.2 12.8 %collective-permute-start.12 = (bf16[384,256]{1,0:T(8,128)(2,1)S(1)}, bf16[384,256]{1,0:T(8,128)(2,1)S(1)}, u32[]{:S(2)}, u32[]{:S(2)}) collective-permute-start(bf16[384,256]{1,0:T(8,128)(2,1)S(1)} %get-tuple-element.49), channel_id=1, source_target_pairs={{0,2},{1,3},{2,0},{3,1},{16,18},{17,19},{18,16},{19,17},{4,6},{5,7... | collective-permute-start | bytes 589832 | tf_op jit(solution)/shard_map/ppermute | solution.py:172
  56.6 8.9 %collective-permute-start.8 = (bf16[2,32,128]{2,1,0:T(8,128)(2,1)S(1)}, bf16[2,32,128]{2,1,0:T(8,128)(2,1)S(1)}, u32[]{:S(2)}, u32[]{:S(2)}) collective-permute-start(bf16[2,32,128]{2,1,0:T(8,128)(2,1)S(1)} %get-tuple-element.54), channel_id=1, source_target_pairs={{0,4},{4,0},{8,12},{12,8},{1,5},{5,1},{9,13},{13,9},{2,6},{6,2},{1... | collective-permute-start | bytes 49160 | tf_op jit(solution)/shard_map/ppermute | solution.py:181
  65.4 10.1 %collective-permute-start.14 = (bf16[384,256]{1,0:T(8,128)(2,1)S(1)}, bf16[384,256]{1,0:T(8,128)(2,1)S(1)}, u32[]{:S(2)}, u32[]{:S(2)}) collective-permute-start(bf16[384,256]{1,0:T(8,128)(2,1)S(1)} %get-tuple-element.62), channel_id=1, source_target_pairs={{0,18},{1,19},{2,16},{3,17},{16,2},{17,3},{18,0},{19,1},{4,22},{5,... | collective-permute-start | bytes 589832 | tf_op jit(solution)/shard_map/ppermute | solution.py:172
  65.5 10.7 %collective-permute-start.15 = (bf16[384,256]{1,0:T(8,128)(2,1)S(1)}, bf16[384,256]{1,0:T(8,128)(2,1)S(1)}, u32[]{:S(2)}, u32[]{:S(2)}) collective-permute-start(bf16[384,256]{1,0:T(8,128)(2,1)S(1)} %get-tuple-element.63), channel_id=1, source_target_pairs={{0,16},{1,17},{2,18},{3,19},{16,0},{17,1},{18,2},{19,3},{4,20},{5,... | collective-permute-start | bytes 589832 | tf_op jit(solution)/shard_map/ppermute | solution.py:172
  67.1 9.4 %collective-permute-start.16 = (bf16[384,256]{1,0:T(8,128)(2,1)S(1)}, bf16[384,256]{1,0:T(8,128)(2,1)S(1)}, u32[]{:S(2)}, u32[]{:S(2)}) collective-permute-start(bf16[384,256]{1,0:T(8,128)(2,1)S(1)} %get-tuple-element.64), channel_id=1, source_target_pairs={{0,2},{1,3},{2,0},{3,1},{16,18},{17,19},{18,16},{19,17},{4,6},{5,7... | collective-permute-start | bytes 589832 | tf_op jit(solution)/shard_map/ppermute | solution.py:172
  69.0 4.6 %collective-permute-start.9 = (bf16[2,32,128]{2,1,0:T(8,128)(2,1)S(1)}, bf16[2,32,128]{2,1,0:T(8,128)(2,1)S(1)}, u32[]{:S(2)}, u32[]{:S(2)}) collective-permute-start(bf16[2,32,128]{2,1,0:T(8,128)(2,1)S(1)} %get-tuple-element.55), channel_id=1, source_target_pairs={{0,8},{4,12},{8,0},{12,4},{1,9},{5,13},{9,1},{13,5},{2,10},{6,14},... | collective-permute-start | bytes 49160 | tf_op jit(solution)/shard_map/ppermute | solution.py:181
  69.0 5.6 %collective-permute-start.10 = (bf16[2,32,128]{2,1,0:T(8,128)(2,1)S(1)}, bf16[2,32,128]{2,1,0:T(8,128)(2,1)S(1)}, u32[]{:S(2)}, u32[]{:S(2)}) collective-permute-start(bf16[2,32,128]{2,1,0:T(8,128)(2,1)S(1)} %get-tuple-element.56), channel_id=1, source_target_pairs={{0,12},{4,8},{8,4},{12,0},{1,13},{5,9},{9,5},{13,1},{2,14},{6,10},... | collective-permute-start | bytes 49160 | tf_op jit(solution)/shard_map/ppermute | solution.py:181
  76.7 4.5 %collective-permute-start.17 = (bf16[2,40,128]{2,1,0:T(8,128)(2,1)S(1)}, bf16[2,40,128]{2,1,0:T(8,128)(2,1)S(1)}, u32[]{:S(2)}, u32[]{:S(2)}) collective-permute-start(bf16[2,40,128]{2,1,0:T(8,128)(2,1)S(1)} %get-tuple-element.66), channel_id=1, source_target_pairs={{0,4},{4,0},{8,12},{12,8},{1,5},{5,1},{9,13},{13,9},{2,6},{6,2},{1... | collective-permute-start | bytes 61448 | tf_op jit(solution)/shard_map/ppermute | solution.py:181
  77.1 4.7 %collective-permute-start.18 = (bf16[2,40,128]{2,1,0:T(8,128)(2,1)S(1)}, bf16[2,40,128]{2,1,0:T(8,128)(2,1)S(1)}, u32[]{:S(2)}, u32[]{:S(2)}) collective-permute-start(bf16[2,40,128]{2,1,0:T(8,128)(2,1)S(1)} %get-tuple-element.67), channel_id=1, source_target_pairs={{0,8},{4,12},{8,0},{12,4},{1,9},{5,13},{9,1},{13,5},{2,10},{6,14},... | collective-permute-start | bytes 61448 | tf_op jit(solution)/shard_map/ppermute | solution.py:181
  80.1 5.6 %collective-permute-start.19 = (bf16[2,40,128]{2,1,0:T(8,128)(2,1)S(1)}, bf16[2,40,128]{2,1,0:T(8,128)(2,1)S(1)}, u32[]{:S(2)}, u32[]{:S(2)}) collective-permute-start(bf16[2,40,128]{2,1,0:T(8,128)(2,1)S(1)} %get-tuple-element.68), channel_id=1, source_target_pairs={{0,12},{4,8},{8,4},{12,0},{1,13},{5,9},{9,5},{13,1},{2,14},{6,10},... | collective-permute-start | bytes 61448 | tf_op jit(solution)/shard_map/ppermute | solution.py:181
  (1 other events, 11.1 us)

commit v5 on v4

--- a/solution.py
+++ b/solution.py
@@ -236,17 +236,17 @@
     )(group, quarter, rows4, gain)
 
 
-def prepare(block, rows4, gain, group, quarter, owner, slot, begin, depth, first):
+def prepare(block, rows4, gain, owner, slot, begin, depth, first):
     tokens = block.shape[0]
     width = rows4.shape[1]
     extra = 16
+    halves = 2
+    piece = tokens // halves
 
     def body(
-        group_ref,
-        quarter_ref,
-        begin_ref,
         owner_ref,
         slot_ref,
+        begin_ref,
         block_ref,
         rows_ref,
         gain_ref,
@@ -256,59 +256,85 @@
         mixed,
         wide,
         gains,
+        held,
+        head,
+        owners,
+        slots,
+        start_at,
         sems,
     ):
-        row = pl.multiple_of(group_ref[0] * (4 * depth), 4 * depth)
-        lane = pl.multiple_of(quarter_ref[0] * depth, depth)
-        loads = [
+        group = lax.axis_index("group")
+        quarter = lax.axis_index("seq") * lax.axis_size("group") + group
+        row = pl.multiple_of(group * (4 * depth), 4 * depth)
+        lane = pl.multiple_of(quarter * depth, depth)
+        small = [
             pltpu.make_async_copy(rows_ref.at[pl.ds(row, 4 * first), :], mixed, sems.at[0]),
             pltpu.make_async_copy(gain_ref.at[:, pl.ds(lane, first)], gains, sems.at[1]),
+            pltpu.make_async_copy(owner_ref, owners, sems.at[2]),
+            pltpu.make_async_copy(slot_ref, slots, sems.at[3]),
+            pltpu.make_async_copy(begin_ref, start_at, sems.at[4]),
         ]
+        loads = []
+        stores = []
         for n, ref in enumerate((near_ref, far_ref)):
-            which = group_ref[0] if n == 0 else 1 - group_ref[0]
+            which = group if n == 0 else 1 - group
             column = pl.multiple_of(which * depth, depth)
-            loads.append(
-                pltpu.make_async_copy(
-                    block_ref.at[:, pl.ds(column, depth)], ref, sems.at[2 + n]
-                )
-            )
-        for copy in loads:
+            for k in range(halves):
+                part = pl.ds(k * piece, piece)
+                at = 6 + 2 * (halves * n + k)
+                loads.append(
+                    pltpu.make_async_copy(
+                        block_ref.at[part, pl.ds(column, depth)], held.at[n, part], sems.at[at]
+                    )
+                )
+                stores.append(
+                    pltpu.make_async_copy(held.at[n, part], ref.at[part, :], sems.at[at + 1])
+                )
+        for copy in small + loads:
             copy.start()
-        loads[0].wait()
-        loads[1].wait()
+        for load, store in zip(loads, stores):
+            load.wait()
+            store.start()
+        for copy in small:
+            copy.wait()
         wide[...] = mixed[...].astype(jnp.float32)
         for n, part in enumerate(scaled_heads(wide, gains[...], first, width)):
-            head_ref[:first, n * width : (n + 1) * width] = part
-        code = (owner_ref[...] * 2 + slot_ref[...]).astype(jnp.float32)
-        start = begin_ref[0]
+            head[:first, n * width : (n + 1) * width] = part
+        code = (owners[...] * 2 + slots[...]).astype(jnp.float32)
+        start = start_at[0]
         high = start // 64
         mark = lax.broadcasted_iota(jnp.int32, (1, 4 * width - tokens), 1)
         mark = jnp.where(mark == 0, high, jnp.where(mark == 1, start - high * 64, 0))
-        head_ref[first:, :tokens] = jnp.broadcast_to(code, (extra, tokens)).astype(jnp.bfloat16)
-        head_ref[first:, tokens:] = jnp.broadcast_to(
+        head[first:, :tokens] = jnp.broadcast_to(code, (extra, tokens)).astype(jnp.bfloat16)
+        head[first:, tokens:] = jnp.broadcast_to(
             mark.astype(jnp.float32), (extra, 4 * width - tokens)
         ).astype(jnp.bfloat16)
-        loads[2].wait()
-        loads[3].wait()
-
-    smem = pl.BlockSpec(memory_space=pltpu.SMEM)
-    vmem = pl.BlockSpec(memory_space=pltpu.VMEM)
-    hbm = pl.BlockSpec(memory_space=pl.ANY)
+        stores.append(pltpu.make_async_copy(head, head_ref, sems.at[5]))
+        stores[-1].start()
+        for store in stores:
+            store.wait()
+
+    anywhere = pl.BlockSpec(memory_space=pl.ANY)
     return pl.pallas_call(
         body,
         out_shape=[jax.ShapeDtypeStruct((first + extra, 4 * width), jnp.bfloat16)]
         + [jax.ShapeDtypeStruct((tokens, depth), jnp.bfloat16)] * 2,
-        in_specs=[smem, smem, smem, vmem, vmem, hbm, hbm, hbm],
-        out_specs=[vmem, vmem, vmem],
+        in_specs=[anywhere] * 6,
+        out_specs=[anywhere] * 3,
         scratch_shapes=[
             pltpu.VMEM((4 * first, width), jnp.bfloat16),
             pltpu.VMEM((4 * first, width), jnp.float32),
             pltpu.VMEM((1, first), jnp.float32),
-            pltpu.SemaphoreType.DMA((4,)),
+            pltpu.VMEM((2, tokens, depth), jnp.bfloat16),
+            pltpu.VMEM((first + extra, 4 * width), jnp.bfloat16),
+            pltpu.VMEM((1, tokens), jnp.int32),
+            pltpu.VMEM((1, tokens), jnp.int32),
+            pltpu.SMEM((1,), jnp.int32),
+            pltpu.SemaphoreType.DMA((6 + 4 * halves,)),
         ],
         compiler_params=pltpu.CompilerParams(vmem_limit_bytes=60 << 20),
         name="prepare",
-    )(group, quarter, begin, owner, slot, block, rows4, gain)
+    )(owner, slot, begin, block, rows4, gain)
 
 
 def partial_products(same, pairs, weights, first_column, columns, first_kind):
@@ -635,8 +661,6 @@
         block,
         rows4,
         norm_gain,
-        group,
-        quarter,
         token_owner.reshape(1, tokens),
         token_slot,
         span_start,

time: 87.1 us -> 85.8 us (0.985)
  Pallas kernels: 21.2 us -> 19.9 us
    pallas_call x1, Pallas kernels: 4.43 us -> 3.11 us  [prepare(): pl.pallas_call(body, out_shape=[jax.ShapeDtypeStruct((first + extra, 4 *...]
  transfers between devices with their start and end apart: 20 -> 20, of which waited for: 8 -> 8; matrix products, arithmetic and copies ran while one was open for 8% -> 9% of each run, Pallas kernels for 19% -> 19%
where the time goes in v5:
time: 85.8 us; the launch traced here: 85.3 us
  starting transfers between devices  30.3 us (35%)
  waiting for transfers between devices  24.9 us (29%)
  Pallas kernels  19.9 us (23%)
  other arithmetic  4.15 us (5%)
  local copies, waits for them, and re-layouts  3.93 us (5%)
  between operations  2.11 us (2%)
    ppermute x8, waiting for transfers between devices, steered(): return lax.ppermute(value, ('group', 'seq', 'tp'), pairs)  13.3 us
    ppermute x8, starting transfers between devices, steered(): return lax.ppermute(value, ('group', 'seq', 'tp'), pairs)  12.1 us
    ppermute x6, starting transfers between devices, spread(): lax.ppermute(piece, 'section', [(i, i ^ n) for i in range(len(pieces))])  8.66 us
    ppermute x3, starting transfers between devices, passed_along(): lax.ppermute(value, axis, [(i, (i + by) % length) for i in range(length)])  7.98 us
    pallas_call x3, Pallas kernels, partial_products(): pl.pallas_call(body, out_shape=[jax.ShapeDtypeStruct((tokens, columns), k...  7.62 us
    ppermute x6, waiting for transfers between devices, spread(): lax.ppermute(piece, 'section', [(i, i ^ n) for i in range(len(pieces))])  7.52 us
    pallas_call x1, Pallas kernels, split_heads(): pl.pallas_call(body, out_shape=[jax.ShapeDtypeStruct((count, 2 * width),...  5.4 us
    ppermute x3, waiting for transfers between devices, passed_along(): lax.ppermute(value, axis, [(i, (i + by) % length) for i in range(length)])  4.02 us
  transfers between devices with their start and end apart: 20, of which 8 were waited for; matrix products, arithmetic and copies ran while one was open for 9% of the time, Pallas kernels for 19%

profile of v5, /device:TPU:0, one launch (start us, length us, event | category | flops | bytes accessed | tf_op | source)
XLA Modules:
  0.0 85.3 jit_solution(6677793642839604202)
XLA Ops:
  0.7 3.1 %prepare.1 = (bf16[272,512]{1,0:T(8,128)(2,1)}, bf16[384,2048]{1,0:T(8,128)(2,1)}, bf16[384,2048]{1,0:T(8,128)(2,1)}) custom-call(s32[1,384]{1,0:T(1,128)} %bitcast.53, s32[1,384]{1,0:T(1,128)} %slot_ref.1, s32[1]{0:T(128)S(6)} %copy.18.begin_ref, bf16[384,4096]{1,0:T(8,128)(2,1)} %bitcast.48, bf16[16384,128]{1,0:T(8,128)(2,1)} %bitcast.46, f32[1,8192]{1,0:T(1,128)} %gain_ref.3), custom_call_target="tpu_custom_call" | custom-call | tf_op jit(solution)/shard_map/prepare/pallas_call | solution.py:318
  3.8 2.1 %collective-permute-start = (bf16[384,2048]{1,0:T(8,128)(2,1)}, bf16[384,2048]{1,0:T(8,128)(2,1)S(1)}, u32[]{:S(2)}, u32[]{:S(2)}) collective-permute-start(bf16[384,2048]{1,0:T(8,128)(2,1)} %get-tuple-element.37), channel_id=1, source_target_pairs={{0,0},{1,2},{2,1},{3,3},{16,16},{17,18},{18,17},{19,19},{4,4},{5,6... | collective-permute-start | bytes 4718600 | tf_op jit(solution)/shard_map/ppermute | solution.py:172
  5.8 3.0 %collective-permute-start.1 = (bf16[384,2048]{1,0:T(8,128)(2,1)}, bf16[384,2048]{1,0:T(8,128)(2,1)S(1)}, u32[]{:S(2)}, u32[]{:S(2)}) collective-permute-start(bf16[384,2048]{1,0:T(8,128)(2,1)} %get-tuple-element.39), channel_id=1, source_target_pairs={{0,16},{1,18},{2,17},{3,19},{16,0},{17,2},{18,1},{19,3},{4,20},{5,... | collective-permute-start | bytes 4718600 | tf_op jit(solution)/shard_map/ppermute | solution.py:172
  8.8 3.6 %collective-permute-start.4 = (bf16[272,512]{1,0:T(8,128)(2,1)}, bf16[272,512]{1,0:T(8,128)(2,1)S(1)}, u32[]{:S(2)}, u32[]{:S(2)}) collective-permute-start(bf16[272,512]{1,0:T(8,128)(2,1)} %get-tuple-element.40), channel_id=1, source_target_pairs={{0,12},{4,0},{8,4},{12,8},{1,13},{5,1},{9,5},{13,9},{2,14},{6,2},{... | collective-permute-start | bytes 835592 | tf_op jit(solution)/shard_map/ppermute | solution.py:17
  12.4 5.4 %split_heads.1 = (bf16[1792,256]{1,0:T(8,128)(2,1)}, bf16[1792,256]{1,0:T(8,128)(2,1)}) custom-call(s32[1]{0:T(128)} %bitcast.23.group_ref, s32[1]{0:T(128)} %bitcast.24.quarter_ref, bf16[16384,128]{1,0:T(8,128)(2,1)} %bitcast.47, f32[1,8192]{1,0:T(1,128)} %gain_ref.3), custom_call_target="tpu_custom_call" | custom-call | tf_op jit(solution)/shard_map/split_heads/pallas_call | solution.py:215
  18.3 1.7 %copy.13 = bf16[4,2,2,32,256]{4,3,2,1,0:T(8,128)(2,1)} copy(bf16[4,2,2,32,256]{4,1,3,2,0:T(2,128)(2,1)} %bitcast.50) | data formatting | bytes 524288 | tf_op jit(solution)/shard_map/transpose | solution.py:710
  20.0 3.9 %collective-permute-start.13 = (bf16[1792,256]{1,0:T(8,128)(2,1)}, bf16[1792,256]{1,0:T(8,128)(2,1)}, u32[]{:S(2)}, u32[]{:S(2)}) collective-permute-start(bf16[1792,256]{1,0:T(8,128)(2,1)} %get-tuple-element.60), channel_id=1, source_target_pairs={{0,12},{4,0},{8,4},{12,8},{1,13},{5,1},{9,5},{13,9},{2,14},{6,2},{... | collective-permute-start | bytes 2752520 | tf_op jit(solution)/shard_map/ppermute | solution.py:17
  25.8 1.5 %multiply_sine_fusion = (f32[384,64]{1,0:T(8,128)}, f32[384,64]{1,0:T(8,128)}) fusion(f32[64]{0:T(128)S(1)} %multiply_exponential_fusion, f32[384]{0:T(512)S(1)} %add_convert_fusion), kind=kLoop, calls=%fused_computation.1 | loop fusion | flops 24576 | bytes 198400 | tf_op jit(solution)/shard_map/sin | solution.py:697
  28.3 2.6 %multiply_reduce_fusion = f32[384]{0:T(512)S(1)} fusion(bf16[384,4096]{1,0:T(8,128)(2,1)} %bitcast.49), kind=kLoop, calls=%fused_computation | loop fusion | flops 4718208 | bytes 3147264 | tf_op jit(solution)/shard_map/reduce_sum | solution.py:686
  31.5 12.4 %collective-permute-done.1.refs_0_.refs_2_ = bf16[384,2048]{1,0:T(8,128)(2,1)S(1)} collective-permute-done((bf16[384,2048]{1,0:T(8,128)(2,1)}, bf16[384,2048]{1,0:T(8,128)(2,1)S(1)}, u32[]{:S(2)}, u32[]{:S(2)}) %collective-permute-start.1) | collective-permute-done | bytes 1572896 | tf_op jit(solution)/shard_map/ppermute | solution.py:172
  44.9 2.4 %keep.1 = (f32[4,64,128]{2,1,0:T(8,128)S(1)}, f32[4,64,128]{2,1,0:T(8,128)S(1)}) custom-call(s32[2]{0:T(128)S(1)} %bitcast.45, bf16[4,2,32,128]{3,2,1,0:T(8,128)(2,1)S(1)} %bitcast.43, bf16[4,2,64,256]{3,2,1,0:T(8,128)(2,1)S(1)} %bitcast.42, bf16[4,2,4,256]{3,2,1,0:T(4,128)(2,1)S(1)} %copy.16.recent_ref), custom_call_target="tpu_custom_call" | custom-call | flops 40000000000 | bytes 1 | tf_op jit(solution)/shard_map/keep/pallas_call | solution.py:622
  47.3 2.2 %partial_products.3 = (f32[384,256]{1,0:T(8,128)S(1)}, bf16[384,256]{1,0:T(8,128)(2,1)S(1)}) custom-call(s32[1]{0:T(128)} %bitcast.14.same_ref, bf16[384,2048]{1,0:T(8,128)(2,1)S(1)} %collective-permute-done.refs_0_, bf16[384,2048]{1,0:T(8,128)(2,1)S(1)} %collective-permute-done.3.refs_1_, bf16[272,512]{1,0:T(8,128)(2,1)S(1)} %collective-permute-done.4.refs_2_.refs_4_, ...), custom_call_target="tpu_custom_call" | custom-call | tf_op jit(solution)/shard_map/partial_products/pallas_call | solution.py:398
  49.5 2.2 %partial_products.4 = (bf16[384,256]{1,0:T(8,128)(2,1)S(1)}, bf16[384,256]{1,0:T(8,128)(2,1)S(1)}) custom-call(s32[1]{0:T(128)} %bitcast.14.same_ref, bf16[384,2048]{1,0:T(8,128)(2,1)S(1)} %collective-permute-done.1.refs_0_.refs_2_, bf16[384,2048]{1,0:T(8,128)(2,1)S(1)} %collective-permute-done.2.refs_1_.refs_3_, ...), custom_call_target="tpu_custom_call" | custom-call | tf_op jit(solution)/shard_map/partial_products/pallas_call | solution.py:398
  51.8 1.6 %collective-permute-start.7 = (bf16[384,256]{1,0:T(8,128)(2,1)S(1)}, bf16[384,256]{1,0:T(8,128)(2,1)S(1)}, u32[]{:S(2)}, u32[]{:S(2)}) collective-permute-start(bf16[384,256]{1,0:T(8,128)(2,1)S(1)} %get-tuple-element.51), channel_id=1, source_target_pairs={{0,18},{1,19},{2,16},{3,17},{16,2},{17,3},{18,0},{19,1},{4,22},{5,... | collective-permute-start | bytes 589832 | tf_op jit(solution)/shard_map/ppermute | solution.py:172
  53.4 1.5 %collective-permute-start.11 = (bf16[384,256]{1,0:T(8,128)(2,1)S(1)}, bf16[384,256]{1,0:T(8,128)(2,1)S(1)}, u32[]{:S(2)}, u32[]{:S(2)}) collective-permute-start(bf16[384,256]{1,0:T(8,128)(2,1)S(1)} %get-tuple-element.53), channel_id=1, source_target_pairs={{0,16},{1,17},{2,18},{3,19},{16,0},{17,1},{18,2},{19,3},{4,20},{5,... | collective-permute-start | bytes 589832 | tf_op jit(solution)/shard_map/ppermute | solution.py:172
  55.3 1.6 %collective-permute-start.8 = (bf16[2,32,128]{2,1,0:T(8,128)(2,1)S(1)}, bf16[2,32,128]{2,1,0:T(8,128)(2,1)S(1)}, u32[]{:S(2)}, u32[]{:S(2)}) collective-permute-start(bf16[2,32,128]{2,1,0:T(8,128)(2,1)S(1)} %get-tuple-element.54), channel_id=1, source_target_pairs={{0,4},{4,0},{8,12},{12,8},{1,5},{5,1},{9,13},{13,9},{2,6},{6,2},{1... | collective-permute-start | bytes 49160 | tf_op jit(solution)/shard_map/ppermute | solution.py:181
  56.9 4.0 %collective-permute-done.13.refs_5_ = bf16[1792,256]{1,0:T(8,128)(2,1)} collective-permute-done((bf16[1792,256]{1,0:T(8,128)(2,1)}, bf16[1792,256]{1,0:T(8,128)(2,1)}, u32[]{:S(2)}, u32[]{:S(2)}) %collective-permute-start.13) | collective-permute-done | bytes 917536 | tf_op jit(solution)/shard_map/ppermute | solution.py:17
  60.9 3.2 %partial_products.5 = (f32[384,256]{1,0:T(8,128)S(1)}, bf16[384,256]{1,0:T(8,128)(2,1)S(1)}, bf16[384,256]{1,0:T(8,128)(2,1)S(1)}, bf16[384,256]{1,0:T(8,128)(2,1)S(1)}) custom-call(s32[1]{0:T(128)} %bitcast.14.same_ref, bf16[384,2048]{1,0:T(8,128)(2,1)S(1)} %collective-permute-done.refs_0_, bf16[384,2048]{1,0:T(8,128)(2,1)S(1)} %collective-permute-done.3.refs_1_, ...), custom_call_target="tpu_custom_call" | custom-call | tf_op jit(solution)/shard_map/partial_products/pallas_call | solution.py:398
  64.2 1.5 %collective-permute-start.15 = (bf16[384,256]{1,0:T(8,128)(2,1)S(1)}, bf16[384,256]{1,0:T(8,128)(2,1)S(1)}, u32[]{:S(2)}, u32[]{:S(2)}) collective-permute-start(bf16[384,256]{1,0:T(8,128)(2,1)S(1)} %get-tuple-element.63), channel_id=1, source_target_pairs={{0,16},{1,17},{2,18},{3,19},{16,0},{17,1},{18,2},{19,3},{4,20},{5,... | collective-permute-start | bytes 589832 | tf_op jit(solution)/shard_map/ppermute | solution.py:172
  65.7 2.0 %collective-permute-start.16 = (bf16[384,256]{1,0:T(8,128)(2,1)S(1)}, bf16[384,256]{1,0:T(8,128)(2,1)S(1)}, u32[]{:S(2)}, u32[]{:S(2)}) collective-permute-start(bf16[384,256]{1,0:T(8,128)(2,1)S(1)} %get-tuple-element.64), channel_id=1, source_target_pairs={{0,2},{1,3},{2,0},{3,1},{16,18},{17,19},{18,16},{19,17},{4,6},{5,7... | collective-permute-start | bytes 589832 | tf_op jit(solution)/shard_map/ppermute | solution.py:172
  67.7 2.6 %collective-permute-start.10 = (bf16[2,32,128]{2,1,0:T(8,128)(2,1)S(1)}, bf16[2,32,128]{2,1,0:T(8,128)(2,1)S(1)}, u32[]{:S(2)}, u32[]{:S(2)}) collective-permute-start(bf16[2,32,128]{2,1,0:T(8,128)(2,1)S(1)} %get-tuple-element.56), channel_id=1, source_target_pairs={{0,12},{4,8},{8,4},{12,0},{1,13},{5,9},{9,5},{13,1},{2,14},{6,10},... | collective-permute-start | bytes 49160 | tf_op jit(solution)/shard_map/ppermute | solution.py:181
  70.3 2.0 %collective-permute-done.9.refs_2_ = bf16[2,32,128]{2,1,0:T(8,128)(2,1)S(1)} collective-permute-done((bf16[2,32,128]{2,1,0:T(8,128)(2,1)S(1)}, bf16[2,32,128]{2,1,0:T(8,128)(2,1)S(1)}, u32[]{:S(2)}, u32[]{:S(2)}) %collective-permute-start.9) | collective-permute-done | bytes 16416 | tf_op jit(solution)/shard_map/ppermute | solution.py:181
  75.8 2.9 %collective-permute-start.18 = (bf16[2,40,128]{2,1,0:T(8,128)(2,1)S(1)}, bf16[2,40,128]{2,1,0:T(8,128)(2,1)S(1)}, u32[]{:S(2)}, u32[]{:S(2)}) collective-permute-start(bf16[2,40,128]{2,1,0:T(8,128)(2,1)S(1)} %get-tuple-element.67), channel_id=1, source_target_pairs={{0,8},{4,12},{8,0},{12,4},{1,9},{5,13},{9,1},{13,5},{2,10},{6,14},... | collective-permute-start | bytes 61448 | tf_op jit(solution)/shard_map/ppermute | solution.py:181
  80.5 3.8 %collective-permute-done.19.rest_3_ = bf16[2,40,128]{2,1,0:T(8,128)(2,1)S(1)} collective-permute-done((bf16[2,40,128]{2,1,0:T(8,128)(2,1)S(1)}, bf16[2,40,128]{2,1,0:T(8,128)(2,1)S(1)}, u32[]{:S(2)}, u32[]{:S(2)}) %collective-permute-start.19) | collective-permute-done | bytes 20512 | tf_op jit(solution)/shard_map/ppermute | solution.py:181
  (50 shorter events, 10.2 us)
Async XLA Ops:
  3.8 23.6 %collective-permute-start = (bf16[384,2048]{1,0:T(8,128)(2,1)}, bf16[384,2048]{1,0:T(8,128)(2,1)S(1)}, u32[]{:S(2)}, u32[]{:S(2)}) collective-permute-start(bf16[384,2048]{1,0:T(8,128)(2,1)} %get-tuple-element.37), channel_id=1, source_target_pairs={{0,0},{1,2},{2,1},{3,3},{16,16},{17,18},{18,17},{19,19},{4,4},{5,6... | collective-permute-start | bytes 4718600 | tf_op jit(solution)/shard_map/ppermute | solution.py:172
  5.8 38.1 %collective-permute-start.1 = (bf16[384,2048]{1,0:T(8,128)(2,1)}, bf16[384,2048]{1,0:T(8,128)(2,1)S(1)}, u32[]{:S(2)}, u32[]{:S(2)}) collective-permute-start(bf16[384,2048]{1,0:T(8,128)(2,1)} %get-tuple-element.39), channel_id=1, source_target_pairs={{0,16},{1,18},{2,17},{3,19},{16,0},{17,2},{18,1},{19,3},{4,20},{5,... | collective-permute-start | bytes 4718600 | tf_op jit(solution)/shard_map/ppermute | solution.py:172
  8.8 11.2 %collective-permute-start.4 = (bf16[272,512]{1,0:T(8,128)(2,1)}, bf16[272,512]{1,0:T(8,128)(2,1)S(1)}, u32[]{:S(2)}, u32[]{:S(2)}) collective-permute-start(bf16[272,512]{1,0:T(8,128)(2,1)} %get-tuple-element.40), channel_id=1, source_target_pairs={{0,12},{4,0},{8,4},{12,8},{1,13},{5,1},{9,5},{13,9},{2,14},{6,2},{... | collective-permute-start | bytes 835592 | tf_op jit(solution)/shard_map/ppermute | solution.py:17
  17.8 29.5 %collective-permute-start.6 = (bf16[1792,256]{1,0:T(8,128)(2,1)}, bf16[1792,256]{1,0:T(8,128)(2,1)}, u32[]{:S(2)}, u32[]{:S(2)}) collective-permute-start(bf16[1792,256]{1,0:T(8,128)(2,1)} %get-tuple-element.47), channel_id=1, source_target_pairs={{0,12},{4,0},{8,4},{12,8},{1,13},{5,1},{9,5},{13,9},{2,14},{6,2},{... | collective-permute-start | bytes 2752520 | tf_op jit(solution)/shard_map/ppermute | solution.py:17
  20.0 40.9 %collective-permute-start.13 = (bf16[1792,256]{1,0:T(8,128)(2,1)}, bf16[1792,256]{1,0:T(8,128)(2,1)}, u32[]{:S(2)}, u32[]{:S(2)}) collective-permute-start(bf16[1792,256]{1,0:T(8,128)(2,1)} %get-tuple-element.60), channel_id=1, source_target_pairs={{0,12},{4,0},{8,4},{12,8},{1,13},{5,1},{9,5},{13,9},{2,14},{6,2},{... | collective-permute-start | bytes 2752520 | tf_op jit(solution)/shard_map/ppermute | solution.py:17
  28.3 16.6 %copy-start.2 = (bf16[4,2,2,32,256]{4,3,2,1,0:T(8,128)(2,1)S(1)}, bf16[4,2,2,32,256]{4,3,2,1,0:T(8,128)(2,1)}, u32[]{:S(2)}) copy-start(bf16[4,2,2,32,256]{4,3,2,1,0:T(8,128)(2,1)} %copy.13) | copy-start | bytes 786436
  28.3 16.6 %copy-start.3 = (s32[1,1,2]{2,1,0:T(1,128)S(1)}, s32[1,1,2]{2,1,0:T(1,128)}, u32[]{:S(2)}) copy-start(s32[1,1,2]{2,1,0:T(1,128)} %param.17) | copy-start | bytes 28
  30.9 16.4 %collective-permute-start.5 = (f32[1,384]{1,0:T(1,128)S(1)}, f32[1,384]{1,0:T(1,128)S(1)}, u32[]{:S(2)}, u32[]{:S(2)}) collective-permute-start(f32[1,384]{1,0:T(1,128)S(1)} %broadcast_in_dim.23.refs_8_), channel_id=1, source_target_pairs={{0,1},{1,0},{2,3},{3,2},{4,5},{5,4},{6,7},{7,6},{8,9},{9,8},{10,11... | collective-permute-start | bytes 4616 | tf_op jit(solution)/shard_map/ppermute | solution.py:176
  31.1 16.2 %collective-permute-start.3 = (bf16[384,2048]{1,0:T(8,128)(2,1)S(1)}, bf16[384,2048]{1,0:T(8,128)(2,1)S(1)}, u32[]{:S(2)}, u32[]{:S(2)}) collective-permute-start(bf16[384,2048]{1,0:T(8,128)(2,1)S(1)} %collective-permute-done.refs_0_), channel_id=1, source_target_pairs={{0,1},{1,0},{2,3},{3,2},{4,5},{5,4},{6,7},{7,6},{8,9},{9,8},{10,11... | collective-permute-start | bytes 4718600 | tf_op jit(solution)/shard_map/ppermute | solution.py:176
  43.9 5.6 %collective-permute-start.2 = (bf16[384,2048]{1,0:T(8,128)(2,1)S(1)}, bf16[384,2048]{1,0:T(8,128)(2,1)S(1)}, u32[]{:S(2)}, u32[]{:S(2)}) collective-permute-start(bf16[384,2048]{1,0:T(8,128)(2,1)S(1)} %collective-permute-done.1.refs_0_.refs_2_), channel_id=1, source_target_pairs={{0,1},{1,0},{2,3},{3,2},{4,5},{5,4},{6,7},{7,6},{8,9},{9,8},{10,11... | collective-permute-start | bytes 4718600 | tf_op jit(solution)/shard_map/ppermute | solution.py:176
  51.8 14.0 %collective-permute-start.7 = (bf16[384,256]{1,0:T(8,128)(2,1)S(1)}, bf16[384,256]{1,0:T(8,128)(2,1)S(1)}, u32[]{:S(2)}, u32[]{:S(2)}) collective-permute-start(bf16[384,256]{1,0:T(8,128)(2,1)S(1)} %get-tuple-element.51), channel_id=1, source_target_pairs={{0,18},{1,19},{2,16},{3,17},{16,2},{17,3},{18,0},{19,1},{4,22},{5,... | collective-permute-start | bytes 589832 | tf_op jit(solution)/shard_map/ppermute | solution.py:172
  53.4 19.9 %copy-start = (f32[384,64]{1,0:T(8,128)S(1)}, f32[384,64]{1,0:T(8,128)}, u32[]{:S(2)}) copy-start(f32[384,64]{1,0:T(8,128)} %get-tuple-element.73.refs_11_) | copy-start | bytes 294916
  53.4 19.9 %copy-start.1 = (f32[384,64]{1,0:T(8,128)S(1)}, f32[384,64]{1,0:T(8,128)}, u32[]{:S(2)}) copy-start(f32[384,64]{1,0:T(8,128)} %get-tuple-element.74.refs_10_) | copy-start | bytes 294916
  53.4 14.3 %collective-permute-start.11 = (bf16[384,256]{1,0:T(8,128)(2,1)S(1)}, bf16[384,256]{1,0:T(8,128)(2,1)S(1)}, u32[]{:S(2)}, u32[]{:S(2)}) collective-permute-start(bf16[384,256]{1,0:T(8,128)(2,1)S(1)} %get-tuple-element.53), channel_id=1, source_target_pairs={{0,16},{1,17},{2,18},{3,19},{16,0},{17,1},{18,2},{19,3},{4,20},{5,... | collective-permute-start | bytes 589832 | tf_op jit(solution)/shard_map/ppermute | solution.py:172
  54.9 12.8 %collective-permute-start.12 = (bf16[384,256]{1,0:T(8,128)(2,1)S(1)}, bf16[384,256]{1,0:T(8,128)(2,1)S(1)}, u32[]{:S(2)}, u32[]{:S(2)}) collective-permute-start(bf16[384,256]{1,0:T(8,128)(2,1)S(1)} %get-tuple-element.49), channel_id=1, source_target_pairs={{0,2},{1,3},{2,0},{3,1},{16,18},{17,19},{18,16},{19,17},{4,6},{5,7... | collective-permute-start | bytes 589832 | tf_op jit(solution)/shard_map/ppermute | solution.py:172
  55.3 8.9 %collective-permute-start.8 = (bf16[2,32,128]{2,1,0:T(8,128)(2,1)S(1)}, bf16[2,32,128]{2,1,0:T(8,128)(2,1)S(1)}, u32[]{:S(2)}, u32[]{:S(2)}) collective-permute-start(bf16[2,32,128]{2,1,0:T(8,128)(2,1)S(1)} %get-tuple-element.54), channel_id=1, source_target_pairs={{0,4},{4,0},{8,12},{12,8},{1,5},{5,1},{9,13},{13,9},{2,6},{6,2},{1... | collective-permute-start | bytes 49160 | tf_op jit(solution)/shard_map/ppermute | solution.py:181
  64.1 10.1 %collective-permute-start.14 = (bf16[384,256]{1,0:T(8,128)(2,1)S(1)}, bf16[384,256]{1,0:T(8,128)(2,1)S(1)}, u32[]{:S(2)}, u32[]{:S(2)}) collective-permute-start(bf16[384,256]{1,0:T(8,128)(2,1)S(1)} %get-tuple-element.62), channel_id=1, source_target_pairs={{0,18},{1,19},{2,16},{3,17},{16,2},{17,3},{18,0},{19,1},{4,22},{5,... | collective-permute-start | bytes 589832 | tf_op jit(solution)/shard_map/ppermute | solution.py:172
  64.2 10.7 %collective-permute-start.15 = (bf16[384,256]{1,0:T(8,128)(2,1)S(1)}, bf16[384,256]{1,0:T(8,128)(2,1)S(1)}, u32[]{:S(2)}, u32[]{:S(2)}) collective-permute-start(bf16[384,256]{1,0:T(8,128)(2,1)S(1)} %get-tuple-element.63), channel_id=1, source_target_pairs={{0,16},{1,17},{2,18},{3,19},{16,0},{17,1},{18,2},{19,3},{4,20},{5,... | collective-permute-start | bytes 589832 | tf_op jit(solution)/shard_map/ppermute | solution.py:172
  65.7 9.3 %collective-permute-start.16 = (bf16[384,256]{1,0:T(8,128)(2,1)S(1)}, bf16[384,256]{1,0:T(8,128)(2,1)S(1)}, u32[]{:S(2)}, u32[]{:S(2)}) collective-permute-start(bf16[384,256]{1,0:T(8,128)(2,1)S(1)} %get-tuple-element.64), channel_id=1, source_target_pairs={{0,2},{1,3},{2,0},{3,1},{16,18},{17,19},{18,16},{19,17},{4,6},{5,7... | collective-permute-start | bytes 589832 | tf_op jit(solution)/shard_map/ppermute | solution.py:172
  67.7 4.6 %collective-permute-start.9 = (bf16[2,32,128]{2,1,0:T(8,128)(2,1)S(1)}, bf16[2,32,128]{2,1,0:T(8,128)(2,1)S(1)}, u32[]{:S(2)}, u32[]{:S(2)}) collective-permute-start(bf16[2,32,128]{2,1,0:T(8,128)(2,1)S(1)} %get-tuple-element.55), channel_id=1, source_target_pairs={{0,8},{4,12},{8,0},{12,4},{1,9},{5,13},{9,1},{13,5},{2,10},{6,14},... | collective-permute-start | bytes 49160 | tf_op jit(solution)/shard_map/ppermute | solution.py:181
  67.7 5.6 %collective-permute-start.10 = (bf16[2,32,128]{2,1,0:T(8,128)(2,1)S(1)}, bf16[2,32,128]{2,1,0:T(8,128)(2,1)S(1)}, u32[]{:S(2)}, u32[]{:S(2)}) collective-permute-start(bf16[2,32,128]{2,1,0:T(8,128)(2,1)S(1)} %get-tuple-element.56), channel_id=1, source_target_pairs={{0,12},{4,8},{8,4},{12,0},{1,13},{5,9},{9,5},{13,1},{2,14},{6,10},... | collective-permute-start | bytes 49160 | tf_op jit(solution)/shard_map/ppermute | solution.py:181
  75.3 4.5 %collective-permute-start.17 = (bf16[2,40,128]{2,1,0:T(8,128)(2,1)S(1)}, bf16[2,40,128]{2,1,0:T(8,128)(2,1)S(1)}, u32[]{:S(2)}, u32[]{:S(2)}) collective-permute-start(bf16[2,40,128]{2,1,0:T(8,128)(2,1)S(1)} %get-tuple-element.66), channel_id=1, source_target_pairs={{0,4},{4,0},{8,12},{12,8},{1,5},{5,1},{9,13},{13,9},{2,6},{6,2},{1... | collective-permute-start | bytes 61448 | tf_op jit(solution)/shard_map/ppermute | solution.py:181
  75.8 4.7 %collective-permute-start.18 = (bf16[2,40,128]{2,1,0:T(8,128)(2,1)S(1)}, bf16[2,40,128]{2,1,0:T(8,128)(2,1)S(1)}, u32[]{:S(2)}, u32[]{:S(2)}) collective-permute-start(bf16[2,40,128]{2,1,0:T(8,128)(2,1)S(1)} %get-tuple-element.67), channel_id=1, source_target_pairs={{0,8},{4,12},{8,0},{12,4},{1,9},{5,13},{9,1},{13,5},{2,10},{6,14},... | collective-permute-start | bytes 61448 | tf_op jit(solution)/shard_map/ppermute | solution.py:181
  78.7 5.6 %collective-permute-start.19 = (bf16[2,40,128]{2,1,0:T(8,128)(2,1)S(1)}, bf16[2,40,128]{2,1,0:T(8,128)(2,1)S(1)}, u32[]{:S(2)}, u32[]{:S(2)}) collective-permute-start(bf16[2,40,128]{2,1,0:T(8,128)(2,1)S(1)} %get-tuple-element.68), channel_id=1, source_target_pairs={{0,12},{4,8},{8,4},{12,0},{1,13},{5,9},{9,5},{13,1},{2,14},{6,10},... | collective-permute-start | bytes 61448 | tf_op jit(solution)/shard_map/ppermute | solution.py:181
  (1 other events, 7.5 us)
